TPU v7x, 32 devices: a whole 2x2x4 slice. The times are simulated.
32 devices in a mesh: section: 4 (over x, core), dp: 8 (over z, y).
Axes of the slice: x: 2, y: 2, z: 4, core: 2. Of those that a mesh axis runs over, the one named last changes fastest.
Arguments:
- section_inputs: bfloat16 [4, 4, 1024, 2048], P('section', None, 'dp'), may hold values from -8 to 8
- top_grads: bfloat16 [4, 1024, 2048], P(None, 'dp'), may hold values from -8 to 8
- query_weight: bfloat16 [4, 2048, 1024], P('section'), may hold values from -0.375 to 0.375
- output_weight: bfloat16 [4, 2048, 1024], P('section'), may hold values from -0.125 to 0.125
- neighbour_kv: bfloat16 [4, 16, 2, 128, 1024], P('section', 'dp'), may hold values from -6 to 6
- nbr_ids: int32 [4, 16, 2], P(None, 'dp'), may hold values from 0 to 15, as said below
- send_list: int32 [8, 8], replicated, may hold values from 0 to 1, as said below
- send_counts: int32 [8, 8], replicated, may hold values from 0 to 1, as said below
Outputs:
- input_grads: bfloat16 [4, 4, 1024, 2048], P('section', None, 'dp')
- query_grads: bfloat16 [4, 2048, 1024], P('section', 'dp')
- output_grads: bfloat16 [4, 2048, 1024], P('section', 'dp')
- kv_grads: bfloat16 [4, 16, 2, 128, 1024], P('section', 'dp')
Inputs may be any that keep to these rules, and one draw needn't show every extreme that they name: `nbr_ids`: the 2 neighbours of a span have different owners. Every neighbour of reader r's spans owned by o is block o * 2 + send_list[o, r]. `send_list`: entry [o, r] is 0 where send_counts[o, r] is 0. `send_counts`: entry [o, r] is 1 where some span of reader r has a neighbour of owner o, else 0.
All inputs are finite; a program needn't handle non-finite values.
Results may differ from a plain program's by a relative error of at most 0.039.
Values may be sent and summed in bfloat16 or wider, within the bound.
No kernel may reach another device: no remote copies, remote signals or barrier semaphores. Data moves between devices by JAX's collectives and lax.ppermute only.
A program may use at most 192 MiB of HBM per device.

v0:
```python
import functools

import jax
import jax.numpy as jnp
from jax import lax
from jax.experimental import pallas as pl
from jax.experimental.pallas import tpu as pltpu
from jax.sharding import PartitionSpec as P

HEADS = 16
HEAD_DIM = 64
SPAN = 64
K_NBR = 2
NBR_LEN = 128
PAIR = 2 * HEAD_DIM
KEYS = K_NBR * NBR_LEN
SCALE = HEAD_DIM ** (-0.5)
BF = jnp.bfloat16
F32 = jnp.float32
ANY = pl.BlockSpec(memory_space=pl.ANY)


def cost(micros_of_work):
    return pl.CostEstimate(flops=0, transcendentals=0, bytes_accessed=int(micros_of_work * 3.6e6))


def nt(a, b):
    return lax.dot_general(a, b, (((1,), (1,)), ((), ())), preferred_element_type=F32)


def nn(a, b):
    return lax.dot_general(a, b, (((1,), (0,)), ((), ())), preferred_element_type=F32)


def tn(a, b):
    return lax.dot_general(a, b, (((0,), (0,)), ((), ())), preferred_element_type=F32)


def head_rows(x):
    heads = x.shape[1] // HEAD_DIM
    if heads == 1:
        return x
    lane = lax.broadcasted_iota(jnp.int32, x.shape, 1) // HEAD_DIM
    zero = jnp.zeros_like(x)
    return jnp.concatenate([jnp.where(lane == h, x, zero) for h in range(heads)], axis=0)


def head_columns(y):
    heads = y.shape[1] // HEAD_DIM
    out = y[:SPAN]
    lane = lax.broadcasted_iota(jnp.int32, out.shape, 1) // HEAD_DIM
    for h in range(1, heads):
        out = jnp.where(lane == h, y[h * SPAN : (h + 1) * SPAN], out)
    return out


def softmax_rows(scores):
    weights = jnp.exp(scores - jnp.max(scores, axis=-1, keepdims=True))
    return weights / jnp.sum(weights, axis=-1, keepdims=True)


def probs_kernel(owners, q_ref, k_ref, out_ref):
    micro = pl.program_id(0)
    tokens, width = q_ref.shape[1], q_ref.shape[2]
    spans = tokens // SPAN
    for span in range(spans):
        refs = [owners[(micro * spans + span) * K_NBR + k] for k in range(K_NBR)]
        for pair in range(width // PAIR):
            cols = slice(pair * PAIR, (pair + 1) * PAIR)
            keys = jnp.concatenate([k_ref[r, :, cols] for r in refs], axis=0)
            rows = head_rows(q_ref[0, span * SPAN : (span + 1) * SPAN, cols])
            out_ref[0, span * (width // PAIR) + pair] = softmax_rows(nt(rows, keys) * SCALE).astype(BF)


def tick_kernel(
    chunks, base, head_major,
    scal,
    arriving, top, w_out, w_query, keys, values, probs, g0, u0, d0, sb0, sa0,
    leaving, g_store, u_store, d_store, s_late, s_early,
    up, wo, wq, kb, vb, pb, datt, dq, gr, sem_up, sem_wo, sem_wq, sem_k, sem_v, sem_p, sem_out, sem_half, sem_head,
):
    micro = scal[base]
    valid = scal[base + 1]
    last = scal[base + 2]
    other = scal[base + 3]
    tokens, model = up.shape
    width = datt.shape[1]
    spans = tokens // SPAN
    refs = spans * K_NBR
    pairs = width // PAIR
    rows = model // chunks
    wide = width // chunks
    groups = 1
    halves = sem_half.shape[0]
    block = model // (2 * halves)
    heads = sem_head.shape[0]
    slice_w = width // heads

    def copy_wo(c):
        return pltpu.make_async_copy(w_out.at[:, pl.ds(c * wide, wide)], wo.at[c], sem_wo.at[c])

    def copy_wq(c):
        return pltpu.make_async_copy(w_query.at[pl.ds(c * rows, rows)], wq.at[c], sem_wq.at[c])

    def copy_v(i):
        return pltpu.make_async_copy(values.at[scal[base + 4 + i]], vb.at[i], sem_v.at[i])

    def copy_k(i):
        return pltpu.make_async_copy(keys.at[scal[base + 4 + i]], kb.at[i], sem_k.at[i])

    @pl.when(valid > 0)
    def _():
        from_top = pltpu.make_async_copy(top.at[micro], up, sem_up)
        from_hop = pltpu.make_async_copy(arriving, up, sem_up)

        @pl.when(last > 0)
        def _():
            from_top.start()

        @pl.when(last == 0)
        def _():
            from_hop.start()

        for c in range(chunks):
            copy_wo(c).start()
        for i in range(refs):
            copy_v(i).start()
        get_probs = pltpu.make_async_copy(probs.at[micro], pb, sem_p)
        get_probs.start()
        for i in range(refs):
            copy_k(i).start()
        for c in range(chunks):
            copy_wq(c).start()

        from_hop.wait()
        save_up = pltpu.make_async_copy(up, u_store.at[micro], sem_out.at[0])
        save_up.start()
        cut = s_early.shape[0]

        def to_swap(late):
            store = s_late.at[micro - cut] if late else s_early.at[micro]
            copies = [pltpu.make_async_copy(dq, store.at[0], sem_out.at[1])]
            for h in range(halves):
                start = pl.multiple_of((2 * h + other) * block, block)
                copies.append(
                    pltpu.make_async_copy(
                        up.at[:, pl.ds(start, block)], store.at[1, :, pl.ds(h * block, block)], sem_half.at[h]
                    )
                )
            return copies

        @pl.when(micro < cut)
        def _():
            for copy in to_swap(False)[1:]:
                copy.start()

        @pl.when(micro >= cut)
        def _():
            for copy in to_swap(True)[1:]:
                copy.start()


        def project(c, carry):
            copy_wo(c).wait()
            datt[:, pl.ds(pl.multiple_of(c * wide, wide), wide)] = nn(up[...], wo[c]).astype(BF)
            return carry

        lax.fori_loop(0, chunks, project, 0)
        if head_major:
            late = [
                pltpu.make_async_copy(
                    datt.at[:, pl.ds(h * slice_w, slice_w)], d_store.at[h, micro], sem_head.at[h]
                )
                for h in range(heads)
            ]
        else:
            late = [pltpu.make_async_copy(datt, d_store.at[micro], sem_head.at[0])]
        for save in late:
            save.start()
        for i in range(refs):
            copy_v(i).wait()
        get_probs.wait()
        for i in range(refs):
            copy_k(i).wait()

        def one_group(index, carry):
            span, first = index // groups, index % groups * (pairs // groups)
            rws = pl.ds(pl.multiple_of(span * SPAN, SPAN), SPAN)
            for step in range(pairs // groups):
                pair = first + step
                cols = pl.ds(pl.multiple_of(pair * PAIR, PAIR), PAIR)
                val = jnp.concatenate([vb[span * K_NBR + k, :, cols] for k in range(K_NBR)], axis=0)
                key = jnp.concatenate([kb[span * K_NBR + k, :, cols] for k in range(K_NBR)], axis=0)
                d_probs = nt(head_rows(datt[rws, cols]), val)
                prob = pb[span * pairs + pair].astype(F32)
                delta = jnp.sum(prob * d_probs, axis=-1, keepdims=True)
                d_scores = (prob * (d_probs - delta) * SCALE).astype(BF)
                dq[rws, cols] = head_columns(nn(d_scores, key)).astype(BF)
            return carry

        lax.fori_loop(0, spans * groups, one_group, 0)

        @pl.when(micro < cut)
        def _():
            to_swap(False)[0].start()

        @pl.when(micro >= cut)
        def _():
            to_swap(True)[0].start()

        def back(c, carry):
            copy_wq(c).wait()
            cols = pl.ds(pl.multiple_of(c * rows, rows), rows)
            gr[:, cols] = (up[:, cols].astype(F32) + nt(dq[...], wq[c])).astype(BF)
            return carry

        lax.fori_loop(0, chunks, back, 0)
        late.append(pltpu.make_async_copy(gr, leaving, sem_out.at[2]))
        late[-1].start()
        late.append(pltpu.make_async_copy(gr, g_store.at[micro], sem_out.at[3]))
        late[-1].start()
        for save in [save_up] + late:
            save.wait()

        @pl.when(micro < cut)
        def _():
            for copy in to_swap(False):
                copy.wait()

        @pl.when(micro >= cut)
        def _():
            for copy in to_swap(True):
                copy.wait()


def weight_grads_kernel(scale, par, x_own, x_got, up_own, att_own, att_got, *parts_and_out):
    parts, out_ref = parts_and_out[:-1], parts_and_out[-1]
    flat, width = att_own.shape
    output_sum = tn(up_own[...], att_own[...])
    query_sum = 0.0
    row = 0
    for dq_own, dq_got, up_got in zip(parts[::3], parts[1::3], parts[2::3]):
        count = dq_got.shape[0] * dq_got.shape[2]
        rws = slice(row, row + count)
        query_sum += tn(x_own[rws, :], dq_own[...].reshape(count, width))
        query_sum += tn(x_got[rws, :], dq_got[...].reshape(count, width))
        output_sum += tn(up_got[...].reshape(count, up_got.shape[-1]), att_got[rws, :])
        row += count
    out_ref[:, :width] = (query_sum * scale).astype(BF)
    out_ref[:, width:] = (output_sum * scale).astype(BF)


def attended_kernel(scal, values, probs, a0, a_store, vb, pb, att, sem_v, sem_p, sem_a):
    micros, tokens, width = a_store.shape
    spans = tokens // SPAN
    pairs = width // PAIR

    def get_probs(m):
        return pltpu.make_async_copy(probs.at[m], pb.at[m], sem_p.at[m])

    def put(m):
        return pltpu.make_async_copy(att.at[m], a_store.at[m], sem_a.at[m])

    @pl.when(scal[0] > 0)
    def _():
        get_values = pltpu.make_async_copy(values, vb, sem_v)
        get_values.start()
        for m in range(micros):
            get_probs(m).start()
        get_values.wait()

        def one(m, carry):
            get_probs(m).wait()
            for span in range(spans):
                rws = slice(span * SPAN, (span + 1) * SPAN)
                owners = [scal[1 + (m * spans + span) * K_NBR + k] for k in range(K_NBR)]
                for pair in range(pairs):
                    cols = slice(pair * PAIR, (pair + 1) * PAIR)
                    val = jnp.concatenate([vb[o, :, cols] for o in owners], axis=0)
                    att[m, rws, cols] = head_columns(nn(pb[m, span * pairs + pair], val)).astype(BF)
            put(m).start()
            return carry

        lax.fori_loop(0, micros, one, 0)
        for m in range(micros):
            put(m).wait()


def block_grads_kernel(micros, local, ids, mask, q_ref, d_ref, kv_ref, out_ref, acc):
    reader = pl.program_id(0)
    rows, width = d_ref.shape[1], d_ref.shape[2]
    tokens = rows // micros
    spans = tokens // SPAN
    readers = pl.num_programs(0)

    @pl.when(reader == 0)
    def _():
        acc[...] = jnp.zeros_like(acc)

    def block(r, which):
        start = pl.multiple_of((r % local * 2 + which) * NBR_LEN, NBR_LEN)
        return kv_ref[r // local, pl.ds(start, NBR_LEN), :]

    def unit(index, carry):
        at = [((index // spans * readers + reader) * spans + index % spans) * K_NBR + k for k in range(K_NBR)]
        rws = pl.ds(pl.multiple_of(index * SPAN, SPAN), SPAN)
        refs = [ids[i] for i in at]
        keep = [mask[i] > 0 for i in at]
        zero = jnp.zeros((NBR_LEN, width), BF)
        key = jnp.concatenate([jnp.where(m, block(r, 0), zero) for m, r in zip(keep, refs)], axis=0)
        val = jnp.concatenate([jnp.where(m, block(r, 1), zero) for m, r in zip(keep, refs)], axis=0)
        q_rows = head_rows(q_ref[0, rws, :])
        d_rows = head_rows(d_ref[0, rws, :])
        scores = nt(key, q_rows) * SCALE
        weights = jnp.exp(scores - jnp.max(scores, axis=0, keepdims=True))
        prob = weights / jnp.sum(weights, axis=0, keepdims=True)
        d_probs = nt(val, d_rows)
        delta = jnp.sum(prob * d_probs, axis=0, keepdims=True)
        d_scores = (prob * (d_probs - delta) * SCALE).astype(BF)
        d_keys = nn(d_scores, q_rows)
        d_values = nn(prob.astype(BF), d_rows)
        fzero = jnp.zeros((NBR_LEN, width), F32)
        for k in range(K_NBR):
            part = slice(k * NBR_LEN, (k + 1) * NBR_LEN)
            acc[refs[k], 0] += jnp.where(keep[k], d_keys[part], fzero)
            acc[refs[k], 1] += jnp.where(keep[k], d_values[part], fzero)
        return carry

    lax.fori_loop(0, micros * spans, unit, 0, unroll=4)

    @pl.when(reader == readers - 1)
    def _():
        out_ref[...] = acc[...].astype(BF)


def body(
    section_inputs,
    top_grads,
    query_weight,
    output_weight,
    neighbour_kv,
    nbr_ids,
    send_list,
    send_counts,
):
    n_section = lax.axis_size("section")
    section_index = lax.axis_index("section")
    n_data = lax.axis_size("dp")
    data_index = lax.axis_index("dp")
    inputs_all = section_inputs[0]
    w_query = query_weight[0]
    w_out = output_weight[0]
    owned = neighbour_kv[0]
    micros, tokens, model = inputs_all.shape
    blk_dev = owned.shape[0]
    width = w_query.shape[1]
    spans = tokens // SPAN
    slice_w = width // n_data
    params = functools.partial(pltpu.CompilerParams, vmem_limit_bytes=56 << 20)

    near = n_data // 2
    mates = data_index ^ jnp.arange(near, dtype=jnp.int32)

    def wanted(owner):
        row = lax.dynamic_index_in_dim(send_list, owner, 0, keepdims=False)
        counts = lax.dynamic_index_in_dim(send_counts, owner, 0, keepdims=False)
        return jnp.take(row, mates), jnp.take(counts, mates)

    wants = [wanted(data_index), wanted(data_index ^ near)]

    def across(which, behind):
        own = owned[:, which]
        if behind is not None:
            own, behind = lax.optimization_barrier((own, behind))
        return own, lax.ppermute(own, "dp", [(i, i ^ near) for i in range(n_data)])

    def picked(copies):
        pieces = []
        for k in range(near):
            piece = []
            for blocks, (which_block, counts) in zip(copies, wants):
                chosen = jnp.zeros((NBR_LEN, width), BF)
                for b in range(blk_dev):
                    chosen = jnp.where((which_block[k] == b) & (counts[k] > 0), blocks[b], chosen)
                piece.append(chosen)
            pieces.append(jnp.stack(piece))
        return pieces

    def fetch(pieces):
        moved = [lax.ppermute(pieces[k], "dp", [(i, i ^ k) for i in range(n_data)]) for k in range(1, near)]
        return jnp.concatenate(pieces[:1] + moved, axis=0)

    def exchange(x):
        return lax.all_to_all(x, "dp", split_axis=0, concat_axis=0, tiled=True)

    key_copies = across(0, None)
    value_copies = across(1, key_copies[1])
    key_pieces, inputs_all = lax.optimization_barrier((picked(key_copies), inputs_all))
    keys = fetch(key_pieces)
    query = nn(inputs_all.reshape(micros * tokens, model), w_query).astype(BF)
    held = lax.optimization_barrier((picked(value_copies), query, inputs_all, owned, nbr_ids))
    value_pieces, query, inputs_all, owned, nbr_ids = held
    values = fetch(value_pieces)
    query = query.reshape(micros, tokens, width)
    apart = (nbr_ids // blk_dev).astype(jnp.int32) ^ data_index
    owners = apart % near * 2 + apart // near

    probs = pl.pallas_call(
        probs_kernel,
        cost_estimate=cost(7),
        out_shape=jax.ShapeDtypeStruct((micros, spans * width // PAIR, 2 * SPAN, KEYS), BF),
        grid_spec=pltpu.PrefetchScalarGridSpec(
            num_scalar_prefetch=1,
            grid=(micros,),
            in_specs=[
                pl.BlockSpec((1, tokens, width), lambda i, o: (i, 0, 0)),
                pl.BlockSpec((n_data, NBR_LEN, width), lambda i, o: (0, 0, 0)),
            ],
            out_specs=pl.BlockSpec((1, spans * width // PAIR, 2 * SPAN, KEYS), lambda i, o: (i, 0, 0, 0)),
        ),
        compiler_params=params(),
    )(owners.reshape(-1), query, keys)

    def by_heads(x):
        return jnp.moveaxis(x.reshape(-1, n_data, slice_w), 1, 0)

    q_rows = micros * tokens
    kv_rows = blk_dev * 2 * NBR_LEN
    id_rows = micros * spans * K_NBR
    id_tile = jnp.broadcast_to(nbr_ids.reshape(1, id_rows, 1).astype(BF), (n_data, id_rows, slice_w))
    sliced = jnp.concatenate([by_heads(query), by_heads(owned), id_tile], axis=1)

    partners = [(i, i ^ 1) for i in range(n_data)]
    parity = data_index % 2
    flat = micros * tokens
    halves = n_data // 2
    half = model // 2
    block = model // n_data

    def swap(x):
        return lax.ppermute(x, "dp", partners)

    flat_in = inputs_all.reshape(flat, model)
    inputs_other = jnp.concatenate(
        [lax.dynamic_slice_in_dim(flat_in, (2 * h + 1 - parity) * block, block, axis=1) for h in range(halves)],
        axis=1,
    )

    chunks = 4
    ticks = micros + 2 * (n_section - 1)
    refs = spans * K_NBR
    micro_at = jnp.arange(ticks, dtype=jnp.int32) - 2 * (n_section - 1 - section_index)
    slot_at = jnp.clip(micro_at, 0, micros - 1)
    is_last = (section_index == n_section - 1).astype(jnp.int32)
    other = (1 - parity).astype(jnp.int32)
    table = jnp.concatenate(
        [
            slot_at[:, None],
            ((micro_at >= 0) & (micro_at < micros)).astype(jnp.int32)[:, None],
            jnp.broadcast_to(jnp.stack([is_last, other]), (ticks, 2)),
            jnp.take(owners.reshape(micros, refs), slot_at, axis=0),
        ],
        axis=1,
    ).astype(jnp.int32)
    scal = table.reshape(-1)
    head_major = slice_w % 128 == 0
    d_shape = (n_data, micros, tokens, slice_w) if head_major else (micros, tokens, width)
    cut = micros // 2
    store_shapes = (
        jax.ShapeDtypeStruct((micros, tokens, model), BF),
        jax.ShapeDtypeStruct((micros, tokens, model), BF),
        jax.ShapeDtypeStruct(d_shape, BF),
        jax.ShapeDtypeStruct((micros - cut, 2, tokens, width), BF),
        jax.ShapeDtypeStruct((cut, 2, tokens, width), BF),
    )

    def tick(index, arriving, stores):
        return pl.pallas_call(
            functools.partial(tick_kernel, chunks, index * table.shape[1], head_major),
            out_shape=(jax.ShapeDtypeStruct((tokens, model), BF), *store_shapes),
            in_specs=[pl.BlockSpec(memory_space=pltpu.SMEM)] + [ANY] * 12,
            out_specs=[ANY] * 6,
            scratch_shapes=[
                pltpu.VMEM((tokens, model), BF),
                pltpu.VMEM((chunks, model, width // chunks), BF),
                pltpu.VMEM((chunks, model // chunks, width), BF),
                pltpu.VMEM((refs, NBR_LEN, width), BF),
                pltpu.VMEM((refs, NBR_LEN, width), BF),
                pltpu.VMEM((spans * width // PAIR, 2 * SPAN, KEYS), BF),
                pltpu.VMEM((tokens, width), BF),
                pltpu.VMEM((tokens, width), BF),
                pltpu.VMEM((tokens, model), BF),
                pltpu.SemaphoreType.DMA,
                pltpu.SemaphoreType.DMA((chunks,)),
                pltpu.SemaphoreType.DMA((chunks,)),
                pltpu.SemaphoreType.DMA((refs,)),
                pltpu.SemaphoreType.DMA((refs,)),
                pltpu.SemaphoreType.DMA,
                pltpu.SemaphoreType.DMA((4,)),
                pltpu.SemaphoreType.DMA((halves,)),
                pltpu.SemaphoreType.DMA((n_data if head_major else 1,)),
            ],
            input_output_aliases={8: 1, 9: 2, 10: 3, 11: 4, 12: 5},
            cost_estimate=cost(11),
            compiler_params=params(),
        )(scal, arriving, top_grads, w_out, w_query, keys, values, probs, *stores)

    def unwritten(*shapes):
        return pl.pallas_call(
            lambda *refs: None,
            out_shape=shapes,
            out_specs=[ANY] * len(shapes),
        )()

    def attend(enabled, store):
        return pl.pallas_call(
            attended_kernel,
            out_shape=jax.ShapeDtypeStruct((micros, tokens, width), BF),
            grid_spec=pltpu.PrefetchScalarGridSpec(
                num_scalar_prefetch=1,
                grid=(1,),
                in_specs=[ANY] * 3,
                out_specs=ANY,
                scratch_shapes=[
                    pltpu.VMEM((n_data, NBR_LEN, width), BF),
                    pltpu.VMEM((micros, spans * width // PAIR, 2 * SPAN, KEYS), BF),
                    pltpu.VMEM((micros, tokens, width), BF),
                    pltpu.SemaphoreType.DMA,
                    pltpu.SemaphoreType.DMA((micros,)),
                    pltpu.SemaphoreType.DMA((micros,)),
                ],
            ),
            input_output_aliases={3: 0},
            cost_estimate=cost(5),
            compiler_params=params(),
        )(jnp.concatenate([enabled[None].astype(jnp.int32), owners.reshape(-1)]), values, probs, store)

    *stores, attended = unwritten(*store_shapes, jax.ShapeDtypeStruct((micros, tokens, width), BF))
    arrived = [jnp.zeros((tokens, model), BF)] * 2
    got = []
    for index in range(ticks):
        if index == micros + 3:
            arrived[index], attended_got = lax.optimization_barrier((arrived[index], attended_got))
        leaving, *stores = tick(index, arrived[index], stores)
        if index == 0:
            sliced, inputs_other, leaving, attended = lax.optimization_barrier((sliced, inputs_other, leaving, attended))
            sliced = exchange(sliced)
            inputs_got = swap(inputs_other)
            attended = attend(1 - is_last, attended)
            stores[0], attended = lax.optimization_barrier((stores[0], attended))
        hops = []
        for s in range(1, n_section):
            if 0 <= index - 2 * (n_section - 1 - s) < micros:
                hops.append((s, s - 1))
        if index > 0:
            held = lax.optimization_barrier((leaving, arrived[index + 1]))
            if hops:
                leaving, arrived[index + 1] = held
        arrived.append(lax.ppermute(leaving, "section", hops) if hops else leaving)
        if index == micros:
            attended = attend(is_last, attended)
            stores[0], attended = lax.optimization_barrier((stores[0], attended))
            held = lax.optimization_barrier((arrived[index + 1], sliced, inputs_got))
            arrived[index + 1], sliced, inputs_got = held
            attended_got = swap(attended.reshape(flat, width))
        if index == ticks - micros + cut - 1:
            stores[4], arrived[index + 1] = lax.optimization_barrier((stores[4], arrived[index + 1]))
            got.append(swap(stores[4]))
    grads_in, upstream, d_store, s_late, s_early = stores
    got[0], s_late, d_store = lax.optimization_barrier((got[0], s_late, d_store))
    got.append(swap(s_late))
    grad_scale = (flat * n_data) ** (-0.5)
    parts = []
    part_specs = []
    for own, part in zip((s_early, s_late), got):
        count = part.shape[0]
        parts += [own, part, part]
        part_specs += [
            pl.BlockSpec((count, 1, tokens, width), lambda j, p: (0, 0, 0, 0)),
            pl.BlockSpec((count, 1, tokens, width), lambda j, p: (0, 0, 0, 0)),
            pl.BlockSpec((count, 1, tokens, block), lambda j, p: (0, 1, 0, j)),
        ]
    terms = pl.pallas_call(
        functools.partial(weight_grads_kernel, grad_scale),
        cost_estimate=cost(9),
        out_shape=jax.ShapeDtypeStruct((half, 2 * width), BF),
        grid_spec=pltpu.PrefetchScalarGridSpec(
            num_scalar_prefetch=1,
            grid=(halves,),
            in_specs=[
                pl.BlockSpec((flat, block), lambda j, p: (0, 2 * j + p[0])),
                pl.BlockSpec((flat, block), lambda j, p: (0, j)),
                pl.BlockSpec((flat, block), lambda j, p: (0, 2 * j + p[0])),
                pl.BlockSpec((flat, width), lambda j, p: (0, 0)),
                pl.BlockSpec((flat, width), lambda j, p: (0, 0)),
                *part_specs,
            ],
            out_specs=pl.BlockSpec((block, 2 * width), lambda j, p: (j, 0)),
        ),
        compiler_params=params(),
    )(
        parity[None].astype(jnp.int32),
        inputs_all.reshape(flat, model),
        inputs_got,
        upstream.reshape(flat, model),
        attended.reshape(flat, width),
        attended_got,
        *parts,
    )
    d_heads = exchange(d_store) if head_major else exchange(by_heads(d_store))
    d_heads = d_heads.reshape(n_data, q_rows, slice_w)
    terms, d_heads = lax.optimization_barrier((terms, d_heads))
    shares = lax.psum_scatter(
        terms,
        "dp",
        scatter_dimension=0,
        tiled=True,
        axis_index_groups=[list(range(p, n_data, 2)) for p in range(2)],
    )

    ids_all = sliced[:, q_rows + kv_rows :, 0].astype(jnp.int32).reshape(n_data, micros, spans, K_NBR)
    ids_all = jnp.moveaxis(ids_all, 0, 1).reshape(micros, n_data * spans, K_NBR)
    owner_all = ids_all // blk_dev
    reader_all = (jnp.arange(n_data * spans, dtype=jnp.int32) // spans)[None, :, None]
    hit_owner = owner_all[..., None] == jnp.arange(n_data, dtype=jnp.int32)
    list_r = jnp.take(send_list, reader_all[0, :, 0], axis=1).T[None, :, None, :]
    count_r = jnp.take(send_counts, reader_all[0, :, 0], axis=1).T[None, :, None, :]
    block_all = owner_all * blk_dev + jnp.sum(jnp.where(hit_owner, list_r, 0), axis=-1)
    mask_all = jnp.sum(jnp.where(hit_owner, count_r, 0), axis=-1)
    blocks = n_data * blk_dev
    block_grads = pl.pallas_call(
        functools.partial(block_grads_kernel, micros, blk_dev),
        cost_estimate=cost(37),
        out_shape=jax.ShapeDtypeStruct((blocks, 2, NBR_LEN, slice_w), BF),
        grid_spec=pltpu.PrefetchScalarGridSpec(
            num_scalar_prefetch=2,
            grid=(n_data,),
            in_specs=[
                pl.BlockSpec((1, q_rows, slice_w), lambda i, a, b: (i, 0, 0)),
                pl.BlockSpec((1, q_rows, slice_w), lambda i, a, b: (i, 0, 0)),
                pl.BlockSpec((n_data, kv_rows, slice_w), lambda i, a, b: (0, q_rows // kv_rows, 0)),
            ],
            out_specs=pl.BlockSpec((blocks, 2, NBR_LEN, slice_w), lambda i, a, b: (0, 0, 0, 0)),
            scratch_shapes=[pltpu.VMEM((blocks, 2, NBR_LEN, slice_w), F32)],
        ),
        compiler_params=params(),
    )(block_all.reshape(-1).astype(jnp.int32), mask_all.reshape(-1).astype(jnp.int32), sliced, d_heads, sliced)
    returned = exchange(block_grads.reshape(n_data, blk_dev, 2, NBR_LEN, slice_w))
    kv_grads = jnp.moveaxis(returned, 0, -2).reshape(blk_dev, 2, NBR_LEN, width)
    return (
        grads_in[None],
        shares[None, :, :width],
        shares[None, :, width:],
        kv_grads[None],
    )


def solution(mesh):
    in_specs = (
        P("section", None, "dp", None),
        P(None, "dp", None),
        P("section", None, None),
        P("section", None, None),
        P("section", "dp", None, None, None),
        P(None, "dp", None),
        P(),
        P(),
    )
    out_specs = (
        P("section", None, "dp", None),
        P("section", "dp", None),
        P("section", "dp", None),
        P("section", "dp", None, None, None),
    )
    return jax.shard_map(body, mesh=mesh, in_specs=in_specs, out_specs=out_specs, check_vma=False)
```

profile of v0, /device:TPU:9, one launch (start us, length us, event | category | flops | bytes accessed | tf_op | source)
XLA Modules:
  0.0 376.8 jit_solution(17577591690848611480)
XLA Ops:
  7.2 1.3 copy.142
  8.5 0.9 slice_bitcast_fusion.2
  9.4 2.3 collective-permute-start
  32.6 1.9 collective-permute-done
  34.4 3.1 collective-permute-start.1
  37.5 1.1 select_select_fusion.5
  38.8 0.8 pad_maximum_fusion.8
  39.6 0.9 pad_maximum_fusion.7
  40.5 0.8 pad_maximum_fusion.6
  41.3 1.2 collective-permute-start.2
  42.6 1.4 collective-permute-start.4
  44.1 3.3 convolution_convert_fusion
  47.4 10.3 %collective-permute-done.1 = bf16[2,128,1024]{2,1,0:T(8,128)(2,1)S(1)} collective-permute-done((bf16[2,128,1024]{2,1,0:T(8,128)(2,1)}, bf16[2,128,1024]{2,1,0:T(8,128)(2,1)S(1)}, u32[]{:S(2)}, u32[]{:S(2)}) %collective-permute-start.1) | collective-permute-done | bytes 524320 | tf_op jit(solution)/shard_map/ppermute | solution.py:375
  58.6 0.8 pad_maximum_fusion.3
  59.5 0.8 pad_maximum_fusion.1
  60.3 0.9 pad_maximum_fusion.2
  63.5 1.0 collective-permute-start.5
  64.5 1.3 collective-permute-start.6
  66.4 2.3 copy.120
  68.7 2.3 copy.121
  71.5 1.1 constant_dynamic-update-slice_fusion.2
  72.6 1.1 constant_dynamic-update-slice_fusion.1
  73.7 1.9 maximum_maximum_fusion
  75.5 1.1 constant_dynamic-update-slice_fusion.k_ref.keys
  76.6 1.4 copy-done.2
  78.0 7.5 %shard_map.111.probs = bf16[4,16,128,256]{3,2,1,0:T(8,128)(2,1)} custom-call(s32[16]{0:T(128)} %reshape.318.owners, bf16[4,128,1024]{2,1,0:T(8,128)(2,1)} %bitcast.122, bf16[8,128,1024]{2,1,0:T(8,128)(2,1)} %copy-done.2), custom_call_target="tpu_custom_call" | custom-call | bytes 25200000 | tf_op jit(solution)/shard_map/pallas_call | solution.py:408
  85.7 1.1 pad_maximum_fusion
  86.8 1.1 constant_dynamic-update-slice_fusion.6
  87.9 1.1 constant_dynamic-update-slice_fusion.5
  89.0 7.6 %collective-permute-done.7 = bf16[2,128,1024]{2,1,0:T(8,128)(2,1)} collective-permute-done((bf16[2,128,1024]{2,1,0:T(8,128)(2,1)}, bf16[2,128,1024]{2,1,0:T(8,128)(2,1)}, u32[]{:S(2)}, u32[]{:S(2)}) %collective-permute-start.7) | collective-permute-done | bytes 524320 | tf_op jit(solution)/shard_map/ppermute | solution.py:390
  96.6 1.1 constant_dynamic-update-slice_fusion.4.values
  97.7 0.9 broadcast_in_dim.76.arriving
  99.2 1.0 shard_map.113
  100.2 7.2 %all-to-all-start = ((bf16[8,1040,128]{2,1,0:T(8,128)(2,1)}), bf16[8,1040,128]{2,1,0:T(8,128)(2,1)S(1)}, u32[]{:S(2)}, u32[]{:S(2)}) async-start(bf16[8,1040,128]{2,1,0:T(8,128)(2,1)} %maximum_maximum_fusion), calls=%async_computation | async-start | bytes 4259840 | tf_op jit(solution)/shard_map/all_to_all | solution.py:394
  108.7 5.7 %shard_map.114.a0 = bf16[4,128,1024]{2,1,0:T(8,128)(2,1)} custom-call(s32[17]{0:T(128)} %get-tuple-element.265.scal, bf16[8,128,1024]{2,1,0:T(8,128)(2,1)} %copy-done.1, bf16[4,16,128,256]{3,2,1,0:T(8,128)(2,1)} %shard_map.111.probs, bf16[4,128,1024]{2,1,0:T(8,128)(2,1)} %get-tuple-element.140.a0), custom_call_target="tpu_custom_call", output_to_operand_aliasing={{}: (3, {})} | custom-call | bytes 18000000 | tf_op jit(solution)/shard_map/pallas_call | solution.py:516
  114.4 1.0 shard_map.115
  116.2 1.0 shard_map.116
  117.2 1.5 collective-permute-start.10
  118.7 1.2 collective-permute-start.12
  119.9 1.0 shard_map.117
  120.9 22.2 %collective-permute-done.10.arriving = bf16[128,2048]{1,0:T(8,128)(2,1)S(1)} collective-permute-done((bf16[128,2048]{1,0:T(8,128)(2,1)}, bf16[128,2048]{1,0:T(8,128)(2,1)S(1)}, u32[]{:S(2)}, u32[]{:S(2)}) %collective-permute-start.10) | collective-permute-done | bytes 524320 | tf_op jit(solution)/shard_map/ppermute | solution.py:559
  143.1 1.3 collective-permute-start.11
  144.4 10.6 %shard_map.118 = (bf16[128,2048]{1,0:T(8,128)(2,1)}, bf16[4,128,2048]{2,1,0:T(8,128)(2,1)}, bf16[4,128,2048]{2,1,0:T(8,128)(2,1)}, bf16[8,4,128,128]{3,2,1,0:T(8...) custom-call(s32[80]{0:T(128)} %reshape.317.scal, ...), custom_call_target="tpu_custom_call", output_to_operand_aliasing={{1}: (8, {}), {2}: (9, {}), {3}: (10, {}), {4}: (11, {}), {... | custom-call | bytes 39600000 | tf_op jit(solution)/shard_map/pallas_call | solution.py:478
  155.0 2.0 collective-permute-done.11.arriving
  157.0 1.9 collective-permute-start.13
  160.1 10.6 %shard_map.120 = (bf16[128,2048]{1,0:T(8,128)(2,1)}, bf16[4,128,2048]{2,1,0:T(8,128)(2,1)}, bf16[4,128,2048]{2,1,0:T(8,128)(2,1)}, bf16[8,4,128,128]{3,2,1,0:T(8...) custom-call(s32[80]{0:T(128)} %reshape.317.scal, ...), custom_call_target="tpu_custom_call", output_to_operand_aliasing={{1}: (8, {}), {2}: (9, {}), {3}: (10, {}), {4}: (11, {}), {... | custom-call | bytes 39600000 | tf_op jit(solution)/shard_map/pallas_call | solution.py:478
  170.8 1.9 collective-permute-start.14
  172.7 10.6 %shard_map.121 = (bf16[128,2048]{1,0:T(8,128)(2,1)}, bf16[4,128,2048]{2,1,0:T(8,128)(2,1)}, bf16[4,128,2048]{2,1,0:T(8,128)(2,1)}, bf16[8,4,128,128]{3,2,1,0:T(8...) custom-call(s32[80]{0:T(128)} %reshape.317.scal, ...), custom_call_target="tpu_custom_call", output_to_operand_aliasing={{1}: (8, {}), {2}: (9, {}), {3}: (10, {}), {4}: (11, {}), {... | custom-call | bytes 39600000 | tf_op jit(solution)/shard_map/pallas_call | solution.py:478
  183.3 2.5 collective-permute-done.14.arriving
  185.8 1.3 collective-permute-start.16
  187.1 10.6 %shard_map.122 = (bf16[128,2048]{1,0:T(8,128)(2,1)}, bf16[4,128,2048]{2,1,0:T(8,128)(2,1)}, bf16[4,128,2048]{2,1,0:T(8,128)(2,1)}, bf16[8,4,128,128]{3,2,1,0:T(8...) custom-call(s32[80]{0:T(128)} %reshape.317.scal, ...), custom_call_target="tpu_custom_call", output_to_operand_aliasing={{1}: (8, {}), {2}: (9, {}), {3}: (10, {}), {4}: (11, {}), {... | custom-call | bytes 39600000 | tf_op jit(solution)/shard_map/pallas_call | solution.py:478
  197.8 1.3 collective-permute-start.17
  199.2 15.7 %collective-permute-done.18.parts_and_out_1_.parts_and_out_2_ = bf16[2,2,128,1024]{3,2,1,0:T(8,128)(2,1)} collective-permute-done((bf16[2,2,128,1024]{3,2,1,0:T(8,128)(2,1)}, bf16[2,2,128,1024]{3,2,1,0:T(8,128)(2,1)}, u32[]{:S(2)}, u32[]{:S(2)}) %collective-permute-start.18) | collective-permute-done | bytes 1048608 | tf_op jit(solution)/shard_map/ppermute | solution.py:441
  214.8 1.0 shard_map.123
  216.6 1.0 shard_map.124
  217.6 4.3 %all-to-all-start.1 = ((bf16[8,4,128,128]{3,2,1,0:T(8,128)(2,1)}), bf16[8,4,128,128]{3,2,1,0:T(8,128)(2,1)}, u32[]{:S(2)}, u32[]{:S(2)}) async-start(bf16[8,4,128,128]{3,2,1,0:T(8,128)(2,1)} %get-tuple-element.226), calls=%async_computation.1 | async-start | bytes 2097152 | tf_op jit(solution)/shard_map/all_to_all | solution.py:394
  222.4 25.3 %collective-permute-done.19.parts_and_out_4_.parts_and_out_5_ = bf16[2,2,128,1024]{3,2,1,0:T(8,128)(2,1)S(1)} collective-permute-done((bf16[2,2,128,1024]{3,2,1,0:T(8,128)(2,1)S(1)}, bf16[2,2,128,1024]{3,2,1,0:T(8,128)(2,1)S(1)}, u32[]{:S(2)}, u32[]{:S(2)}) %collective-permute-start.19) | collective-permute-done | bytes 1048608 | tf_op jit(solution)/shard_map/ppermute | solution.py:441
  247.8 1.0 copy-done.7
  248.8 9.0 %shard_map.125 = bf16[1024,2048]{1,0:T(8,128)(2,1)} custom-call(s32[1]{0:T(128)} %bitcast.44.par, bf16[512,2048]{1,0:T(8,128)(2,1)} %bitcast.112, bf16[512,1024]{1,0:T(8,128)(2,1)} %collective-permute-done.12.x_got, bf16[512,2048]{1,0:T(8,128)(2,1)} %bitcast.106, bf16[512,1024]{1,0:T(8,128)(2,1)} %bitcast.109, bf16[512,1024]{1,0:T(8,128)(2,1)} %copy-done.11, ...), custom_call_target="tpu_custom_call" | custom-call | bytes 32400000 | tf_op jit(solution)/shard_map/pallas_call | solution.py:583
  261.6 25.6 %shard_map.126 = bf16[16,2,128,128]{3,2,1,0:T(8,128)(2,1)} custom-call(s32[128]{0:T(128)} %multiply_add_fusion.ids, s32[128]{0:T(128)} %reshape.327.mask, bf16[8,1040,128]{2,1,0:T(8,128)(2,1)} %copy-done.4, bf16[8,512,128]{2,1,0:T(8,128)(2,1)} %bitcast.46.d_ref, bf16[8,1040,128]{2,1,0:T(8,128)(2,1)} %copy-done.4), custom_call_target="tpu_custom_call" | custom-call | bytes 133200000 | tf_op jit(solution)/shard_map/pallas_call | solution.py:631
  287.2 53.2 %all_to_all.15 = bf16[8,2,2,128,128]{4,3,2,1,0:T(8,128)(2,1)S(1)} all-to-all(bf16[8,2,2,128,128]{4,3,2,1,0:T(8,128)(2,1)} %bitcast.121), channel_id=1, replica_groups=mesh['section'=4,'dp'=8] {'dp'}, dimensions={0} | all-to-all | bytes 2097152 | tf_op jit(solution)/shard_map/all_to_all | solution.py:394
  341.1 1.3 broadcast_in_dim_reshape.3
  342.3 25.4 %reduce-scatter.2.cloned.1.call-done = bf16[256,2048]{1,0:T(8,128)(2,1)} async-done(((bf16[1024,2048]{1,0:T(8,128)(2,1)}), bf16[256,2048]{1,0:T(8,128)(2,1)}) %reduce-scatter.2.cloned.1.call-update) | async-done | bytes 1048592 | tf_op jit(solution)/shard_map/reduce_scatter | solution.py:613
  367.7 2.2 slice_bitcast_fusion
  (136 shorter events, 19.8 us)
Async XLA Ops:
  7.2 4.6 %copy-start.19 = (s32[8,8]{1,0:T(8,128)S(1)}, s32[8,8]{1,0:T(8,128)}, u32[]{:S(2)}) copy-start(s32[8,8]{1,0:T(8,128)} %param.18) | copy-start | bytes 772
  7.2 4.6 %copy-start.20 = (s32[8,8]{1,0:T(8,128)S(1)}, s32[8,8]{1,0:T(8,128)}, u32[]{:S(2)}) copy-start(s32[8,8]{1,0:T(8,128)} %param.19) | copy-start | bytes 772
  8.5 24.0 %copy-start.9 = (bf16[1,2,2,128,1024]{4,3,2,1,0:T(8,128)(2,1)S(1)}, bf16[1,2,2,128,1024]{4,3,2,1,0:T(8,128)(2,1)}, u32[]{:S(2)}) copy-start(bf16[1,2,2,128,1024]{4,3,2,1,0:T(8,128)(2,1)} %param.16) | copy-start | bytes 3145732
  9.4 25.1 %collective-permute-start = (bf16[2,128,1024]{2,1,0:T(8,128)(2,1)S(1)}, bf16[2,128,1024]{2,1,0:T(8,128)(2,1)S(1)}, u32[]{:S(2)}, u32[]{:S(2)}) collective-permute-start(bf16[2,128,1024]{2,1,0:T(8,128)(2,1)S(1)} %get-tuple-element.242), channel_id=1, source_target_pairs={{0,4},{1,5},{2,6},{3,7},{4,0},{5,1},{6,2},{7,3},{8,12},{9,13},{10,... | collective-permute-start | bytes 1572872 | tf_op jit(solution)/shard_map/ppermute | solution.py:375
  34.4 23.3 %collective-permute-start.1 = (bf16[2,128,1024]{2,1,0:T(8,128)(2,1)}, bf16[2,128,1024]{2,1,0:T(8,128)(2,1)S(1)}, u32[]{:S(2)}, u32[]{:S(2)}) collective-permute-start(bf16[2,128,1024]{2,1,0:T(8,128)(2,1)} %get-tuple-element.118), channel_id=1, source_target_pairs={{0,4},{1,5},{2,6},{3,7},{4,0},{5,1},{6,2},{7,3},{8,12},{9,13},{10,... | collective-permute-start | bytes 1572872 | tf_op jit(solution)/shard_map/ppermute | solution.py:375
  38.6 5.4 %copy-start.5 = (bf16[1,4,128,2048]{3,2,1,0:T(8,128)(2,1)S(1)}, bf16[1,4,128,2048]{3,2,1,0:T(8,128)(2,1)}, u32[]{:S(2)}) copy-start(bf16[1,4,128,2048]{3,2,1,0:T(8,128)(2,1)} %param.12) | copy-start | bytes 6291460
  39.6 4.5 %copy-start = (bf16[1,2048,1024]{2,1,0:T(8,128)(2,1)S(1)}, bf16[1,2048,1024]{2,1,0:T(8,128)(2,1)}, u32[]{:S(2)}) copy-start(bf16[1,2048,1024]{2,1,0:T(8,128)(2,1)} %param.14) | copy-start | bytes 12582916
  41.3 29.6 %collective-permute-start.2 = (bf16[2,128,1024]{2,1,0:T(8,128)(2,1)}, bf16[2,128,1024]{2,1,0:T(8,128)(2,1)}, u32[]{:S(2)}, u32[]{:S(2)}) collective-permute-start(bf16[2,128,1024]{2,1,0:T(8,128)(2,1)} %pad_maximum_fusion.6), channel_id=1, source_target_pairs={{0,1},{1,0},{2,3},{3,2},{4,5},{5,4},{6,7},{7,6},{8,9},{9,8},{10,11... | collective-permute-start | bytes 1572872 | tf_op jit(solution)/shard_map/ppermute | solution.py:390
  42.6 30.0 %collective-permute-start.3 = (bf16[2,128,1024]{2,1,0:T(8,128)(2,1)}, bf16[2,128,1024]{2,1,0:T(8,128)(2,1)}, u32[]{:S(2)}, u32[]{:S(2)}) collective-permute-start(bf16[2,128,1024]{2,1,0:T(8,128)(2,1)} %pad_maximum_fusion.7), channel_id=1, source_target_pairs={{0,2},{1,3},{2,0},{3,1},{4,6},{5,7},{6,4},{7,5},{8,10},{9,11},{10,... | collective-permute-start | bytes 1572872 | tf_op jit(solution)/shard_map/ppermute | solution.py:390
  42.6 32.9 %collective-permute-start.4 = (bf16[2,128,1024]{2,1,0:T(8,128)(2,1)}, bf16[2,128,1024]{2,1,0:T(8,128)(2,1)}, u32[]{:S(2)}, u32[]{:S(2)}) collective-permute-start(bf16[2,128,1024]{2,1,0:T(8,128)(2,1)} %pad_maximum_fusion.8), channel_id=1, source_target_pairs={{0,3},{1,2},{2,1},{3,0},{4,7},{5,6},{6,5},{7,4},{8,11},{9,10},{10,... | collective-permute-start | bytes 1572872 | tf_op jit(solution)/shard_map/ppermute | solution.py:390
  57.8 3.4 copy-start.22
  63.5 23.3 %collective-permute-start.5 = (bf16[2,128,1024]{2,1,0:T(8,128)(2,1)}, bf16[2,128,1024]{2,1,0:T(8,128)(2,1)}, u32[]{:S(2)}, u32[]{:S(2)}) collective-permute-start(bf16[2,128,1024]{2,1,0:T(8,128)(2,1)} %pad_maximum_fusion.2), channel_id=1, source_target_pairs={{0,1},{1,0},{2,3},{3,2},{4,5},{5,4},{6,7},{7,6},{8,9},{9,8},{10,11... | collective-permute-start | bytes 1572872 | tf_op jit(solution)/shard_map/ppermute | solution.py:390
  64.5 23.3 %collective-permute-start.6 = (bf16[2,128,1024]{2,1,0:T(8,128)(2,1)}, bf16[2,128,1024]{2,1,0:T(8,128)(2,1)}, u32[]{:S(2)}, u32[]{:S(2)}) collective-permute-start(bf16[2,128,1024]{2,1,0:T(8,128)(2,1)} %pad_maximum_fusion.3), channel_id=1, source_target_pairs={{0,2},{1,3},{2,0},{3,1},{4,6},{5,7},{6,4},{7,5},{8,10},{9,11},{10,... | collective-permute-start | bytes 1572872 | tf_op jit(solution)/shard_map/ppermute | solution.py:390
  70.9 2.7 copy-start.8
  71.0 25.7 %collective-permute-start.7 = (bf16[2,128,1024]{2,1,0:T(8,128)(2,1)}, bf16[2,128,1024]{2,1,0:T(8,128)(2,1)}, u32[]{:S(2)}, u32[]{:S(2)}) collective-permute-start(bf16[2,128,1024]{2,1,0:T(8,128)(2,1)} %pad_maximum_fusion.4), channel_id=1, source_target_pairs={{0,3},{1,2},{2,1},{3,0},{4,7},{5,6},{6,5},{7,4},{8,11},{9,10},{10,... | collective-permute-start | bytes 1572872 | tf_op jit(solution)/shard_map/ppermute | solution.py:390
  76.6 1.4 copy-start.2
  78.0 7.5 %copy-start.10 = (bf16[2,128,1024]{2,1,0:T(8,128)(2,1)S(1)}, bf16[2,128,1024]{2,1,0:T(8,128)(2,1)}, u32[]{:S(2)}) copy-start(bf16[2,128,1024]{2,1,0:T(8,128)(2,1)} %pad_maximum_fusion.1) | copy-start | bytes 1572868
  78.0 7.5 %copy-start.6 = (bf16[1,4,128,2048]{3,2,1,0:T(8,128)(2,1)S(1)}, bf16[1,4,128,2048]{3,2,1,0:T(8,128)(2,1)}, u32[]{:S(2)}) copy-start(bf16[1,4,128,2048]{3,2,1,0:T(8,128)(2,1)} %param.12) | copy-start | bytes 6291460
  97.7 1.5 copy-start.1
  100.2 7.9 %copy-start.21 = (s32[16]{0:T(128)S(1)}, s32[16]{0:T(128)}, u32[]{:S(2)}) copy-start(s32[16]{0:T(128)} %reshape.318.owners) | copy-start | bytes 196
  100.2 59.9 %all-to-all-start = ((bf16[8,1040,128]{2,1,0:T(8,128)(2,1)}), bf16[8,1040,128]{2,1,0:T(8,128)(2,1)S(1)}, u32[]{:S(2)}, u32[]{:S(2)}) async-start(bf16[8,1040,128]{2,1,0:T(8,128)(2,1)} %maximum_maximum_fusion), calls=%async_computation | async-start | bytes 4259840 | tf_op jit(solution)/shard_map/all_to_all | solution.py:394
  107.4 8.0 %collective-permute-start.8 = (bf16[128,2048]{1,0:T(8,128)(2,1)}, bf16[128,2048]{1,0:T(8,128)(2,1)S(1)}, u32[]{:S(2)}, u32[]{:S(2)}) collective-permute-start(bf16[128,2048]{1,0:T(8,128)(2,1)} %get-tuple-element.147), channel_id=1, source_target_pairs={{24,16},{25,17},{26,18},{27,19},{28,20},{29,21},{30,22},{31,23}} | collective-permute-start | bytes 1572872 | tf_op jit(solution)/shard_map/ppermute | solution.py:559
  115.4 0.8 copy-start.13
  115.4 1.8 collective-permute-start.9
  117.2 2.7 copy-start.15
  117.2 25.9 %collective-permute-start.10 = (bf16[128,2048]{1,0:T(8,128)(2,1)}, bf16[128,2048]{1,0:T(8,128)(2,1)S(1)}, u32[]{:S(2)}, u32[]{:S(2)}) collective-permute-start(bf16[128,2048]{1,0:T(8,128)(2,1)} %get-tuple-element.163), channel_id=1, source_target_pairs={{16,8},{24,16},{17,9},{25,17},{18,10},{26,18},{19,11},{27,19},{20,... | collective-permute-start | bytes 1572872 | tf_op jit(solution)/shard_map/ppermute | solution.py:559
  118.7 41.4 %collective-permute-start.12 = (bf16[512,1024]{1,0:T(8,128)(2,1)}, bf16[512,1024]{1,0:T(8,128)(2,1)}, u32[]{:S(2)}, u32[]{:S(2)}) collective-permute-start(bf16[512,1024]{1,0:T(8,128)(2,1)} %pad_maximum_fusion), channel_id=1, source_target_pairs={{0,1},{1,0},{2,3},{3,2},{4,5},{5,4},{6,7},{7,6},{8,9},{9,8},{10,11... | collective-permute-start | bytes 3145736 | tf_op jit(solution)/shard_map/ppermute | solution.py:441
  143.1 1.3 copy-start.16
  143.1 13.9 %collective-permute-start.11 = (bf16[128,2048]{1,0:T(8,128)(2,1)}, bf16[128,2048]{1,0:T(8,128)(2,1)S(1)}, u32[]{:S(2)}, u32[]{:S(2)}) collective-permute-start(bf16[128,2048]{1,0:T(8,128)(2,1)} %get-tuple-element.171), channel_id=1, source_target_pairs={{16,8},{24,16},{17,9},{25,17},{18,10},{26,18},{19,11},{27,19},{20,... | collective-permute-start | bytes 1572872 | tf_op jit(solution)/shard_map/ppermute | solution.py:559
  157.0 2.7 copy-start.12
  157.0 13.7 %collective-permute-start.13 = (bf16[128,2048]{1,0:T(8,128)(2,1)}, bf16[128,2048]{1,0:T(8,128)(2,1)}, u32[]{:S(2)}, u32[]{:S(2)}) collective-permute-start(bf16[128,2048]{1,0:T(8,128)(2,1)} %get-tuple-element.184), channel_id=1, source_target_pairs={{8,0},{16,8},{9,1},{17,9},{10,2},{18,10},{11,3},{19,11},{12,4},{20... | collective-permute-start | bytes 1572872 | tf_op jit(solution)/shard_map/ppermute | solution.py:559
  159.7 27.4 %collective-permute-start.15 = (bf16[512,1024]{1,0:T(8,128)(2,1)}, bf16[512,1024]{1,0:T(8,128)(2,1)S(1)}, u32[]{:S(2)}, u32[]{:S(2)}) collective-permute-start(bf16[512,1024]{1,0:T(8,128)(2,1)} %bitcast.108), channel_id=1, source_target_pairs={{0,1},{1,0},{2,3},{3,2},{4,5},{5,4},{6,7},{7,6},{8,9},{9,8},{10,11... | collective-permute-start | bytes 3145736 | tf_op jit(solution)/shard_map/ppermute | solution.py:441
  160.1 99.2 %copy-start.4 = (bf16[8,1040,128]{2,1,0:T(8,128)(2,1)}, bf16[8,1040,128]{2,1,0:T(8,128)(2,1)S(1)}, u32[]{:S(2)}) copy-start(bf16[8,1040,128]{2,1,0:T(8,128)(2,1)S(1)} %all-to-all-done.q_ref.kv_ref) | copy-start | bytes 6389764
  170.8 15.0 %collective-permute-start.14 = (bf16[128,2048]{1,0:T(8,128)(2,1)}, bf16[128,2048]{1,0:T(8,128)(2,1)S(1)}, u32[]{:S(2)}, u32[]{:S(2)}) collective-permute-start(bf16[128,2048]{1,0:T(8,128)(2,1)} %get-tuple-element.192), channel_id=1, source_target_pairs={{8,0},{16,8},{9,1},{17,9},{10,2},{18,10},{11,3},{19,11},{12,4},{20... | collective-permute-start | bytes 1572872 | tf_op jit(solution)/shard_map/ppermute | solution.py:559
  185.8 1.3 copy-start.18
  185.8 11.9 %collective-permute-start.16 = (bf16[128,2048]{1,0:T(8,128)(2,1)}, bf16[128,2048]{1,0:T(8,128)(2,1)S(1)}, u32[]{:S(2)}, u32[]{:S(2)}) collective-permute-start(bf16[128,2048]{1,0:T(8,128)(2,1)} %get-tuple-element.202), channel_id=1, source_target_pairs={{8,0},{9,1},{10,2},{11,3},{12,4},{13,5},{14,6},{15,7}} | collective-permute-start | bytes 1572872 | tf_op jit(solution)/shard_map/ppermute | solution.py:559
  187.1 10.6 %copy-start.11 = (bf16[512,1024]{1,0:T(8,128)(2,1)}, bf16[512,1024]{1,0:T(8,128)(2,1)S(1)}, u32[]{:S(2)}) copy-start(bf16[512,1024]{1,0:T(8,128)(2,1)S(1)} %collective-permute-done.15.att_got) | copy-start | bytes 3145732
  197.7 17.1 %copy-start.14 = (bf16[128,2048]{1,0:T(8,128)(2,1)}, bf16[128,2048]{1,0:T(8,128)(2,1)S(1)}, u32[]{:S(2)}) copy-start(bf16[128,2048]{1,0:T(8,128)(2,1)S(1)} %collective-permute-done.16.arriving) | copy-start | bytes 1572868
  197.7 17.1 %collective-permute-start.18 = (bf16[2,2,128,1024]{3,2,1,0:T(8,128)(2,1)}, bf16[2,2,128,1024]{3,2,1,0:T(8,128)(2,1)}, u32[]{:S(2)}, u32[]{:S(2)}) collective-permute-start(bf16[2,2,128,1024]{3,2,1,0:T(8,128)(2,1)} %get-tuple-element.211.sa0), channel_id=1, source_target_pairs={{0,1},{1,0},{2,3},{3,2},{4,5},{5,4},{6,7},{7,6},{8,9},{9,8},{10,11... | collective-permute-start | bytes 3145736 | tf_op jit(solution)/shard_map/ppermute | solution.py:441
  197.8 18.0 %collective-permute-start.17 = (bf16[128,2048]{1,0:T(8,128)(2,1)}, bf16[128,2048]{1,0:T(8,128)(2,1)S(1)}, u32[]{:S(2)}, u32[]{:S(2)}) collective-permute-start(bf16[128,2048]{1,0:T(8,128)(2,1)} %get-tuple-element.203), channel_id=1, source_target_pairs={{8,0},{9,1},{10,2},{11,3},{12,4},{13,5},{14,6},{15,7}} | collective-permute-start | bytes 1572872 | tf_op jit(solution)/shard_map/ppermute | solution.py:559
  215.8 0.8 copy-start.17
  217.6 4.6 %copy-start.3 = (bf16[2,2,128,1024]{3,2,1,0:T(8,128)(2,1)S(1)}, bf16[2,2,128,1024]{3,2,1,0:T(8,128)(2,1)}, u32[]{:S(2)}) copy-start(bf16[2,2,128,1024]{3,2,1,0:T(8,128)(2,1)} %get-tuple-element.225.parts_and_out_3_) | copy-start | bytes 3145732
  217.6 40.2 %all-to-all-start.1 = ((bf16[8,4,128,128]{3,2,1,0:T(8,128)(2,1)}), bf16[8,4,128,128]{3,2,1,0:T(8,128)(2,1)}, u32[]{:S(2)}, u32[]{:S(2)}) async-start(bf16[8,4,128,128]{3,2,1,0:T(8,128)(2,1)} %get-tuple-element.226), calls=%async_computation.1 | async-start | bytes 2097152 | tf_op jit(solution)/shard_map/all_to_all | solution.py:394
  221.9 145.8 %reduce-scatter.2.cloned.1.call-start = ((), (), s32[]{:S(2)}) async-start(), calls=%async_computation.4 | async-start | bytes 5242880 | tf_op jit(solution)/shard_map/reduce_scatter | solution.py:613
  222.2 25.5 %collective-permute-start.19 = (bf16[2,2,128,1024]{3,2,1,0:T(8,128)(2,1)S(1)}, bf16[2,2,128,1024]{3,2,1,0:T(8,128)(2,1)S(1)}, u32[]{:S(2)}, u32[]{:S(2)}) collective-permute-start(bf16[2,2,128,1024]{3,2,1,0:T(8,128)(2,1)S(1)} %copy-done.3), channel_id=1, source_target_pairs={{0,1},{1,0},{2,3},{3,2},{4,5},{5,4},{6,7},{7,6},{8,9},{9,8},{10,11... | collective-permute-start | bytes 3145736 | tf_op jit(solution)/shard_map/ppermute | solution.py:441
  247.8 1.0 copy-start.7
Sparse Core Ops, SparseCore 0:
  258.0 109.6 reduce-scatter.1
where the time goes:
time: 378 us; the launch traced here: 377 us
  waiting for transfers between devices  113 us (30%)
  Pallas kernels  96.8 us (26%)
  blocking collectives  53.2 us (14%)
  starting transfers between devices  35.3 us (9%)
  local copies, waits for them, and re-layouts  33.4 us (9%)
  between operations  29.9 us (8%)
  other arithmetic  12 us (3%)
    all_to_all x1, blocking collectives, exchange(): return lax.all_to_all(x, 'dp', split_axis=0, concat_axis=0, tiled=True)  53.2 us
    pallas_call x10, Pallas kernels, tick(): pl.pallas_call(functools.partial(tick_kernel, chunks, index * table.shape...  48.2 us
    ppermute x4, waiting for transfers between devices, swap(): return lax.ppermute(x, 'dp', partners)  41 us
    ppermute x8, waiting for transfers between devices, body(): arrived.append(lax.ppermute(leaving, 'section', hops) if hops else leaving)  26.7 us
    pallas_call x1, Pallas kernels, body(): pl.pallas_call(functools.partial(block_grads_kernel, micros, blk_dev), co...  25.6 us
    reduce_scatter x1, waiting for transfers between devices, body(): lax.psum_scatter(terms, 'dp', scatter_dimension=0, tiled=True, axis_index...  25.4 us
    ppermute x2, waiting for transfers between devices, across(): lax.ppermute(own, 'dp', [(i, i ^ near) for i in range(n_data)])  12.2 us
    all_to_all x2, starting transfers between devices, exchange(): return lax.all_to_all(x, 'dp', split_axis=0, concat_axis=0, tiled=True)  11.5 us
  transfers between devices with their start and end apart: 23, of which 9 were waited for; matrix products, arithmetic and copies ran while one was open for 10% of the time, Pallas kernels for 25%

commit v1 on v0

--- a/solution.py
+++ b/solution.py
@@ -73,12 +73,17 @@
 
 
 def tick_kernel(
-    chunks, base, head_major,
+    chunks, base, head_major, live,
     scal,
-    arriving, top, w_out, w_query, keys, values, probs, g0, u0, d0, sb0, sa0,
-    leaving, g_store, u_store, d_store, s_late, s_early,
-    up, wo, wq, kb, vb, pb, datt, dq, gr, sem_up, sem_wo, sem_wq, sem_k, sem_v, sem_p, sem_out, sem_half, sem_head,
+    arriving, top, w_out, w_query, keys, values, probs,
+    *refs,
 ):
+    count = 3 + len(live)
+    leaving, g_store, u_store, d_store, *s_stores = refs[count : 2 * count + 1]
+    (
+        up, wo, wq, kb, vb, pb, datt, dq, gr,
+        sem_up, sem_wo, sem_wq, sem_k, sem_v, sem_p, sem_out, sem_half, sem_head,
+    ) = refs[2 * count + 1 :]
     micro = scal[base]
     valid = scal[base + 1]
     last = scal[base + 2]
@@ -86,7 +91,7 @@
     tokens, model = up.shape
     width = datt.shape[1]
     spans = tokens // SPAN
-    refs = spans * K_NBR
+    span_refs = spans * K_NBR
     pairs = width // PAIR
     rows = model // chunks
     wide = width // chunks
@@ -123,11 +128,11 @@
 
         for c in range(chunks):
             copy_wo(c).start()
-        for i in range(refs):
+        for i in range(span_refs):
             copy_v(i).start()
         get_probs = pltpu.make_async_copy(probs.at[micro], pb, sem_p)
         get_probs.start()
-        for i in range(refs):
+        for i in range(span_refs):
             copy_k(i).start()
         for c in range(chunks):
             copy_wq(c).start()
@@ -135,10 +140,8 @@
         from_hop.wait()
         save_up = pltpu.make_async_copy(up, u_store.at[micro], sem_out.at[0])
         save_up.start()
-        cut = s_early.shape[0]
-
-        def to_swap(late):
-            store = s_late.at[micro - cut] if late else s_early.at[micro]
+        def to_swap(group):
+            store = s_stores[group].at[micro - live[group][0]]
             copies = [pltpu.make_async_copy(dq, store.at[0], sem_out.at[1])]
             for h in range(halves):
                 start = pl.multiple_of((2 * h + other) * block, block)
@@ -149,16 +152,14 @@
                 )
             return copies
 
-        @pl.when(micro < cut)
-        def _():
-            for copy in to_swap(False)[1:]:
-                copy.start()
-
-        @pl.when(micro >= cut)
-        def _():
-            for copy in to_swap(True)[1:]:
-                copy.start()
-
+        def swap_copies(do):
+            for group, (first, end) in enumerate(live):
+
+                @pl.when((micro >= first) & (micro < end))
+                def _():
+                    do(to_swap(group))
+
+        swap_copies(lambda copies: [copy.start() for copy in copies[1:]])
 
         def project(c, carry):
             copy_wo(c).wait()
@@ -177,10 +178,10 @@
             late = [pltpu.make_async_copy(datt, d_store.at[micro], sem_head.at[0])]
         for save in late:
             save.start()
-        for i in range(refs):
+        for i in range(span_refs):
             copy_v(i).wait()
         get_probs.wait()
-        for i in range(refs):
+        for i in range(span_refs):
             copy_k(i).wait()
 
         def one_group(index, carry):
@@ -200,13 +201,7 @@
 
         lax.fori_loop(0, spans * groups, one_group, 0)
 
-        @pl.when(micro < cut)
-        def _():
-            to_swap(False)[0].start()
-
-        @pl.when(micro >= cut)
-        def _():
-            to_swap(True)[0].start()
+        swap_copies(lambda copies: copies[0].start())
 
         def back(c, carry):
             copy_wq(c).wait()
@@ -222,15 +217,7 @@
         for save in [save_up] + late:
             save.wait()
 
-        @pl.when(micro < cut)
-        def _():
-            for copy in to_swap(False):
-                copy.wait()
-
-        @pl.when(micro >= cut)
-        def _():
-            for copy in to_swap(True):
-                copy.wait()
+        swap_copies(lambda copies: [copy.wait() for copy in copies])
 
 
 def weight_grads_kernel(scale, par, x_own, x_got, up_own, att_own, att_got, *parts_and_out):
@@ -465,21 +452,22 @@
     scal = table.reshape(-1)
     head_major = slice_w % 128 == 0
     d_shape = (n_data, micros, tokens, slice_w) if head_major else (micros, tokens, width)
-    cut = micros // 2
+    swap_groups = [(micros - 1, micros), (micros - 2, micros - 1), (0, micros - 2)]
     store_shapes = (
         jax.ShapeDtypeStruct((micros, tokens, model), BF),
         jax.ShapeDtypeStruct((micros, tokens, model), BF),
         jax.ShapeDtypeStruct(d_shape, BF),
-        jax.ShapeDtypeStruct((micros - cut, 2, tokens, width), BF),
-        jax.ShapeDtypeStruct((cut, 2, tokens, width), BF),
+        *(jax.ShapeDtypeStruct((end - first, 2, tokens, width), BF) for first, end in swap_groups),
     )
 
     def tick(index, arriving, stores):
-        return pl.pallas_call(
-            functools.partial(tick_kernel, chunks, index * table.shape[1], head_major),
-            out_shape=(jax.ShapeDtypeStruct((tokens, model), BF), *store_shapes),
-            in_specs=[pl.BlockSpec(memory_space=pltpu.SMEM)] + [ANY] * 12,
-            out_specs=[ANY] * 6,
+        live = [group for group in swap_groups if ticks - micros + group[1] > index]
+        count = 3 + len(live)
+        out = pl.pallas_call(
+            functools.partial(tick_kernel, chunks, index * table.shape[1], head_major, live),
+            out_shape=(jax.ShapeDtypeStruct((tokens, model), BF), *store_shapes[:count]),
+            in_specs=[pl.BlockSpec(memory_space=pltpu.SMEM)] + [ANY] * (7 + count),
+            out_specs=[ANY] * (1 + count),
             scratch_shapes=[
                 pltpu.VMEM((tokens, model), BF),
                 pltpu.VMEM((chunks, model, width // chunks), BF),
@@ -500,10 +488,11 @@
                 pltpu.SemaphoreType.DMA((halves,)),
                 pltpu.SemaphoreType.DMA((n_data if head_major else 1,)),
             ],
-            input_output_aliases={8: 1, 9: 2, 10: 3, 11: 4, 12: 5},
+            input_output_aliases={8 + i: 1 + i for i in range(count)},
             cost_estimate=cost(11),
             compiler_params=params(),
-        )(scal, arriving, top_grads, w_out, w_query, keys, values, probs, *stores)
+        )(scal, arriving, top_grads, w_out, w_query, keys, values, probs, *stores[:count])
+        return (*out, *stores[count:])
 
     def unwritten(*shapes):
         return pl.pallas_call(
@@ -563,16 +552,20 @@
             held = lax.optimization_barrier((arrived[index + 1], sliced, inputs_got))
             arrived[index + 1], sliced, inputs_got = held
             attended_got = swap(attended.reshape(flat, width))
-        if index == ticks - micros + cut - 1:
-            stores[4], arrived[index + 1] = lax.optimization_barrier((stores[4], arrived[index + 1]))
-            got.append(swap(stores[4]))
-    grads_in, upstream, d_store, s_late, s_early = stores
-    got[0], s_late, d_store = lax.optimization_barrier((got[0], s_late, d_store))
-    got.append(swap(s_late))
+        for group, (_, end) in enumerate(swap_groups):
+            if end == index - (ticks - micros) + 1:
+                at = 3 + group
+                if hops:
+                    stores[at], arrived[index + 1] = lax.optimization_barrier((stores[at], arrived[index + 1]))
+                if got:
+                    stores[at], got[-1] = lax.optimization_barrier((stores[at], got[-1]))
+                got.append(swap(stores[at]))
+    grads_in, upstream, d_store, *s_stores = stores
+
     grad_scale = (flat * n_data) ** (-0.5)
     parts = []
     part_specs = []
-    for own, part in zip((s_early, s_late), got):
+    for own, part in zip(s_stores[::-1], got):
         count = part.shape[0]
         parts += [own, part, part]
         part_specs += [

time: 378 us -> 372 us (0.984)
  waiting for transfers between devices: 113 us -> 107 us
    reduce_scatter x1, waiting for transfers between devices: 25.4 us -> 15 us  [body(): lax.psum_scatter(terms, 'dp', scatter_dimension=0, tiled=True, axis_index...]
    ppermute x4 -> x5, waiting for transfers between devices: 41 us -> 44.6 us  [swap(): return lax.ppermute(x, 'dp', partners)]
    unnamed x56 -> x60, local copies, waits for them, and re-layouts: 10 us -> 9.79 us
  transfers between devices with their start and end apart: 23 -> 24, of which waited for: 9 -> 11; matrix products, arithmetic and copies ran while one was open for 10% -> 10% of each run, Pallas kernels for 25% -> 26%
where the time goes in v1:
time: 372 us; the launch traced here: 371 us
  waiting for transfers between devices  107 us (29%)
  Pallas kernels  98.5 us (26%)
  blocking collectives  52.1 us (14%)
  starting transfers between devices  34.7 us (9%)
  local copies, waits for them, and re-layouts  33.3 us (9%)
  between operations  29.8 us (8%)
  other arithmetic  12.1 us (3%)
    all_to_all x1, blocking collectives, exchange(): return lax.all_to_all(x, 'dp', split_axis=0, concat_axis=0, tiled=True)  52.1 us
    pallas_call x10, Pallas kernels, tick(): pl.pallas_call(functools.partial(tick_kernel, chunks, index * table.shape...  48.4 us
    ppermute x5, waiting for transfers between devices, swap(): return lax.ppermute(x, 'dp', partners)  44.6 us
    ppermute x8, waiting for transfers between devices, body(): arrived.append(lax.ppermute(leaving, 'section', hops) if hops else leaving)  27.5 us
    pallas_call x1, Pallas kernels, body(): pl.pallas_call(functools.partial(block_grads_kernel, micros, blk_dev), co...  25.6 us
    reduce_scatter x1, waiting for transfers between devices, body(): lax.psum_scatter(terms, 'dp', scatter_dimension=0, tiled=True, axis_index...  15 us
    ppermute x2, waiting for transfers between devices, across(): lax.ppermute(own, 'dp', [(i, i ^ near) for i in range(n_data)])  12.1 us
    all_to_all x2, starting transfers between devices, exchange(): return lax.all_to_all(x, 'dp', split_axis=0, concat_axis=0, tiled=True)  11.5 us
  transfers between devices with their start and end apart: 24, of which 11 were waited for; matrix products, arithmetic and copies ran while one was open for 10% of the time, Pallas kernels for 26%

profile of v1, /device:TPU:9, one launch (start us, length us, event | category | flops | bytes accessed | tf_op | source)
XLA Modules:
  0.0 370.9 jit_solution(11111812709756337372)
XLA Ops:
  7.2 1.3 copy.149
  8.5 0.9 slice_bitcast_fusion.2
  9.4 2.3 collective-permute-start
  32.5 2.0 collective-permute-done
  34.4 3.1 collective-permute-start.1
  37.5 1.1 select_select_fusion.5
  39.7 0.9 pad_maximum_fusion.7
  40.6 0.9 pad_maximum_fusion.8
  41.5 1.3 collective-permute-start.2
  42.8 1.4 collective-permute-start.4
  44.2 3.3 convolution_convert_fusion
  47.5 10.2 %collective-permute-done.1 = bf16[2,128,1024]{2,1,0:T(8,128)(2,1)S(1)} collective-permute-done((bf16[2,128,1024]{2,1,0:T(8,128)(2,1)}, bf16[2,128,1024]{2,1,0:T(8,128)(2,1)S(1)}, u32[]{:S(2)}, u32[]{:S(2)}) %collective-permute-start.1) | collective-permute-done | bytes 524320 | tf_op jit(solution)/shard_map/ppermute | solution.py:362
  57.8 0.8 pad_maximum_fusion.1
  58.6 0.8 pad_maximum_fusion.2
  59.5 0.8 pad_maximum_fusion.3
  60.3 0.9 pad_maximum_fusion.4
  62.8 1.0 collective-permute-start.5
  63.8 1.3 collective-permute-start.6
  66.2 2.3 copy.127
  68.5 2.3 copy.128
  71.6 1.1 constant_dynamic-update-slice_fusion.2
  72.6 1.1 constant_dynamic-update-slice_fusion.1
  73.7 1.8 maximum_maximum_fusion
  75.6 1.1 constant_dynamic-update-slice_fusion.k_ref.keys
  76.7 1.4 copy-done.2
  78.1 7.5 %shard_map.111.probs = bf16[4,16,128,256]{3,2,1,0:T(8,128)(2,1)} custom-call(s32[16]{0:T(128)} %reshape.318.owners, bf16[4,128,1024]{2,1,0:T(8,128)(2,1)} %bitcast.122, bf16[8,128,1024]{2,1,0:T(8,128)(2,1)} %copy-done.2), custom_call_target="tpu_custom_call" | custom-call | bytes 25200000 | tf_op jit(solution)/shard_map/pallas_call | solution.py:395
  85.8 1.1 pad_maximum_fusion
  86.9 1.1 constant_dynamic-update-slice_fusion.6
  88.0 1.1 constant_dynamic-update-slice_fusion.5
  89.1 7.7 %collective-permute-done.7 = bf16[2,128,1024]{2,1,0:T(8,128)(2,1)} collective-permute-done((bf16[2,128,1024]{2,1,0:T(8,128)(2,1)}, bf16[2,128,1024]{2,1,0:T(8,128)(2,1)}, u32[]{:S(2)}, u32[]{:S(2)}) %collective-permute-start.7) | collective-permute-done | bytes 524320 | tf_op jit(solution)/shard_map/ppermute | solution.py:377
  96.8 1.1 constant_dynamic-update-slice_fusion.4.values
  97.9 1.0 broadcast_in_dim.76.arriving
  99.4 1.0 shard_map.113
  100.4 7.2 %all-to-all-start = ((bf16[8,1040,128]{2,1,0:T(8,128)(2,1)}), bf16[8,1040,128]{2,1,0:T(8,128)(2,1)S(1)}, u32[]{:S(2)}, u32[]{:S(2)}) async-start(bf16[8,1040,128]{2,1,0:T(8,128)(2,1)} %maximum_maximum_fusion), calls=%async_computation | async-start | bytes 4259840 | tf_op jit(solution)/shard_map/all_to_all | solution.py:381
  108.9 5.7 %shard_map.114.a0 = bf16[4,128,1024]{2,1,0:T(8,128)(2,1)} custom-call(s32[17]{0:T(128)} %get-tuple-element.283.scal, bf16[8,128,1024]{2,1,0:T(8,128)(2,1)} %copy-done.1, bf16[4,16,128,256]{3,2,1,0:T(8,128)(2,1)} %shard_map.111.probs, bf16[4,128,1024]{2,1,0:T(8,128)(2,1)} %get-tuple-element.150.a0), custom_call_target="tpu_custom_call", output_to_operand_aliasing={{}: (3, {})} | custom-call | bytes 18000000 | tf_op jit(solution)/shard_map/pallas_call | solution.py:505
  114.7 1.0 shard_map.115
  116.5 1.2 shard_map.116
  117.7 1.3 collective-permute-start.10
  119.0 1.3 collective-permute-start.12
  120.2 1.0 shard_map.117
  121.2 22.1 %collective-permute-done.10.arriving = bf16[128,2048]{1,0:T(8,128)(2,1)S(1)} collective-permute-done((bf16[128,2048]{1,0:T(8,128)(2,1)}, bf16[128,2048]{1,0:T(8,128)(2,1)S(1)}, u32[]{:S(2)}, u32[]{:S(2)}) %collective-permute-start.10) | collective-permute-done | bytes 524320 | tf_op jit(solution)/shard_map/ppermute | solution.py:548
  143.3 1.3 collective-permute-start.11
  144.6 10.6 %shard_map.118 = (bf16[128,2048]{1,0:T(8,128)(2,1)}, bf16[4,128,2048]{2,1,0:T(8,128)(2,1)}, bf16[4,128,2048]{2,1,0:T(8,128)(2,1)}, bf16[8,4,128,128]{3,2,1,0:T(8...) custom-call(s32[80]{0:T(128)} %reshape.317.scal, ...), custom_call_target="tpu_custom_call", output_to_operand_aliasing={{1}: (8, {}), {2}: (9, {}), {3}: (10, {}), {4}: (11, {}), {... | custom-call | bytes 39600000 | tf_op jit(solution)/shard_map/pallas_call | solution.py:466
  155.1 2.2 collective-permute-done.11.arriving
  157.4 1.9 collective-permute-start.13
  160.3 10.6 %shard_map.120 = (bf16[128,2048]{1,0:T(8,128)(2,1)}, bf16[4,128,2048]{2,1,0:T(8,128)(2,1)}, bf16[4,128,2048]{2,1,0:T(8,128)(2,1)}, bf16[8,4,128,128]{3,2,1,0:T(8...) custom-call(s32[80]{0:T(128)} %reshape.317.scal, ...), custom_call_target="tpu_custom_call", output_to_operand_aliasing={{1}: (8, {}), {2}: (9, {}), {3}: (10, {}), {4}: (11, {}), {... | custom-call | bytes 39600000 | tf_op jit(solution)/shard_map/pallas_call | solution.py:466
  170.9 1.9 collective-permute-start.14
  172.8 10.6 %shard_map.121 = (bf16[128,2048]{1,0:T(8,128)(2,1)}, bf16[4,128,2048]{2,1,0:T(8,128)(2,1)}, bf16[4,128,2048]{2,1,0:T(8,128)(2,1)}, bf16[8,4,128,128]{3,2,1,0:T(8...) custom-call(s32[80]{0:T(128)} %reshape.317.scal, ...), custom_call_target="tpu_custom_call", output_to_operand_aliasing={{1}: (8, {}), {2}: (9, {}), {3}: (10, {}), {4}: (11, {}), {... | custom-call | bytes 39600000 | tf_op jit(solution)/shard_map/pallas_call | solution.py:466
  183.4 2.7 collective-permute-done.14.arriving
  186.1 1.3 collective-permute-start.16
  187.4 10.6 %shard_map.122 = (bf16[128,2048]{1,0:T(8,128)(2,1)}, bf16[4,128,2048]{2,1,0:T(8,128)(2,1)}, bf16[4,128,2048]{2,1,0:T(8,128)(2,1)}, bf16[8,4,128,128]{3,2,1,0:T(8...) custom-call(s32[80]{0:T(128)} %reshape.317.scal, ...), custom_call_target="tpu_custom_call", output_to_operand_aliasing={{1}: (8, {}), {2}: (9, {}), {3}: (10, {}), {4}: (11, {}), {... | custom-call | bytes 39600000 | tf_op jit(solution)/shard_map/pallas_call | solution.py:466
  198.0 1.3 collective-permute-start.17
  199.5 1.0 shard_map.123
  201.9 1.0 shard_map.124
  202.9 4.3 %all-to-all-start.1 = ((bf16[8,4,128,128]{3,2,1,0:T(8,128)(2,1)}), bf16[8,4,128,128]{3,2,1,0:T(8,128)(2,1)}, u32[]{:S(2)}, u32[]{:S(2)}) async-start(bf16[8,4,128,128]{3,2,1,0:T(8,128)(2,1)} %get-tuple-element.244), calls=%async_computation.1 | async-start | bytes 2097152 | tf_op jit(solution)/shard_map/all_to_all | solution.py:381
  207.5 13.2 %collective-permute-done.18.parts_and_out_1_.parts_and_out_2_ = bf16[2,2,128,1024]{3,2,1,0:T(8,128)(2,1)} collective-permute-done((bf16[2,2,128,1024]{3,2,1,0:T(8,128)(2,1)}, bf16[2,2,128,1024]{3,2,1,0:T(8,128)(2,1)}, u32[]{:S(2)}, u32[]{:S(2)}) %collective-permute-start.18) | collective-permute-done | bytes 1048608 | tf_op jit(solution)/shard_map/ppermute | solution.py:428
  220.7 18.4 %collective-permute-done.19.parts_and_out_4_.parts_and_out_5_ = bf16[1,2,128,1024]{3,2,1,0:T(8,128)(2,1)S(1)} collective-permute-done((bf16[1,2,128,1024]{3,2,1,0:T(8,128)(2,1)S(1)}, bf16[1,2,128,1024]{3,2,1,0:T(8,128)(2,1)S(1)}, u32[]{:S(2)}, u32[]{:S(2)}) %collective-permute-start.19) | collective-permute-done | bytes 524320 | tf_op jit(solution)/shard_map/ppermute | solution.py:428
  239.1 13.0 %collective-permute-done.20.parts_and_out_7_.parts_and_out_8_ = bf16[1,2,128,1024]{3,2,1,0:T(8,128)(2,1)S(1)} collective-permute-done((bf16[1,2,128,1024]{3,2,1,0:T(8,128)(2,1)S(1)}, bf16[1,2,128,1024]{3,2,1,0:T(8,128)(2,1)S(1)}, u32[]{:S(2)}, u32[]{:S(2)}) %collective-permute-start.20) | collective-permute-done | bytes 524320 | tf_op jit(solution)/shard_map/ppermute | solution.py:428
  252.9 10.5 %shard_map.125 = bf16[1024,2048]{1,0:T(8,128)(2,1)} custom-call(s32[1]{0:T(128)} %bitcast.44.par, bf16[512,2048]{1,0:T(8,128)(2,1)} %bitcast.112, bf16[512,1024]{1,0:T(8,128)(2,1)} %collective-permute-done.12.x_got, bf16[512,2048]{1,0:T(8,128)(2,1)} %bitcast.106, bf16[512,1024]{1,0:T(8,128)(2,1)} %bitcast.109, bf16[512,1024]{1,0:T(8,128)(2,1)} %copy-done.13, ...), custom_call_target="tpu_custom_call" | custom-call | bytes 32400000 | tf_op jit(solution)/shard_map/pallas_call | solution.py:576
  267.1 25.6 %shard_map.126 = bf16[16,2,128,128]{3,2,1,0:T(8,128)(2,1)} custom-call(s32[128]{0:T(128)} %multiply_add_fusion.ids, s32[128]{0:T(128)} %reshape.327.mask, bf16[8,1040,128]{2,1,0:T(8,128)(2,1)} %copy-done.5, bf16[8,512,128]{2,1,0:T(8,128)(2,1)} %bitcast.46.d_ref, bf16[8,1040,128]{2,1,0:T(8,128)(2,1)} %copy-done.5), custom_call_target="tpu_custom_call" | custom-call | bytes 133200000 | tf_op jit(solution)/shard_map/pallas_call | solution.py:624
  292.8 52.1 %all_to_all.15 = bf16[8,2,2,128,128]{4,3,2,1,0:T(8,128)(2,1)S(1)} all-to-all(bf16[8,2,2,128,128]{4,3,2,1,0:T(8,128)(2,1)} %bitcast.121), channel_id=1, replica_groups=mesh['section'=4,'dp'=8] {'dp'}, dimensions={0} | all-to-all | bytes 2097152 | tf_op jit(solution)/shard_map/all_to_all | solution.py:381
  345.6 1.3 broadcast_in_dim_reshape.3
  346.9 15.0 %reduce-scatter.2.cloned.1.call-done = bf16[256,2048]{1,0:T(8,128)(2,1)} async-done(((bf16[1024,2048]{1,0:T(8,128)(2,1)}), bf16[256,2048]{1,0:T(8,128)(2,1)}) %reduce-scatter.2.cloned.1.call-update) | async-done | bytes 1048592 | tf_op jit(solution)/shard_map/reduce_scatter | solution.py:606
  361.9 2.2 slice_bitcast_fusion
  (142 shorter events, 20.9 us)
Async XLA Ops:
  7.2 4.6 %copy-start.22 = (s32[8,8]{1,0:T(8,128)S(1)}, s32[8,8]{1,0:T(8,128)}, u32[]{:S(2)}) copy-start(s32[8,8]{1,0:T(8,128)} %param.19) | copy-start | bytes 772
  7.2 4.6 %copy-start.21 = (s32[8,8]{1,0:T(8,128)S(1)}, s32[8,8]{1,0:T(8,128)}, u32[]{:S(2)}) copy-start(s32[8,8]{1,0:T(8,128)} %param.18) | copy-start | bytes 772
  8.5 23.9 %copy-start.9 = (bf16[1,2,2,128,1024]{4,3,2,1,0:T(8,128)(2,1)S(1)}, bf16[1,2,2,128,1024]{4,3,2,1,0:T(8,128)(2,1)}, u32[]{:S(2)}) copy-start(bf16[1,2,2,128,1024]{4,3,2,1,0:T(8,128)(2,1)} %param.16) | copy-start | bytes 3145732
  9.4 25.1 %collective-permute-start = (bf16[2,128,1024]{2,1,0:T(8,128)(2,1)S(1)}, bf16[2,128,1024]{2,1,0:T(8,128)(2,1)S(1)}, u32[]{:S(2)}, u32[]{:S(2)}) collective-permute-start(bf16[2,128,1024]{2,1,0:T(8,128)(2,1)S(1)} %get-tuple-element.260), channel_id=1, source_target_pairs={{0,4},{1,5},{2,6},{3,7},{4,0},{5,1},{6,2},{7,3},{8,12},{9,13},{10,... | collective-permute-start | bytes 1572872 | tf_op jit(solution)/shard_map/ppermute | solution.py:362
  34.4 23.3 %collective-permute-start.1 = (bf16[2,128,1024]{2,1,0:T(8,128)(2,1)}, bf16[2,128,1024]{2,1,0:T(8,128)(2,1)S(1)}, u32[]{:S(2)}, u32[]{:S(2)}) collective-permute-start(bf16[2,128,1024]{2,1,0:T(8,128)(2,1)} %get-tuple-element.127), channel_id=1, source_target_pairs={{0,4},{1,5},{2,6},{3,7},{4,0},{5,1},{6,2},{7,3},{8,12},{9,13},{10,... | collective-permute-start | bytes 1572872 | tf_op jit(solution)/shard_map/ppermute | solution.py:362
  38.6 5.5 %copy-start.6 = (bf16[1,4,128,2048]{3,2,1,0:T(8,128)(2,1)S(1)}, bf16[1,4,128,2048]{3,2,1,0:T(8,128)(2,1)}, u32[]{:S(2)}) copy-start(bf16[1,4,128,2048]{3,2,1,0:T(8,128)(2,1)} %param.12) | copy-start | bytes 6291460
  38.8 5.4 %copy-start = (bf16[1,2048,1024]{2,1,0:T(8,128)(2,1)S(1)}, bf16[1,2048,1024]{2,1,0:T(8,128)(2,1)}, u32[]{:S(2)}) copy-start(bf16[1,2048,1024]{2,1,0:T(8,128)(2,1)} %param.14) | copy-start | bytes 12582916
  41.5 29.5 %collective-permute-start.2 = (bf16[2,128,1024]{2,1,0:T(8,128)(2,1)}, bf16[2,128,1024]{2,1,0:T(8,128)(2,1)}, u32[]{:S(2)}, u32[]{:S(2)}) collective-permute-start(bf16[2,128,1024]{2,1,0:T(8,128)(2,1)} %pad_maximum_fusion.6), channel_id=1, source_target_pairs={{0,1},{1,0},{2,3},{3,2},{4,5},{5,4},{6,7},{7,6},{8,9},{9,8},{10,11... | collective-permute-start | bytes 1572872 | tf_op jit(solution)/shard_map/ppermute | solution.py:377
  42.8 29.9 %collective-permute-start.3 = (bf16[2,128,1024]{2,1,0:T(8,128)(2,1)}, bf16[2,128,1024]{2,1,0:T(8,128)(2,1)}, u32[]{:S(2)}, u32[]{:S(2)}) collective-permute-start(bf16[2,128,1024]{2,1,0:T(8,128)(2,1)} %pad_maximum_fusion.7), channel_id=1, source_target_pairs={{0,2},{1,3},{2,0},{3,1},{4,6},{5,7},{6,4},{7,5},{8,10},{9,11},{10,... | collective-permute-start | bytes 1572872 | tf_op jit(solution)/shard_map/ppermute | solution.py:377
  42.8 32.8 %collective-permute-start.4 = (bf16[2,128,1024]{2,1,0:T(8,128)(2,1)}, bf16[2,128,1024]{2,1,0:T(8,128)(2,1)}, u32[]{:S(2)}, u32[]{:S(2)}) collective-permute-start(bf16[2,128,1024]{2,1,0:T(8,128)(2,1)} %pad_maximum_fusion.8), channel_id=1, source_target_pairs={{0,3},{1,2},{2,1},{3,0},{4,7},{5,6},{6,5},{7,4},{8,11},{9,10},{10,... | collective-permute-start | bytes 1572872 | tf_op jit(solution)/shard_map/ppermute | solution.py:377
  57.8 3.4 copy-start.24
  62.8 24.1 %collective-permute-start.5 = (bf16[2,128,1024]{2,1,0:T(8,128)(2,1)}, bf16[2,128,1024]{2,1,0:T(8,128)(2,1)}, u32[]{:S(2)}, u32[]{:S(2)}) collective-permute-start(bf16[2,128,1024]{2,1,0:T(8,128)(2,1)} %pad_maximum_fusion.2), channel_id=1, source_target_pairs={{0,1},{1,0},{2,3},{3,2},{4,5},{5,4},{6,7},{7,6},{8,9},{9,8},{10,11... | collective-permute-start | bytes 1572872 | tf_op jit(solution)/shard_map/ppermute | solution.py:377
  63.8 24.2 %collective-permute-start.6 = (bf16[2,128,1024]{2,1,0:T(8,128)(2,1)}, bf16[2,128,1024]{2,1,0:T(8,128)(2,1)}, u32[]{:S(2)}, u32[]{:S(2)}) collective-permute-start(bf16[2,128,1024]{2,1,0:T(8,128)(2,1)} %pad_maximum_fusion.3), channel_id=1, source_target_pairs={{0,2},{1,3},{2,0},{3,1},{4,6},{5,7},{6,4},{7,5},{8,10},{9,11},{10,... | collective-permute-start | bytes 1572872 | tf_op jit(solution)/shard_map/ppermute | solution.py:377
  71.0 2.7 copy-start.8
  71.0 25.8 %collective-permute-start.7 = (bf16[2,128,1024]{2,1,0:T(8,128)(2,1)}, bf16[2,128,1024]{2,1,0:T(8,128)(2,1)}, u32[]{:S(2)}, u32[]{:S(2)}) collective-permute-start(bf16[2,128,1024]{2,1,0:T(8,128)(2,1)} %pad_maximum_fusion.4), channel_id=1, source_target_pairs={{0,3},{1,2},{2,1},{3,0},{4,7},{5,6},{6,5},{7,4},{8,11},{9,10},{10,... | collective-permute-start | bytes 1572872 | tf_op jit(solution)/shard_map/ppermute | solution.py:377
  76.6 1.4 copy-start.2
  78.1 7.5 %copy-start.12 = (bf16[2,128,1024]{2,1,0:T(8,128)(2,1)S(1)}, bf16[2,128,1024]{2,1,0:T(8,128)(2,1)}, u32[]{:S(2)}) copy-start(bf16[2,128,1024]{2,1,0:T(8,128)(2,1)} %pad_maximum_fusion.1) | copy-start | bytes 1572868
  78.1 7.5 %copy-start.7 = (bf16[1,4,128,2048]{3,2,1,0:T(8,128)(2,1)S(1)}, bf16[1,4,128,2048]{3,2,1,0:T(8,128)(2,1)}, u32[]{:S(2)}) copy-start(bf16[1,4,128,2048]{3,2,1,0:T(8,128)(2,1)} %param.12) | copy-start | bytes 6291460
  97.9 1.5 copy-start.1
  100.4 7.9 %copy-start.23 = (s32[16]{0:T(128)S(1)}, s32[16]{0:T(128)}, u32[]{:S(2)}) copy-start(s32[16]{0:T(128)} %reshape.318.owners) | copy-start | bytes 196
  100.4 59.9 %all-to-all-start = ((bf16[8,1040,128]{2,1,0:T(8,128)(2,1)}), bf16[8,1040,128]{2,1,0:T(8,128)(2,1)S(1)}, u32[]{:S(2)}, u32[]{:S(2)}) async-start(bf16[8,1040,128]{2,1,0:T(8,128)(2,1)} %maximum_maximum_fusion), calls=%async_computation | async-start | bytes 4259840 | tf_op jit(solution)/shard_map/all_to_all | solution.py:381
  107.6 8.1 %collective-permute-start.8 = (bf16[128,2048]{1,0:T(8,128)(2,1)}, bf16[128,2048]{1,0:T(8,128)(2,1)S(1)}, u32[]{:S(2)}, u32[]{:S(2)}) collective-permute-start(bf16[128,2048]{1,0:T(8,128)(2,1)} %get-tuple-element.158), channel_id=1, source_target_pairs={{24,16},{25,17},{26,18},{27,19},{28,20},{29,21},{30,22},{31,23}} | collective-permute-start | bytes 1572872 | tf_op jit(solution)/shard_map/ppermute | solution.py:548
  115.7 0.8 copy-start.15
  115.7 1.9 collective-permute-start.9
  117.6 2.6 copy-start.17
  117.7 25.6 %collective-permute-start.10 = (bf16[128,2048]{1,0:T(8,128)(2,1)}, bf16[128,2048]{1,0:T(8,128)(2,1)S(1)}, u32[]{:S(2)}, u32[]{:S(2)}) collective-permute-start(bf16[128,2048]{1,0:T(8,128)(2,1)} %get-tuple-element.176), channel_id=1, source_target_pairs={{16,8},{24,16},{17,9},{25,17},{18,10},{26,18},{19,11},{27,19},{20,... | collective-permute-start | bytes 1572872 | tf_op jit(solution)/shard_map/ppermute | solution.py:548
  119.0 41.3 %collective-permute-start.12 = (bf16[512,1024]{1,0:T(8,128)(2,1)}, bf16[512,1024]{1,0:T(8,128)(2,1)}, u32[]{:S(2)}, u32[]{:S(2)}) collective-permute-start(bf16[512,1024]{1,0:T(8,128)(2,1)} %pad_maximum_fusion), channel_id=1, source_target_pairs={{0,1},{1,0},{2,3},{3,2},{4,5},{5,4},{6,7},{7,6},{8,9},{9,8},{10,11... | collective-permute-start | bytes 3145736 | tf_op jit(solution)/shard_map/ppermute | solution.py:428
  143.3 1.3 copy-start.18
  143.3 14.1 %collective-permute-start.11 = (bf16[128,2048]{1,0:T(8,128)(2,1)}, bf16[128,2048]{1,0:T(8,128)(2,1)S(1)}, u32[]{:S(2)}, u32[]{:S(2)}) collective-permute-start(bf16[128,2048]{1,0:T(8,128)(2,1)} %get-tuple-element.185), channel_id=1, source_target_pairs={{16,8},{24,16},{17,9},{25,17},{18,10},{26,18},{19,11},{27,19},{20,... | collective-permute-start | bytes 1572872 | tf_op jit(solution)/shard_map/ppermute | solution.py:548
  157.4 2.7 copy-start.14
  157.4 13.5 %collective-permute-start.13 = (bf16[128,2048]{1,0:T(8,128)(2,1)}, bf16[128,2048]{1,0:T(8,128)(2,1)}, u32[]{:S(2)}, u32[]{:S(2)}) collective-permute-start(bf16[128,2048]{1,0:T(8,128)(2,1)} %get-tuple-element.199), channel_id=1, source_target_pairs={{8,0},{16,8},{9,1},{17,9},{10,2},{18,10},{11,3},{19,11},{12,4},{20... | collective-permute-start | bytes 1572872 | tf_op jit(solution)/shard_map/ppermute | solution.py:548
  160.0 27.3 %collective-permute-start.15 = (bf16[512,1024]{1,0:T(8,128)(2,1)}, bf16[512,1024]{1,0:T(8,128)(2,1)S(1)}, u32[]{:S(2)}, u32[]{:S(2)}) collective-permute-start(bf16[512,1024]{1,0:T(8,128)(2,1)} %bitcast.108), channel_id=1, source_target_pairs={{0,1},{1,0},{2,3},{3,2},{4,5},{5,4},{6,7},{7,6},{8,9},{9,8},{10,11... | collective-permute-start | bytes 3145736 | tf_op jit(solution)/shard_map/ppermute | solution.py:428
  160.3 104.6 %copy-start.5 = (bf16[8,1040,128]{2,1,0:T(8,128)(2,1)}, bf16[8,1040,128]{2,1,0:T(8,128)(2,1)S(1)}, u32[]{:S(2)}) copy-start(bf16[8,1040,128]{2,1,0:T(8,128)(2,1)S(1)} %all-to-all-done.q_ref.kv_ref) | copy-start | bytes 6389764
  170.9 15.2 %collective-permute-start.14 = (bf16[128,2048]{1,0:T(8,128)(2,1)}, bf16[128,2048]{1,0:T(8,128)(2,1)S(1)}, u32[]{:S(2)}, u32[]{:S(2)}) collective-permute-start(bf16[128,2048]{1,0:T(8,128)(2,1)} %get-tuple-element.208), channel_id=1, source_target_pairs={{8,0},{16,8},{9,1},{17,9},{10,2},{18,10},{11,3},{19,11},{12,4},{20... | collective-permute-start | bytes 1572872 | tf_op jit(solution)/shard_map/ppermute | solution.py:548
  186.1 1.3 copy-start.19
  186.1 11.9 %collective-permute-start.16 = (bf16[128,2048]{1,0:T(8,128)(2,1)}, bf16[128,2048]{1,0:T(8,128)(2,1)S(1)}, u32[]{:S(2)}, u32[]{:S(2)}) collective-permute-start(bf16[128,2048]{1,0:T(8,128)(2,1)} %get-tuple-element.219), channel_id=1, source_target_pairs={{8,0},{9,1},{10,2},{11,3},{12,4},{13,5},{14,6},{15,7}} | collective-permute-start | bytes 1572872 | tf_op jit(solution)/shard_map/ppermute | solution.py:548
  187.4 10.6 %copy-start.13 = (bf16[512,1024]{1,0:T(8,128)(2,1)}, bf16[512,1024]{1,0:T(8,128)(2,1)S(1)}, u32[]{:S(2)}) copy-start(bf16[512,1024]{1,0:T(8,128)(2,1)S(1)} %collective-permute-done.15.att_got) | copy-start | bytes 3145732
  198.0 1.4 copy-start.16
  198.0 3.0 collective-permute-start.17
  199.4 21.3 %collective-permute-start.18 = (bf16[2,2,128,1024]{3,2,1,0:T(8,128)(2,1)}, bf16[2,2,128,1024]{3,2,1,0:T(8,128)(2,1)}, u32[]{:S(2)}, u32[]{:S(2)}) collective-permute-start(bf16[2,2,128,1024]{3,2,1,0:T(8,128)(2,1)} %get-tuple-element.237.parts_and_out_0_), channel_id=1, source_target_pairs={{0,1},{1,0},{2,3},{3,2},{4,5},{5,4},{6,7},{7,6},{8,9},{9,8},{10,11... | collective-permute-start | bytes 3145736 | tf_op jit(solution)/shard_map/ppermute | solution.py:428
  201.1 0.8 copy-start.20
  202.8 17.9 %copy-start.4 = (bf16[1,2,128,1024]{3,2,1,0:T(8,128)(2,1)S(1)}, bf16[1,2,128,1024]{3,2,1,0:T(8,128)(2,1)}, u32[]{:S(2)}) copy-start(bf16[1,2,128,1024]{3,2,1,0:T(8,128)(2,1)} %get-tuple-element.240.parts_and_out_3_) | copy-start | bytes 1572868
  202.8 36.2 %copy-start.3 = (bf16[1,2,128,1024]{3,2,1,0:T(8,128)(2,1)S(1)}, bf16[1,2,128,1024]{3,2,1,0:T(8,128)(2,1)}, u32[]{:S(2)}) copy-start(bf16[1,2,128,1024]{3,2,1,0:T(8,128)(2,1)} %get-tuple-element.243.parts_and_out_6_) | copy-start | bytes 1572868
  202.9 60.5 %all-to-all-start.1 = ((bf16[8,4,128,128]{3,2,1,0:T(8,128)(2,1)}), bf16[8,4,128,128]{3,2,1,0:T(8,128)(2,1)}, u32[]{:S(2)}, u32[]{:S(2)}) async-start(bf16[8,4,128,128]{3,2,1,0:T(8,128)(2,1)} %get-tuple-element.244), calls=%async_computation.1 | async-start | bytes 2097152 | tf_op jit(solution)/shard_map/all_to_all | solution.py:381
  207.2 154.7 %reduce-scatter.2.cloned.1.call-start = ((), (), s32[]{:S(2)}) async-start(), calls=%async_computation.4 | async-start | bytes 5242880 | tf_op jit(solution)/shard_map/reduce_scatter | solution.py:606
  220.7 18.4 %collective-permute-start.19 = (bf16[1,2,128,1024]{3,2,1,0:T(8,128)(2,1)S(1)}, bf16[1,2,128,1024]{3,2,1,0:T(8,128)(2,1)S(1)}, u32[]{:S(2)}, u32[]{:S(2)}) collective-permute-start(bf16[1,2,128,1024]{3,2,1,0:T(8,128)(2,1)S(1)} %copy-done.4), channel_id=1, source_target_pairs={{0,1},{1,0},{2,3},{3,2},{4,5},{5,4},{6,7},{7,6},{8,9},{9,8},{10,11... | collective-permute-start | bytes 1572872 | tf_op jit(solution)/shard_map/ppermute | solution.py:428
  239.1 13.0 %copy-start.10 = (bf16[1,2,128,1024]{3,2,1,0:T(8,128)(2,1)}, bf16[1,2,128,1024]{3,2,1,0:T(8,128)(2,1)S(1)}, u32[]{:S(2)}) copy-start(bf16[1,2,128,1024]{3,2,1,0:T(8,128)(2,1)S(1)} %collective-permute-done.19.parts_and_out_4_.parts_and_out_5_) | copy-start | bytes 1572868
  239.1 13.0 %collective-permute-start.20 = (bf16[1,2,128,1024]{3,2,1,0:T(8,128)(2,1)S(1)}, bf16[1,2,128,1024]{3,2,1,0:T(8,128)(2,1)S(1)}, u32[]{:S(2)}, u32[]{:S(2)}) collective-permute-start(bf16[1,2,128,1024]{3,2,1,0:T(8,128)(2,1)S(1)} %copy-done.3), channel_id=1, source_target_pairs={{0,1},{1,0},{2,3},{3,2},{4,5},{5,4},{6,7},{7,6},{8,9},{9,8},{10,11... | collective-permute-start | bytes 1572872 | tf_op jit(solution)/shard_map/ppermute | solution.py:428
  252.1 0.8 copy-start.11
Sparse Core Ops, SparseCore 0:
  263.5 98.3 reduce-scatter.1

commit v2 on v1

--- a/solution.py
+++ b/solution.py
@@ -557,10 +557,11 @@
                 at = 3 + group
                 if hops:
                     stores[at], arrived[index + 1] = lax.optimization_barrier((stores[at], arrived[index + 1]))
-                if got:
-                    stores[at], got[-1] = lax.optimization_barrier((stores[at], got[-1]))
+                if group == 0:
+                    stores[at], got = lax.optimization_barrier((stores[at], got))
                 got.append(swap(stores[at]))
     grads_in, upstream, d_store, *s_stores = stores
+    got[-1], d_store = lax.optimization_barrier((got[-1], d_store))
 
     grad_scale = (flat * n_data) ** (-0.5)
     parts = []

time: 372 us -> 379 us (1.019)
    ppermute x5, waiting for transfers between devices: 44.6 us -> 34.9 us  [swap(): return lax.ppermute(x, 'dp', partners)]
    all_to_all x2, waiting for transfers between devices: 0.01 us -> 7.12 us  [exchange(): return lax.all_to_all(x, 'dp', split_axis=0, concat_axis=0, tiled=True)]
    reduce_scatter x1, waiting for transfers between devices: 15 us -> 20.7 us  [body(): lax.psum_scatter(terms, 'dp', scatter_dimension=0, tiled=True, axis_index...]
    unnamed x60 -> x56, local copies, waits for them, and re-layouts: 9.79 us -> 9.79 us
  transfers between devices with their start and end apart: 24 -> 24, of which waited for: 11 -> 10; matrix products, arithmetic and copies ran while one was open for 10% -> 10% of each run, Pallas kernels for 26% -> 26%
where the time goes in v2:
time: 379 us; the launch traced here: 378 us
  waiting for transfers between devices  109 us (29%)
  Pallas kernels  98.5 us (26%)
  blocking collectives  55.4 us (15%)
  starting transfers between devices  36.1 us (10%)
  local copies, waits for them, and re-layouts  33.3 us (9%)
  between operations  30 us (8%)
  other arithmetic  12 us (3%)
    all_to_all x1, blocking collectives, exchange(): return lax.all_to_all(x, 'dp', split_axis=0, concat_axis=0, tiled=True)  55.4 us
    pallas_call x10, Pallas kernels, tick(): pl.pallas_call(functools.partial(tick_kernel, chunks, index * table.shape...  48.4 us
    ppermute x5, waiting for transfers between devices, swap(): return lax.ppermute(x, 'dp', partners)  34.9 us
    ppermute x8, waiting for transfers between devices, body(): arrived.append(lax.ppermute(leaving, 'section', hops) if hops else leaving)  27 us
    pallas_call x1, Pallas kernels, body(): pl.pallas_call(functools.partial(block_grads_kernel, micros, blk_dev), co...  25.6 us
    reduce_scatter x1, waiting for transfers between devices, body(): lax.psum_scatter(terms, 'dp', scatter_dimension=0, tiled=True, axis_index...  20.7 us
    ppermute x2, waiting for transfers between devices, across(): lax.ppermute(own, 'dp', [(i, i ^ near) for i in range(n_data)])  11.9 us
    all_to_all x2, starting transfers between devices, exchange(): return lax.all_to_all(x, 'dp', split_axis=0, concat_axis=0, tiled=True)  11.4 us
  transfers between devices with their start and end apart: 24, of which 10 were waited for; matrix products, arithmetic and copies ran while one was open for 10% of the time, Pallas kernels for 26%

profile of v2, /device:TPU:9, one launch (start us, length us, event | category | flops | bytes accessed | tf_op | source)
XLA Modules:
  0.0 378.0 jit_solution(11427904670844701753)
XLA Ops:
  7.2 1.3 copy.149
  8.5 0.9 slice_bitcast_fusion.2
  9.4 2.3 collective-permute-start
  32.7 1.7 collective-permute-done
  34.4 3.1 collective-permute-start.1
  37.5 1.1 select_select_fusion.5
  39.7 0.9 pad_maximum_fusion.7
  40.5 0.9 pad_maximum_fusion.8
  41.5 1.3 collective-permute-start.2
  42.8 1.4 collective-permute-start.4
  44.2 3.3 convolution_convert_fusion
  47.5 10.2 %collective-permute-done.1 = bf16[2,128,1024]{2,1,0:T(8,128)(2,1)S(1)} collective-permute-done((bf16[2,128,1024]{2,1,0:T(8,128)(2,1)}, bf16[2,128,1024]{2,1,0:T(8,128)(2,1)S(1)}, u32[]{:S(2)}, u32[]{:S(2)}) %collective-permute-start.1) | collective-permute-done | bytes 524320 | tf_op jit(solution)/shard_map/ppermute | solution.py:362
  57.8 0.8 pad_maximum_fusion.1
  58.6 0.9 pad_maximum_fusion.2
  60.3 0.8 pad_maximum_fusion.4
  62.8 1.0 collective-permute-start.5
  63.8 1.3 collective-permute-start.6
  66.2 2.3 copy.127
  68.5 2.3 copy.128
  71.6 1.1 constant_dynamic-update-slice_fusion.2
  72.6 1.1 constant_dynamic-update-slice_fusion.1
  73.7 1.8 maximum_maximum_fusion
  75.6 1.1 constant_dynamic-update-slice_fusion.k_ref.keys
  76.7 1.4 copy-done.2
  78.1 7.5 %shard_map.111.probs = bf16[4,16,128,256]{3,2,1,0:T(8,128)(2,1)} custom-call(s32[16]{0:T(128)} %reshape.318.owners, bf16[4,128,1024]{2,1,0:T(8,128)(2,1)} %bitcast.122, bf16[8,128,1024]{2,1,0:T(8,128)(2,1)} %copy-done.2), custom_call_target="tpu_custom_call" | custom-call | bytes 25200000 | tf_op jit(solution)/shard_map/pallas_call | solution.py:395
  85.8 1.1 pad_maximum_fusion
  86.9 1.1 constant_dynamic-update-slice_fusion.6
  88.0 1.1 constant_dynamic-update-slice_fusion.5
  89.1 7.7 %collective-permute-done.7 = bf16[2,128,1024]{2,1,0:T(8,128)(2,1)} collective-permute-done((bf16[2,128,1024]{2,1,0:T(8,128)(2,1)}, bf16[2,128,1024]{2,1,0:T(8,128)(2,1)}, u32[]{:S(2)}, u32[]{:S(2)}) %collective-permute-start.7) | collective-permute-done | bytes 524320 | tf_op jit(solution)/shard_map/ppermute | solution.py:377
  96.8 1.1 constant_dynamic-update-slice_fusion.4.values
  97.9 0.9 broadcast_in_dim.76.arriving
  99.3 1.0 shard_map.113
  100.3 7.2 %all-to-all-start = ((bf16[8,1040,128]{2,1,0:T(8,128)(2,1)}), bf16[8,1040,128]{2,1,0:T(8,128)(2,1)S(1)}, u32[]{:S(2)}, u32[]{:S(2)}) async-start(bf16[8,1040,128]{2,1,0:T(8,128)(2,1)} %maximum_maximum_fusion), calls=%async_computation | async-start | bytes 4259840 | tf_op jit(solution)/shard_map/all_to_all | solution.py:381
  108.9 5.7 %shard_map.114.a0 = bf16[4,128,1024]{2,1,0:T(8,128)(2,1)} custom-call(s32[17]{0:T(128)} %get-tuple-element.285.scal, bf16[8,128,1024]{2,1,0:T(8,128)(2,1)} %copy-done.1, bf16[4,16,128,256]{3,2,1,0:T(8,128)(2,1)} %shard_map.111.probs, bf16[4,128,1024]{2,1,0:T(8,128)(2,1)} %get-tuple-element.151.a0), custom_call_target="tpu_custom_call", output_to_operand_aliasing={{}: (3, {})} | custom-call | bytes 18000000 | tf_op jit(solution)/shard_map/pallas_call | solution.py:505
  114.6 1.0 shard_map.115
  116.4 1.2 shard_map.116
  117.6 1.3 collective-permute-start.10
  118.9 1.2 collective-permute-start.12
  120.1 1.0 shard_map.117
  121.1 22.3 %collective-permute-done.10.arriving = bf16[128,2048]{1,0:T(8,128)(2,1)S(1)} collective-permute-done((bf16[128,2048]{1,0:T(8,128)(2,1)}, bf16[128,2048]{1,0:T(8,128)(2,1)S(1)}, u32[]{:S(2)}, u32[]{:S(2)}) %collective-permute-start.10) | collective-permute-done | bytes 524320 | tf_op jit(solution)/shard_map/ppermute | solution.py:548
  143.4 1.3 collective-permute-start.11
  144.7 10.6 %shard_map.118 = (bf16[128,2048]{1,0:T(8,128)(2,1)}, bf16[4,128,2048]{2,1,0:T(8,128)(2,1)}, bf16[4,128,2048]{2,1,0:T(8,128)(2,1)}, bf16[8,4,128,128]{3,2,1,0:T(8...) custom-call(s32[80]{0:T(128)} %reshape.317.scal, ...), custom_call_target="tpu_custom_call", output_to_operand_aliasing={{1}: (8, {}), {2}: (9, {}), {3}: (10, {}), {4}: (11, {}), {... | custom-call | bytes 39600000 | tf_op jit(solution)/shard_map/pallas_call | solution.py:466
  155.3 2.2 collective-permute-done.11.arriving
  157.5 1.9 collective-permute-start.13
  160.4 10.6 %shard_map.120 = (bf16[128,2048]{1,0:T(8,128)(2,1)}, bf16[4,128,2048]{2,1,0:T(8,128)(2,1)}, bf16[4,128,2048]{2,1,0:T(8,128)(2,1)}, bf16[8,4,128,128]{3,2,1,0:T(8...) custom-call(s32[80]{0:T(128)} %reshape.317.scal, ...), custom_call_target="tpu_custom_call", output_to_operand_aliasing={{1}: (8, {}), {2}: (9, {}), {3}: (10, {}), {4}: (11, {}), {... | custom-call | bytes 39600000 | tf_op jit(solution)/shard_map/pallas_call | solution.py:466
  171.0 1.9 collective-permute-start.14
  173.0 10.6 %shard_map.121 = (bf16[128,2048]{1,0:T(8,128)(2,1)}, bf16[4,128,2048]{2,1,0:T(8,128)(2,1)}, bf16[4,128,2048]{2,1,0:T(8,128)(2,1)}, bf16[8,4,128,128]{3,2,1,0:T(8...) custom-call(s32[80]{0:T(128)} %reshape.317.scal, ...), custom_call_target="tpu_custom_call", output_to_operand_aliasing={{1}: (8, {}), {2}: (9, {}), {3}: (10, {}), {4}: (11, {}), {... | custom-call | bytes 39600000 | tf_op jit(solution)/shard_map/pallas_call | solution.py:466
  183.6 2.5 collective-permute-done.14.arriving
  186.0 1.3 collective-permute-start.16
  187.4 10.6 %shard_map.122 = (bf16[128,2048]{1,0:T(8,128)(2,1)}, bf16[4,128,2048]{2,1,0:T(8,128)(2,1)}, bf16[4,128,2048]{2,1,0:T(8,128)(2,1)}, bf16[8,4,128,128]{3,2,1,0:T(8...) custom-call(s32[80]{0:T(128)} %reshape.317.scal, ...), custom_call_target="tpu_custom_call", output_to_operand_aliasing={{1}: (8, {}), {2}: (9, {}), {3}: (10, {}), {4}: (11, {}), {... | custom-call | bytes 39600000 | tf_op jit(solution)/shard_map/pallas_call | solution.py:466
  198.1 1.3 collective-permute-start.17
  199.4 1.0 shard_map.123
  200.4 1.5 collective-permute-start.19
  202.7 1.0 shard_map.124
  203.7 26.5 %collective-permute-done.19.parts_and_out_4_.parts_and_out_5_ = bf16[1,2,128,1024]{3,2,1,0:T(8,128)(2,1)S(1)} collective-permute-done((bf16[1,2,128,1024]{3,2,1,0:T(8,128)(2,1)}, bf16[1,2,128,1024]{3,2,1,0:T(8,128)(2,1)S(1)}, u32[]{:S(2)}, u32[]{:S(2)}) %collective-permute-start.19) | collective-permute-done | bytes 524320 | tf_op jit(solution)/shard_map/ppermute | solution.py:428
  231.0 8.3 %collective-permute-done.20.parts_and_out_7_.parts_and_out_8_ = bf16[1,2,128,1024]{3,2,1,0:T(8,128)(2,1)} collective-permute-done((bf16[1,2,128,1024]{3,2,1,0:T(8,128)(2,1)}, bf16[1,2,128,1024]{3,2,1,0:T(8,128)(2,1)}, u32[]{:S(2)}, u32[]{:S(2)}) %collective-permute-start.20) | collective-permute-done | bytes 524320 | tf_op jit(solution)/shard_map/ppermute | solution.py:428
  239.4 4.2 %all-to-all-start.1 = ((bf16[8,4,128,128]{3,2,1,0:T(8,128)(2,1)}), bf16[8,4,128,128]{3,2,1,0:T(8,128)(2,1)}, u32[]{:S(2)}, u32[]{:S(2)}) async-start(bf16[8,4,128,128]{3,2,1,0:T(8,128)(2,1)} %get-tuple-element.246), calls=%async_computation.1 | async-start | bytes 2097152 | tf_op jit(solution)/shard_map/all_to_all | solution.py:381
  243.8 10.5 %shard_map.125 = bf16[1024,2048]{1,0:T(8,128)(2,1)} custom-call(s32[1]{0:T(128)} %bitcast.44.par, bf16[512,2048]{1,0:T(8,128)(2,1)} %bitcast.112, bf16[512,1024]{1,0:T(8,128)(2,1)} %collective-permute-done.12.x_got, bf16[512,2048]{1,0:T(8,128)(2,1)} %bitcast.106, bf16[512,1024]{1,0:T(8,128)(2,1)} %bitcast.109, bf16[512,1024]{1,0:T(8,128)(2,1)} %copy-done.11, ...), custom_call_target="tpu_custom_call" | custom-call | bytes 32400000 | tf_op jit(solution)/shard_map/pallas_call | solution.py:577
  254.3 7.1 %all-to-all-done.1 = bf16[8,4,128,128]{3,2,1,0:T(8,128)(2,1)} async-done(((bf16[8,4,128,128]{3,2,1,0:T(8,128)(2,1)}), bf16[8,4,128,128]{3,2,1,0:T(8,128)(2,1)}, u32[]{:S(2)}, u32[]{:S(2)}) %all-to-all-start.1) | async-done | bytes 1048608 | tf_op jit(solution)/shard_map/all_to_all | solution.py:381
  265.2 25.6 %shard_map.126 = bf16[16,2,128,128]{3,2,1,0:T(8,128)(2,1)} custom-call(s32[128]{0:T(128)} %multiply_add_fusion.ids, s32[128]{0:T(128)} %reshape.327.mask, bf16[8,1040,128]{2,1,0:T(8,128)(2,1)} %copy-done.3, bf16[8,512,128]{2,1,0:T(8,128)(2,1)} %bitcast.46.d_ref, bf16[8,1040,128]{2,1,0:T(8,128)(2,1)} %copy-done.3), custom_call_target="tpu_custom_call" | custom-call | bytes 133200000 | tf_op jit(solution)/shard_map/pallas_call | solution.py:625
  290.8 55.4 %all_to_all.15 = bf16[8,2,2,128,128]{4,3,2,1,0:T(8,128)(2,1)S(1)} all-to-all(bf16[8,2,2,128,128]{4,3,2,1,0:T(8,128)(2,1)} %bitcast.121), channel_id=1, replica_groups=mesh['section'=4,'dp'=8] {'dp'}, dimensions={0} | all-to-all | bytes 2097152 | tf_op jit(solution)/shard_map/all_to_all | solution.py:381
  346.9 1.3 broadcast_in_dim_reshape.3
  348.2 20.7 %reduce-scatter.2.cloned.1.call-done = bf16[256,2048]{1,0:T(8,128)(2,1)} async-done(((bf16[1024,2048]{1,0:T(8,128)(2,1)}), bf16[256,2048]{1,0:T(8,128)(2,1)}) %reduce-scatter.2.cloned.1.call-update) | async-done | bytes 1048592 | tf_op jit(solution)/shard_map/reduce_scatter | solution.py:607
  368.9 2.2 slice_bitcast_fusion
  (138 shorter events, 21.1 us)
Async XLA Ops:
  7.2 4.6 %copy-start.20 = (s32[8,8]{1,0:T(8,128)S(1)}, s32[8,8]{1,0:T(8,128)}, u32[]{:S(2)}) copy-start(s32[8,8]{1,0:T(8,128)} %param.19) | copy-start | bytes 772
  7.2 4.6 %copy-start.19 = (s32[8,8]{1,0:T(8,128)S(1)}, s32[8,8]{1,0:T(8,128)}, u32[]{:S(2)}) copy-start(s32[8,8]{1,0:T(8,128)} %param.18) | copy-start | bytes 772
  8.5 24.1 %copy-start.8 = (bf16[1,2,2,128,1024]{4,3,2,1,0:T(8,128)(2,1)S(1)}, bf16[1,2,2,128,1024]{4,3,2,1,0:T(8,128)(2,1)}, u32[]{:S(2)}) copy-start(bf16[1,2,2,128,1024]{4,3,2,1,0:T(8,128)(2,1)} %param.16) | copy-start | bytes 3145732
  9.4 25.1 %collective-permute-start = (bf16[2,128,1024]{2,1,0:T(8,128)(2,1)S(1)}, bf16[2,128,1024]{2,1,0:T(8,128)(2,1)S(1)}, u32[]{:S(2)}, u32[]{:S(2)}) collective-permute-start(bf16[2,128,1024]{2,1,0:T(8,128)(2,1)S(1)} %get-tuple-element.262), channel_id=1, source_target_pairs={{0,4},{1,5},{2,6},{3,7},{4,0},{5,1},{6,2},{7,3},{8,12},{9,13},{10,... | collective-permute-start | bytes 1572872 | tf_op jit(solution)/shard_map/ppermute | solution.py:362
  34.4 23.3 %collective-permute-start.1 = (bf16[2,128,1024]{2,1,0:T(8,128)(2,1)}, bf16[2,128,1024]{2,1,0:T(8,128)(2,1)S(1)}, u32[]{:S(2)}, u32[]{:S(2)}) collective-permute-start(bf16[2,128,1024]{2,1,0:T(8,128)(2,1)} %get-tuple-element.128), channel_id=1, source_target_pairs={{0,4},{1,5},{2,6},{3,7},{4,0},{5,1},{6,2},{7,3},{8,12},{9,13},{10,... | collective-permute-start | bytes 1572872 | tf_op jit(solution)/shard_map/ppermute | solution.py:362
  38.6 5.5 %copy-start.4 = (bf16[1,4,128,2048]{3,2,1,0:T(8,128)(2,1)S(1)}, bf16[1,4,128,2048]{3,2,1,0:T(8,128)(2,1)}, u32[]{:S(2)}) copy-start(bf16[1,4,128,2048]{3,2,1,0:T(8,128)(2,1)} %param.12) | copy-start | bytes 6291460
  38.8 5.4 %copy-start = (bf16[1,2048,1024]{2,1,0:T(8,128)(2,1)S(1)}, bf16[1,2048,1024]{2,1,0:T(8,128)(2,1)}, u32[]{:S(2)}) copy-start(bf16[1,2048,1024]{2,1,0:T(8,128)(2,1)} %param.14) | copy-start | bytes 12582916
  41.5 29.5 %collective-permute-start.2 = (bf16[2,128,1024]{2,1,0:T(8,128)(2,1)}, bf16[2,128,1024]{2,1,0:T(8,128)(2,1)}, u32[]{:S(2)}, u32[]{:S(2)}) collective-permute-start(bf16[2,128,1024]{2,1,0:T(8,128)(2,1)} %pad_maximum_fusion.6), channel_id=1, source_target_pairs={{0,1},{1,0},{2,3},{3,2},{4,5},{5,4},{6,7},{7,6},{8,9},{9,8},{10,11... | collective-permute-start | bytes 1572872 | tf_op jit(solution)/shard_map/ppermute | solution.py:377
  42.8 29.9 %collective-permute-start.3 = (bf16[2,128,1024]{2,1,0:T(8,128)(2,1)}, bf16[2,128,1024]{2,1,0:T(8,128)(2,1)}, u32[]{:S(2)}, u32[]{:S(2)}) collective-permute-start(bf16[2,128,1024]{2,1,0:T(8,128)(2,1)} %pad_maximum_fusion.7), channel_id=1, source_target_pairs={{0,2},{1,3},{2,0},{3,1},{4,6},{5,7},{6,4},{7,5},{8,10},{9,11},{10,... | collective-permute-start | bytes 1572872 | tf_op jit(solution)/shard_map/ppermute | solution.py:377
  42.8 32.8 %collective-permute-start.4 = (bf16[2,128,1024]{2,1,0:T(8,128)(2,1)}, bf16[2,128,1024]{2,1,0:T(8,128)(2,1)}, u32[]{:S(2)}, u32[]{:S(2)}) collective-permute-start(bf16[2,128,1024]{2,1,0:T(8,128)(2,1)} %pad_maximum_fusion.8), channel_id=1, source_target_pairs={{0,3},{1,2},{2,1},{3,0},{4,7},{5,6},{6,5},{7,4},{8,11},{9,10},{10,... | collective-permute-start | bytes 1572872 | tf_op jit(solution)/shard_map/ppermute | solution.py:377
  57.8 3.4 copy-start.22
  62.8 24.1 %collective-permute-start.5 = (bf16[2,128,1024]{2,1,0:T(8,128)(2,1)}, bf16[2,128,1024]{2,1,0:T(8,128)(2,1)}, u32[]{:S(2)}, u32[]{:S(2)}) collective-permute-start(bf16[2,128,1024]{2,1,0:T(8,128)(2,1)} %pad_maximum_fusion.2), channel_id=1, source_target_pairs={{0,1},{1,0},{2,3},{3,2},{4,5},{5,4},{6,7},{7,6},{8,9},{9,8},{10,11... | collective-permute-start | bytes 1572872 | tf_op jit(solution)/shard_map/ppermute | solution.py:377
  63.8 24.2 %collective-permute-start.6 = (bf16[2,128,1024]{2,1,0:T(8,128)(2,1)}, bf16[2,128,1024]{2,1,0:T(8,128)(2,1)}, u32[]{:S(2)}, u32[]{:S(2)}) collective-permute-start(bf16[2,128,1024]{2,1,0:T(8,128)(2,1)} %pad_maximum_fusion.3), channel_id=1, source_target_pairs={{0,2},{1,3},{2,0},{3,1},{4,6},{5,7},{6,4},{7,5},{8,10},{9,11},{10,... | collective-permute-start | bytes 1572872 | tf_op jit(solution)/shard_map/ppermute | solution.py:377
  71.0 2.7 copy-start.7
  71.0 25.8 %collective-permute-start.7 = (bf16[2,128,1024]{2,1,0:T(8,128)(2,1)}, bf16[2,128,1024]{2,1,0:T(8,128)(2,1)}, u32[]{:S(2)}, u32[]{:S(2)}) collective-permute-start(bf16[2,128,1024]{2,1,0:T(8,128)(2,1)} %pad_maximum_fusion.4), channel_id=1, source_target_pairs={{0,3},{1,2},{2,1},{3,0},{4,7},{5,6},{6,5},{7,4},{8,11},{9,10},{10,... | collective-permute-start | bytes 1572872 | tf_op jit(solution)/shard_map/ppermute | solution.py:377
  76.6 1.4 copy-start.2
  78.1 7.5 %copy-start.10 = (bf16[2,128,1024]{2,1,0:T(8,128)(2,1)S(1)}, bf16[2,128,1024]{2,1,0:T(8,128)(2,1)}, u32[]{:S(2)}) copy-start(bf16[2,128,1024]{2,1,0:T(8,128)(2,1)} %pad_maximum_fusion.1) | copy-start | bytes 1572868
  78.1 7.5 %copy-start.5 = (bf16[1,4,128,2048]{3,2,1,0:T(8,128)(2,1)S(1)}, bf16[1,4,128,2048]{3,2,1,0:T(8,128)(2,1)}, u32[]{:S(2)}) copy-start(bf16[1,4,128,2048]{3,2,1,0:T(8,128)(2,1)} %param.12) | copy-start | bytes 6291460
  97.9 1.5 copy-start.1
  100.3 7.9 %copy-start.21 = (s32[16]{0:T(128)S(1)}, s32[16]{0:T(128)}, u32[]{:S(2)}) copy-start(s32[16]{0:T(128)} %reshape.318.owners) | copy-start | bytes 196
  100.3 60.0 %all-to-all-start = ((bf16[8,1040,128]{2,1,0:T(8,128)(2,1)}), bf16[8,1040,128]{2,1,0:T(8,128)(2,1)S(1)}, u32[]{:S(2)}, u32[]{:S(2)}) async-start(bf16[8,1040,128]{2,1,0:T(8,128)(2,1)} %maximum_maximum_fusion), calls=%async_computation | async-start | bytes 4259840 | tf_op jit(solution)/shard_map/all_to_all | solution.py:381
  107.5 8.1 %collective-permute-start.8 = (bf16[128,2048]{1,0:T(8,128)(2,1)}, bf16[128,2048]{1,0:T(8,128)(2,1)S(1)}, u32[]{:S(2)}, u32[]{:S(2)}) collective-permute-start(bf16[128,2048]{1,0:T(8,128)(2,1)} %get-tuple-element.159), channel_id=1, source_target_pairs={{24,16},{25,17},{26,18},{27,19},{28,20},{29,21},{30,22},{31,23}} | collective-permute-start | bytes 1572872 | tf_op jit(solution)/shard_map/ppermute | solution.py:548
  115.6 0.8 copy-start.13
  115.6 1.9 collective-permute-start.9
  117.6 2.6 copy-start.15
  117.6 25.8 %collective-permute-start.10 = (bf16[128,2048]{1,0:T(8,128)(2,1)}, bf16[128,2048]{1,0:T(8,128)(2,1)S(1)}, u32[]{:S(2)}, u32[]{:S(2)}) collective-permute-start(bf16[128,2048]{1,0:T(8,128)(2,1)} %get-tuple-element.177), channel_id=1, source_target_pairs={{16,8},{24,16},{17,9},{25,17},{18,10},{26,18},{19,11},{27,19},{20,... | collective-permute-start | bytes 1572872 | tf_op jit(solution)/shard_map/ppermute | solution.py:548
  118.9 41.5 %collective-permute-start.12 = (bf16[512,1024]{1,0:T(8,128)(2,1)}, bf16[512,1024]{1,0:T(8,128)(2,1)}, u32[]{:S(2)}, u32[]{:S(2)}) collective-permute-start(bf16[512,1024]{1,0:T(8,128)(2,1)} %pad_maximum_fusion), channel_id=1, source_target_pairs={{0,1},{1,0},{2,3},{3,2},{4,5},{5,4},{6,7},{7,6},{8,9},{9,8},{10,11... | collective-permute-start | bytes 3145736 | tf_op jit(solution)/shard_map/ppermute | solution.py:428
  143.4 1.3 copy-start.16
  143.4 14.1 %collective-permute-start.11 = (bf16[128,2048]{1,0:T(8,128)(2,1)}, bf16[128,2048]{1,0:T(8,128)(2,1)S(1)}, u32[]{:S(2)}, u32[]{:S(2)}) collective-permute-start(bf16[128,2048]{1,0:T(8,128)(2,1)} %get-tuple-element.186), channel_id=1, source_target_pairs={{16,8},{24,16},{17,9},{25,17},{18,10},{26,18},{19,11},{27,19},{20,... | collective-permute-start | bytes 1572872 | tf_op jit(solution)/shard_map/ppermute | solution.py:548
  157.5 2.7 copy-start.12
  157.5 13.5 %collective-permute-start.13 = (bf16[128,2048]{1,0:T(8,128)(2,1)}, bf16[128,2048]{1,0:T(8,128)(2,1)}, u32[]{:S(2)}, u32[]{:S(2)}) collective-permute-start(bf16[128,2048]{1,0:T(8,128)(2,1)} %get-tuple-element.200), channel_id=1, source_target_pairs={{8,0},{16,8},{9,1},{17,9},{10,2},{18,10},{11,3},{19,11},{12,4},{20... | collective-permute-start | bytes 1572872 | tf_op jit(solution)/shard_map/ppermute | solution.py:548
  160.2 27.2 %collective-permute-start.15 = (bf16[512,1024]{1,0:T(8,128)(2,1)}, bf16[512,1024]{1,0:T(8,128)(2,1)S(1)}, u32[]{:S(2)}, u32[]{:S(2)}) collective-permute-start(bf16[512,1024]{1,0:T(8,128)(2,1)} %bitcast.108), channel_id=1, source_target_pairs={{0,1},{1,0},{2,3},{3,2},{4,5},{5,4},{6,7},{7,6},{8,9},{9,8},{10,11... | collective-permute-start | bytes 3145736 | tf_op jit(solution)/shard_map/ppermute | solution.py:428
  160.4 102.6 %copy-start.3 = (bf16[8,1040,128]{2,1,0:T(8,128)(2,1)}, bf16[8,1040,128]{2,1,0:T(8,128)(2,1)S(1)}, u32[]{:S(2)}) copy-start(bf16[8,1040,128]{2,1,0:T(8,128)(2,1)S(1)} %all-to-all-done.q_ref.kv_ref) | copy-start | bytes 6389764
  171.0 15.0 %collective-permute-start.14 = (bf16[128,2048]{1,0:T(8,128)(2,1)}, bf16[128,2048]{1,0:T(8,128)(2,1)S(1)}, u32[]{:S(2)}, u32[]{:S(2)}) collective-permute-start(bf16[128,2048]{1,0:T(8,128)(2,1)} %get-tuple-element.209), channel_id=1, source_target_pairs={{8,0},{16,8},{9,1},{17,9},{10,2},{18,10},{11,3},{19,11},{12,4},{20... | collective-permute-start | bytes 1572872 | tf_op jit(solution)/shard_map/ppermute | solution.py:548
  186.0 1.3 copy-start.17
  186.0 12.0 %collective-permute-start.16 = (bf16[128,2048]{1,0:T(8,128)(2,1)}, bf16[128,2048]{1,0:T(8,128)(2,1)S(1)}, u32[]{:S(2)}, u32[]{:S(2)}) collective-permute-start(bf16[128,2048]{1,0:T(8,128)(2,1)} %get-tuple-element.220), channel_id=1, source_target_pairs={{8,0},{9,1},{10,2},{11,3},{12,4},{13,5},{14,6},{15,7}} | collective-permute-start | bytes 1572872 | tf_op jit(solution)/shard_map/ppermute | solution.py:548
  187.4 10.6 %copy-start.11 = (bf16[512,1024]{1,0:T(8,128)(2,1)}, bf16[512,1024]{1,0:T(8,128)(2,1)S(1)}, u32[]{:S(2)}) copy-start(bf16[512,1024]{1,0:T(8,128)(2,1)S(1)} %collective-permute-done.15.att_got) | copy-start | bytes 3145732
  198.0 1.4 copy-start.14
  198.0 32.2 %collective-permute-start.18 = (bf16[2,2,128,1024]{3,2,1,0:T(8,128)(2,1)}, bf16[2,2,128,1024]{3,2,1,0:T(8,128)(2,1)S(1)}, u32[]{:S(2)}, u32[]{:S(2)}) collective-permute-start(bf16[2,2,128,1024]{3,2,1,0:T(8,128)(2,1)} %get-tuple-element.238.parts_and_out_0_), channel_id=1, source_target_pairs={{0,1},{1,0},{2,3},{3,2},{4,5},{5,4},{6,7},{7,6},{8,9},{9,8},{10,11... | collective-permute-start | bytes 3145736 | tf_op jit(solution)/shard_map/ppermute | solution.py:428
  198.1 3.8 %collective-permute-start.17 = (bf16[128,2048]{1,0:T(8,128)(2,1)}, bf16[128,2048]{1,0:T(8,128)(2,1)S(1)}, u32[]{:S(2)}, u32[]{:S(2)}) collective-permute-start(bf16[128,2048]{1,0:T(8,128)(2,1)} %get-tuple-element.221), channel_id=1, source_target_pairs={{8,0},{9,1},{10,2},{11,3},{12,4},{13,5},{14,6},{15,7}} | collective-permute-start | bytes 1572872 | tf_op jit(solution)/shard_map/ppermute | solution.py:548
  200.4 29.8 %collective-permute-start.19 = (bf16[1,2,128,1024]{3,2,1,0:T(8,128)(2,1)}, bf16[1,2,128,1024]{3,2,1,0:T(8,128)(2,1)S(1)}, u32[]{:S(2)}, u32[]{:S(2)}) collective-permute-start(bf16[1,2,128,1024]{3,2,1,0:T(8,128)(2,1)} %get-tuple-element.240.parts_and_out_3_), channel_id=1, source_target_pairs={{0,1},{1,0},{2,3},{3,2},{4,5},{5,4},{6,7},{7,6},{8,9},{9,8},{10,11... | collective-permute-start | bytes 1572872 | tf_op jit(solution)/shard_map/ppermute | solution.py:428
  201.9 0.8 copy-start.18
  230.2 0.8 copy-start.9
  231.0 12.8 %copy-start.6 = (bf16[2,2,128,1024]{3,2,1,0:T(8,128)(2,1)}, bf16[2,2,128,1024]{3,2,1,0:T(8,128)(2,1)S(1)}, u32[]{:S(2)}) copy-start(bf16[2,2,128,1024]{3,2,1,0:T(8,128)(2,1)S(1)} %collective-permute-done.18.parts_and_out_1_.parts_and_out_2_) | copy-start | bytes 3145732
  231.0 8.3 %collective-permute-start.20 = (bf16[1,2,128,1024]{3,2,1,0:T(8,128)(2,1)}, bf16[1,2,128,1024]{3,2,1,0:T(8,128)(2,1)}, u32[]{:S(2)}, u32[]{:S(2)}) collective-permute-start(bf16[1,2,128,1024]{3,2,1,0:T(8,128)(2,1)} %get-tuple-element.243.parts_and_out_6_), channel_id=1, source_target_pairs={{0,1},{1,0},{2,3},{3,2},{4,5},{5,4},{6,7},{7,6},{8,9},{9,8},{10,11... | collective-permute-start | bytes 1572872 | tf_op jit(solution)/shard_map/ppermute | solution.py:428
  239.4 22.1 %all-to-all-start.1 = ((bf16[8,4,128,128]{3,2,1,0:T(8,128)(2,1)}), bf16[8,4,128,128]{3,2,1,0:T(8,128)(2,1)}, u32[]{:S(2)}, u32[]{:S(2)}) async-start(bf16[8,4,128,128]{3,2,1,0:T(8,128)(2,1)} %get-tuple-element.246), calls=%async_computation.1 | async-start | bytes 2097152 | tf_op jit(solution)/shard_map/all_to_all | solution.py:381
  243.6 125.3 %reduce-scatter.2.cloned.1.call-start = ((), (), s32[]{:S(2)}) async-start(), calls=%async_computation.4 | async-start | bytes 5242880 | tf_op jit(solution)/shard_map/reduce_scatter | solution.py:607
Sparse Core Ops, SparseCore 0:
  261.6 107.2 reduce-scatter.1

commit v3 on v2

--- a/solution.py
+++ b/solution.py
@@ -558,10 +558,9 @@
                 if hops:
                     stores[at], arrived[index + 1] = lax.optimization_barrier((stores[at], arrived[index + 1]))
                 if group == 0:
-                    stores[at], got = lax.optimization_barrier((stores[at], got))
+                    stores[at], stores[2], got = lax.optimization_barrier((stores[at], stores[2], got))
                 got.append(swap(stores[at]))
     grads_in, upstream, d_store, *s_stores = stores
-    got[-1], d_store = lax.optimization_barrier((got[-1], d_store))
 
     grad_scale = (flat * n_data) ** (-0.5)
     parts = []

time: 379 us -> 376 us (level)
    all_to_all x2, waiting for transfers between devices: 7.12 us -> 0.01 us  [exchange(): return lax.all_to_all(x, 'dp', split_axis=0, concat_axis=0, tiled=True)]
    ppermute x5, waiting for transfers between devices: 34.9 us -> 40.5 us  [swap(): return lax.ppermute(x, 'dp', partners)]
    unnamed x56 -> x58, local copies, waits for them, and re-layouts: 9.79 us -> 9.77 us
  transfers between devices with their start and end apart: 24 -> 24, of which waited for: 10 -> 9; matrix products, arithmetic and copies ran while one was open for 10% -> 10% of each run, Pallas kernels for 26% -> 26%
where the time goes in v3:
time: 376 us; the launch traced here: 375 us
  waiting for transfers between devices  108 us (29%)
  Pallas kernels  98.5 us (26%)
  blocking collectives  53.9 us (14%)
  starting transfers between devices  36.2 us (10%)
  local copies, waits for them, and re-layouts  33 us (9%)
  between operations  29.8 us (8%)
  other arithmetic  12 us (3%)
    all_to_all x1, blocking collectives, exchange(): return lax.all_to_all(x, 'dp', split_axis=0, concat_axis=0, tiled=True)  53.9 us
    pallas_call x10, Pallas kernels, tick(): pl.pallas_call(functools.partial(tick_kernel, chunks, index * table.shape...  48.4 us
    ppermute x5, waiting for transfers between devices, swap(): return lax.ppermute(x, 'dp', partners)  40.5 us
    ppermute x8, waiting for transfers between devices, body(): arrived.append(lax.ppermute(leaving, 'section', hops) if hops else leaving)  27.1 us
    pallas_call x1, Pallas kernels, body(): pl.pallas_call(functools.partial(block_grads_kernel, micros, blk_dev), co...  25.6 us
    reduce_scatter x1, waiting for transfers between devices, body(): lax.psum_scatter(terms, 'dp', scatter_dimension=0, tiled=True, axis_index...  20.5 us
    ppermute x2, waiting for transfers between devices, across(): lax.ppermute(own, 'dp', [(i, i ^ near) for i in range(n_data)])  12.3 us
    all_to_all x2, starting transfers between devices, exchange(): return lax.all_to_all(x, 'dp', split_axis=0, concat_axis=0, tiled=True)  11.4 us
  transfers between devices with their start and end apart: 24, of which 9 were waited for; matrix products, arithmetic and copies ran while one was open for 10% of the time, Pallas kernels for 26%

profile of v3, /device:TPU:9, one launch (start us, length us, event | category | flops | bytes accessed | tf_op | source)
XLA Modules:
  0.0 375.0 jit_solution(2062725520245981583)
XLA Ops:
  7.2 1.3 copy.149
  8.5 0.9 slice_bitcast_fusion.2
  9.4 2.3 collective-permute-start
  32.3 2.1 collective-permute-done
  34.4 3.1 collective-permute-start.1
  37.5 1.1 select_select_fusion.5
  38.8 0.8 pad_maximum_fusion.6
  39.7 0.9 pad_maximum_fusion.7
  40.5 0.9 pad_maximum_fusion.8
  41.5 1.3 collective-permute-start.2
  42.8 1.4 collective-permute-start.4
  44.2 3.3 convolution_convert_fusion
  47.5 10.2 %collective-permute-done.1 = bf16[2,128,1024]{2,1,0:T(8,128)(2,1)S(1)} collective-permute-done((bf16[2,128,1024]{2,1,0:T(8,128)(2,1)}, bf16[2,128,1024]{2,1,0:T(8,128)(2,1)S(1)}, u32[]{:S(2)}, u32[]{:S(2)}) %collective-permute-start.1) | collective-permute-done | bytes 524320 | tf_op jit(solution)/shard_map/ppermute | solution.py:362
  57.8 0.8 pad_maximum_fusion.1
  58.6 0.8 pad_maximum_fusion.2
  60.3 0.8 pad_maximum_fusion.4
  62.7 1.0 collective-permute-start.5
  63.7 1.3 collective-permute-start.6
  66.1 2.3 copy.127
  68.4 2.3 copy.128
  71.4 1.1 constant_dynamic-update-slice_fusion.2
  72.5 1.1 constant_dynamic-update-slice_fusion.1
  73.6 1.8 maximum_maximum_fusion
  75.4 1.1 constant_dynamic-update-slice_fusion.k_ref.keys
  76.5 1.4 copy-done.2
  77.9 7.5 %shard_map.111.probs = bf16[4,16,128,256]{3,2,1,0:T(8,128)(2,1)} custom-call(s32[16]{0:T(128)} %reshape.318.owners, bf16[4,128,1024]{2,1,0:T(8,128)(2,1)} %bitcast.122, bf16[8,128,1024]{2,1,0:T(8,128)(2,1)} %copy-done.2), custom_call_target="tpu_custom_call" | custom-call | bytes 25200000 | tf_op jit(solution)/shard_map/pallas_call | solution.py:395
  85.6 1.1 pad_maximum_fusion
  86.7 1.1 constant_dynamic-update-slice_fusion.6
  87.8 1.1 constant_dynamic-update-slice_fusion.5
  88.9 7.9 %collective-permute-done.7 = bf16[2,128,1024]{2,1,0:T(8,128)(2,1)} collective-permute-done((bf16[2,128,1024]{2,1,0:T(8,128)(2,1)}, bf16[2,128,1024]{2,1,0:T(8,128)(2,1)}, u32[]{:S(2)}, u32[]{:S(2)}) %collective-permute-start.7) | collective-permute-done | bytes 524320 | tf_op jit(solution)/shard_map/ppermute | solution.py:377
  96.8 1.1 constant_dynamic-update-slice_fusion.4.values
  97.9 0.9 broadcast_in_dim.76.arriving
  99.3 1.0 shard_map.113
  100.3 7.2 %all-to-all-start = ((bf16[8,1040,128]{2,1,0:T(8,128)(2,1)}), bf16[8,1040,128]{2,1,0:T(8,128)(2,1)S(1)}, u32[]{:S(2)}, u32[]{:S(2)}) async-start(bf16[8,1040,128]{2,1,0:T(8,128)(2,1)} %maximum_maximum_fusion), calls=%async_computation | async-start | bytes 4259840 | tf_op jit(solution)/shard_map/all_to_all | solution.py:381
  108.8 5.7 %shard_map.114.a0 = bf16[4,128,1024]{2,1,0:T(8,128)(2,1)} custom-call(s32[17]{0:T(128)} %get-tuple-element.283.scal, bf16[8,128,1024]{2,1,0:T(8,128)(2,1)} %copy-done.1, bf16[4,16,128,256]{3,2,1,0:T(8,128)(2,1)} %shard_map.111.probs, bf16[4,128,1024]{2,1,0:T(8,128)(2,1)} %get-tuple-element.150.a0), custom_call_target="tpu_custom_call", output_to_operand_aliasing={{}: (3, {})} | custom-call | bytes 18000000 | tf_op jit(solution)/shard_map/pallas_call | solution.py:505
  114.6 1.0 shard_map.115
  116.4 1.2 shard_map.116
  117.6 1.3 collective-permute-start.10
  118.9 1.3 collective-permute-start.12
  120.1 1.0 shard_map.117
  121.1 22.2 %collective-permute-done.10.arriving = bf16[128,2048]{1,0:T(8,128)(2,1)S(1)} collective-permute-done((bf16[128,2048]{1,0:T(8,128)(2,1)}, bf16[128,2048]{1,0:T(8,128)(2,1)S(1)}, u32[]{:S(2)}, u32[]{:S(2)}) %collective-permute-start.10) | collective-permute-done | bytes 524320 | tf_op jit(solution)/shard_map/ppermute | solution.py:548
  143.3 1.3 collective-permute-start.11
  144.6 10.6 %shard_map.118 = (bf16[128,2048]{1,0:T(8,128)(2,1)}, bf16[4,128,2048]{2,1,0:T(8,128)(2,1)}, bf16[4,128,2048]{2,1,0:T(8,128)(2,1)}, bf16[8,4,128,128]{3,2,1,0:T(8...) custom-call(s32[80]{0:T(128)} %reshape.317.scal, ...), custom_call_target="tpu_custom_call", output_to_operand_aliasing={{1}: (8, {}), {2}: (9, {}), {3}: (10, {}), {4}: (11, {}), {... | custom-call | bytes 39600000 | tf_op jit(solution)/shard_map/pallas_call | solution.py:466
  155.2 2.2 collective-permute-done.11.arriving
  157.4 1.9 collective-permute-start.13
  160.3 10.6 %shard_map.120 = (bf16[128,2048]{1,0:T(8,128)(2,1)}, bf16[4,128,2048]{2,1,0:T(8,128)(2,1)}, bf16[4,128,2048]{2,1,0:T(8,128)(2,1)}, bf16[8,4,128,128]{3,2,1,0:T(8...) custom-call(s32[80]{0:T(128)} %reshape.317.scal, ...), custom_call_target="tpu_custom_call", output_to_operand_aliasing={{1}: (8, {}), {2}: (9, {}), {3}: (10, {}), {4}: (11, {}), {... | custom-call | bytes 39600000 | tf_op jit(solution)/shard_map/pallas_call | solution.py:466
  171.0 1.9 collective-permute-start.14
  172.9 10.6 %shard_map.121 = (bf16[128,2048]{1,0:T(8,128)(2,1)}, bf16[4,128,2048]{2,1,0:T(8,128)(2,1)}, bf16[4,128,2048]{2,1,0:T(8,128)(2,1)}, bf16[8,4,128,128]{3,2,1,0:T(8...) custom-call(s32[80]{0:T(128)} %reshape.317.scal, ...), custom_call_target="tpu_custom_call", output_to_operand_aliasing={{1}: (8, {}), {2}: (9, {}), {3}: (10, {}), {4}: (11, {}), {... | custom-call | bytes 39600000 | tf_op jit(solution)/shard_map/pallas_call | solution.py:466
  183.5 2.6 collective-permute-done.14.arriving
  186.1 1.3 collective-permute-start.16
  187.4 10.6 %shard_map.122 = (bf16[128,2048]{1,0:T(8,128)(2,1)}, bf16[4,128,2048]{2,1,0:T(8,128)(2,1)}, bf16[4,128,2048]{2,1,0:T(8,128)(2,1)}, bf16[8,4,128,128]{3,2,1,0:T(8...) custom-call(s32[80]{0:T(128)} %reshape.317.scal, ...), custom_call_target="tpu_custom_call", output_to_operand_aliasing={{1}: (8, {}), {2}: (9, {}), {3}: (10, {}), {4}: (11, {}), {... | custom-call | bytes 39600000 | tf_op jit(solution)/shard_map/pallas_call | solution.py:466
  198.1 1.3 collective-permute-start.17
  199.5 1.0 shard_map.123
  200.5 1.5 collective-permute-start.19
  202.8 1.0 shard_map.124
  203.8 22.5 %collective-permute-done.19.parts_and_out_4_.parts_and_out_5_ = bf16[1,2,128,1024]{3,2,1,0:T(8,128)(2,1)S(1)} collective-permute-done((bf16[1,2,128,1024]{3,2,1,0:T(8,128)(2,1)}, bf16[1,2,128,1024]{3,2,1,0:T(8,128)(2,1)S(1)}, u32[]{:S(2)}, u32[]{:S(2)}) %collective-permute-start.19) | collective-permute-done | bytes 524320 | tf_op jit(solution)/shard_map/ppermute | solution.py:428
  226.3 4.2 %all-to-all-start.1 = ((bf16[8,4,128,128]{3,2,1,0:T(8,128)(2,1)}), bf16[8,4,128,128]{3,2,1,0:T(8,128)(2,1)}, u32[]{:S(2)}, u32[]{:S(2)}) async-start(bf16[8,4,128,128]{3,2,1,0:T(8,128)(2,1)} %get-tuple-element.244), calls=%async_computation.1 | async-start | bytes 2097152 | tf_op jit(solution)/shard_map/all_to_all | solution.py:381
  230.9 18.0 %collective-permute-done.20.parts_and_out_7_.parts_and_out_8_ = bf16[1,2,128,1024]{3,2,1,0:T(8,128)(2,1)S(1)} collective-permute-done((bf16[1,2,128,1024]{3,2,1,0:T(8,128)(2,1)S(1)}, bf16[1,2,128,1024]{3,2,1,0:T(8,128)(2,1)S(1)}, u32[]{:S(2)}, u32[]{:S(2)}) %collective-permute-start.20) | collective-permute-done | bytes 524320 | tf_op jit(solution)/shard_map/ppermute | solution.py:428
  249.7 10.5 %shard_map.125 = bf16[1024,2048]{1,0:T(8,128)(2,1)} custom-call(s32[1]{0:T(128)} %bitcast.44.par, bf16[512,2048]{1,0:T(8,128)(2,1)} %bitcast.112, bf16[512,1024]{1,0:T(8,128)(2,1)} %collective-permute-done.12.x_got, bf16[512,2048]{1,0:T(8,128)(2,1)} %bitcast.106, bf16[512,1024]{1,0:T(8,128)(2,1)} %bitcast.109, bf16[512,1024]{1,0:T(8,128)(2,1)} %copy-done.12, ...), custom_call_target="tpu_custom_call" | custom-call | bytes 32400000 | tf_op jit(solution)/shard_map/pallas_call | solution.py:576
  263.9 25.6 %shard_map.126 = bf16[16,2,128,128]{3,2,1,0:T(8,128)(2,1)} custom-call(s32[128]{0:T(128)} %multiply_add_fusion.ids, s32[128]{0:T(128)} %reshape.327.mask, bf16[8,1040,128]{2,1,0:T(8,128)(2,1)} %copy-done.4, bf16[8,512,128]{2,1,0:T(8,128)(2,1)} %bitcast.46.d_ref, bf16[8,1040,128]{2,1,0:T(8,128)(2,1)} %copy-done.4), custom_call_target="tpu_custom_call" | custom-call | bytes 133200000 | tf_op jit(solution)/shard_map/pallas_call | solution.py:624
  289.6 53.9 %all_to_all.15 = bf16[8,2,2,128,128]{4,3,2,1,0:T(8,128)(2,1)S(1)} all-to-all(bf16[8,2,2,128,128]{4,3,2,1,0:T(8,128)(2,1)} %bitcast.121), channel_id=1, replica_groups=mesh['section'=4,'dp'=8] {'dp'}, dimensions={0} | all-to-all | bytes 2097152 | tf_op jit(solution)/shard_map/all_to_all | solution.py:381
  344.1 1.3 broadcast_in_dim_reshape.3
  345.4 20.5 %reduce-scatter.2.cloned.1.call-done = bf16[256,2048]{1,0:T(8,128)(2,1)} async-done(((bf16[1024,2048]{1,0:T(8,128)(2,1)}), bf16[256,2048]{1,0:T(8,128)(2,1)}) %reduce-scatter.2.cloned.1.call-update) | async-done | bytes 1048592 | tf_op jit(solution)/shard_map/reduce_scatter | solution.py:606
  365.9 2.2 slice_bitcast_fusion
  (140 shorter events, 20.2 us)
Async XLA Ops:
  7.2 4.6 %copy-start.21 = (s32[8,8]{1,0:T(8,128)S(1)}, s32[8,8]{1,0:T(8,128)}, u32[]{:S(2)}) copy-start(s32[8,8]{1,0:T(8,128)} %param.19) | copy-start | bytes 772
  7.2 4.6 %copy-start.20 = (s32[8,8]{1,0:T(8,128)S(1)}, s32[8,8]{1,0:T(8,128)}, u32[]{:S(2)}) copy-start(s32[8,8]{1,0:T(8,128)} %param.18) | copy-start | bytes 772
  8.5 23.7 %copy-start.8 = (bf16[1,2,2,128,1024]{4,3,2,1,0:T(8,128)(2,1)S(1)}, bf16[1,2,2,128,1024]{4,3,2,1,0:T(8,128)(2,1)}, u32[]{:S(2)}) copy-start(bf16[1,2,2,128,1024]{4,3,2,1,0:T(8,128)(2,1)} %param.16) | copy-start | bytes 3145732
  9.4 25.1 %collective-permute-start = (bf16[2,128,1024]{2,1,0:T(8,128)(2,1)S(1)}, bf16[2,128,1024]{2,1,0:T(8,128)(2,1)S(1)}, u32[]{:S(2)}, u32[]{:S(2)}) collective-permute-start(bf16[2,128,1024]{2,1,0:T(8,128)(2,1)S(1)} %get-tuple-element.260), channel_id=1, source_target_pairs={{0,4},{1,5},{2,6},{3,7},{4,0},{5,1},{6,2},{7,3},{8,12},{9,13},{10,... | collective-permute-start | bytes 1572872 | tf_op jit(solution)/shard_map/ppermute | solution.py:362
  34.4 23.3 %collective-permute-start.1 = (bf16[2,128,1024]{2,1,0:T(8,128)(2,1)}, bf16[2,128,1024]{2,1,0:T(8,128)(2,1)S(1)}, u32[]{:S(2)}, u32[]{:S(2)}) collective-permute-start(bf16[2,128,1024]{2,1,0:T(8,128)(2,1)} %get-tuple-element.127), channel_id=1, source_target_pairs={{0,4},{1,5},{2,6},{3,7},{4,0},{5,1},{6,2},{7,3},{8,12},{9,13},{10,... | collective-permute-start | bytes 1572872 | tf_op jit(solution)/shard_map/ppermute | solution.py:362
  38.6 5.5 %copy-start.5 = (bf16[1,4,128,2048]{3,2,1,0:T(8,128)(2,1)S(1)}, bf16[1,4,128,2048]{3,2,1,0:T(8,128)(2,1)}, u32[]{:S(2)}) copy-start(bf16[1,4,128,2048]{3,2,1,0:T(8,128)(2,1)} %param.12) | copy-start | bytes 6291460
  38.8 5.4 %copy-start = (bf16[1,2048,1024]{2,1,0:T(8,128)(2,1)S(1)}, bf16[1,2048,1024]{2,1,0:T(8,128)(2,1)}, u32[]{:S(2)}) copy-start(bf16[1,2048,1024]{2,1,0:T(8,128)(2,1)} %param.14) | copy-start | bytes 12582916
  41.5 29.4 %collective-permute-start.2 = (bf16[2,128,1024]{2,1,0:T(8,128)(2,1)}, bf16[2,128,1024]{2,1,0:T(8,128)(2,1)}, u32[]{:S(2)}, u32[]{:S(2)}) collective-permute-start(bf16[2,128,1024]{2,1,0:T(8,128)(2,1)} %pad_maximum_fusion.6), channel_id=1, source_target_pairs={{0,1},{1,0},{2,3},{3,2},{4,5},{5,4},{6,7},{7,6},{8,9},{9,8},{10,11... | collective-permute-start | bytes 1572872 | tf_op jit(solution)/shard_map/ppermute | solution.py:377
  42.8 29.7 %collective-permute-start.3 = (bf16[2,128,1024]{2,1,0:T(8,128)(2,1)}, bf16[2,128,1024]{2,1,0:T(8,128)(2,1)}, u32[]{:S(2)}, u32[]{:S(2)}) collective-permute-start(bf16[2,128,1024]{2,1,0:T(8,128)(2,1)} %pad_maximum_fusion.7), channel_id=1, source_target_pairs={{0,2},{1,3},{2,0},{3,1},{4,6},{5,7},{6,4},{7,5},{8,10},{9,11},{10,... | collective-permute-start | bytes 1572872 | tf_op jit(solution)/shard_map/ppermute | solution.py:377
  42.8 32.7 %collective-permute-start.4 = (bf16[2,128,1024]{2,1,0:T(8,128)(2,1)}, bf16[2,128,1024]{2,1,0:T(8,128)(2,1)}, u32[]{:S(2)}, u32[]{:S(2)}) collective-permute-start(bf16[2,128,1024]{2,1,0:T(8,128)(2,1)} %pad_maximum_fusion.8), channel_id=1, source_target_pairs={{0,3},{1,2},{2,1},{3,0},{4,7},{5,6},{6,5},{7,4},{8,11},{9,10},{10,... | collective-permute-start | bytes 1572872 | tf_op jit(solution)/shard_map/ppermute | solution.py:377
  57.8 3.4 copy-start.23
  62.7 24.1 %collective-permute-start.5 = (bf16[2,128,1024]{2,1,0:T(8,128)(2,1)}, bf16[2,128,1024]{2,1,0:T(8,128)(2,1)}, u32[]{:S(2)}, u32[]{:S(2)}) collective-permute-start(bf16[2,128,1024]{2,1,0:T(8,128)(2,1)} %pad_maximum_fusion.2), channel_id=1, source_target_pairs={{0,1},{1,0},{2,3},{3,2},{4,5},{5,4},{6,7},{7,6},{8,9},{9,8},{10,11... | collective-permute-start | bytes 1572872 | tf_op jit(solution)/shard_map/ppermute | solution.py:377
  63.7 24.1 %collective-permute-start.6 = (bf16[2,128,1024]{2,1,0:T(8,128)(2,1)}, bf16[2,128,1024]{2,1,0:T(8,128)(2,1)}, u32[]{:S(2)}, u32[]{:S(2)}) collective-permute-start(bf16[2,128,1024]{2,1,0:T(8,128)(2,1)} %pad_maximum_fusion.3), channel_id=1, source_target_pairs={{0,2},{1,3},{2,0},{3,1},{4,6},{5,7},{6,4},{7,5},{8,10},{9,11},{10,... | collective-permute-start | bytes 1572872 | tf_op jit(solution)/shard_map/ppermute | solution.py:377
  70.8 2.7 copy-start.7
  70.9 25.9 %collective-permute-start.7 = (bf16[2,128,1024]{2,1,0:T(8,128)(2,1)}, bf16[2,128,1024]{2,1,0:T(8,128)(2,1)}, u32[]{:S(2)}, u32[]{:S(2)}) collective-permute-start(bf16[2,128,1024]{2,1,0:T(8,128)(2,1)} %pad_maximum_fusion.4), channel_id=1, source_target_pairs={{0,3},{1,2},{2,1},{3,0},{4,7},{5,6},{6,5},{7,4},{8,11},{9,10},{10,... | collective-permute-start | bytes 1572872 | tf_op jit(solution)/shard_map/ppermute | solution.py:377
  76.5 1.4 copy-start.2
  77.9 7.5 %copy-start.11 = (bf16[2,128,1024]{2,1,0:T(8,128)(2,1)S(1)}, bf16[2,128,1024]{2,1,0:T(8,128)(2,1)}, u32[]{:S(2)}) copy-start(bf16[2,128,1024]{2,1,0:T(8,128)(2,1)} %pad_maximum_fusion.1) | copy-start | bytes 1572868
  77.9 7.5 %copy-start.6 = (bf16[1,4,128,2048]{3,2,1,0:T(8,128)(2,1)S(1)}, bf16[1,4,128,2048]{3,2,1,0:T(8,128)(2,1)}, u32[]{:S(2)}) copy-start(bf16[1,4,128,2048]{3,2,1,0:T(8,128)(2,1)} %param.12) | copy-start | bytes 6291460
  97.9 1.5 copy-start.1
  100.3 7.9 %copy-start.22 = (s32[16]{0:T(128)S(1)}, s32[16]{0:T(128)}, u32[]{:S(2)}) copy-start(s32[16]{0:T(128)} %reshape.318.owners) | copy-start | bytes 196
  100.3 60.0 %all-to-all-start = ((bf16[8,1040,128]{2,1,0:T(8,128)(2,1)}), bf16[8,1040,128]{2,1,0:T(8,128)(2,1)S(1)}, u32[]{:S(2)}, u32[]{:S(2)}) async-start(bf16[8,1040,128]{2,1,0:T(8,128)(2,1)} %maximum_maximum_fusion), calls=%async_computation | async-start | bytes 4259840 | tf_op jit(solution)/shard_map/all_to_all | solution.py:381
  107.5 8.0 %collective-permute-start.8 = (bf16[128,2048]{1,0:T(8,128)(2,1)}, bf16[128,2048]{1,0:T(8,128)(2,1)S(1)}, u32[]{:S(2)}, u32[]{:S(2)}) collective-permute-start(bf16[128,2048]{1,0:T(8,128)(2,1)} %get-tuple-element.158), channel_id=1, source_target_pairs={{24,16},{25,17},{26,18},{27,19},{28,20},{29,21},{30,22},{31,23}} | collective-permute-start | bytes 1572872 | tf_op jit(solution)/shard_map/ppermute | solution.py:548
  115.6 0.8 copy-start.14
  115.6 1.9 collective-permute-start.9
  117.6 2.6 copy-start.16
  117.6 25.7 %collective-permute-start.10 = (bf16[128,2048]{1,0:T(8,128)(2,1)}, bf16[128,2048]{1,0:T(8,128)(2,1)S(1)}, u32[]{:S(2)}, u32[]{:S(2)}) collective-permute-start(bf16[128,2048]{1,0:T(8,128)(2,1)} %get-tuple-element.176), channel_id=1, source_target_pairs={{16,8},{24,16},{17,9},{25,17},{18,10},{26,18},{19,11},{27,19},{20,... | collective-permute-start | bytes 1572872 | tf_op jit(solution)/shard_map/ppermute | solution.py:548
  118.9 41.4 %collective-permute-start.12 = (bf16[512,1024]{1,0:T(8,128)(2,1)}, bf16[512,1024]{1,0:T(8,128)(2,1)}, u32[]{:S(2)}, u32[]{:S(2)}) collective-permute-start(bf16[512,1024]{1,0:T(8,128)(2,1)} %pad_maximum_fusion), channel_id=1, source_target_pairs={{0,1},{1,0},{2,3},{3,2},{4,5},{5,4},{6,7},{7,6},{8,9},{9,8},{10,11... | collective-permute-start | bytes 3145736 | tf_op jit(solution)/shard_map/ppermute | solution.py:428
  143.3 1.3 copy-start.17
  143.3 14.1 %collective-permute-start.11 = (bf16[128,2048]{1,0:T(8,128)(2,1)}, bf16[128,2048]{1,0:T(8,128)(2,1)S(1)}, u32[]{:S(2)}, u32[]{:S(2)}) collective-permute-start(bf16[128,2048]{1,0:T(8,128)(2,1)} %get-tuple-element.185), channel_id=1, source_target_pairs={{16,8},{24,16},{17,9},{25,17},{18,10},{26,18},{19,11},{27,19},{20,... | collective-permute-start | bytes 1572872 | tf_op jit(solution)/shard_map/ppermute | solution.py:548
  157.4 2.7 copy-start.13
  157.4 13.5 %collective-permute-start.13 = (bf16[128,2048]{1,0:T(8,128)(2,1)}, bf16[128,2048]{1,0:T(8,128)(2,1)}, u32[]{:S(2)}, u32[]{:S(2)}) collective-permute-start(bf16[128,2048]{1,0:T(8,128)(2,1)} %get-tuple-element.199), channel_id=1, source_target_pairs={{8,0},{16,8},{9,1},{17,9},{10,2},{18,10},{11,3},{19,11},{12,4},{20... | collective-permute-start | bytes 1572872 | tf_op jit(solution)/shard_map/ppermute | solution.py:548
  160.1 27.3 %collective-permute-start.15 = (bf16[512,1024]{1,0:T(8,128)(2,1)}, bf16[512,1024]{1,0:T(8,128)(2,1)S(1)}, u32[]{:S(2)}, u32[]{:S(2)}) collective-permute-start(bf16[512,1024]{1,0:T(8,128)(2,1)} %bitcast.108), channel_id=1, source_target_pairs={{0,1},{1,0},{2,3},{3,2},{4,5},{5,4},{6,7},{7,6},{8,9},{9,8},{10,11... | collective-permute-start | bytes 3145736 | tf_op jit(solution)/shard_map/ppermute | solution.py:428
  160.3 101.4 %copy-start.4 = (bf16[8,1040,128]{2,1,0:T(8,128)(2,1)}, bf16[8,1040,128]{2,1,0:T(8,128)(2,1)S(1)}, u32[]{:S(2)}) copy-start(bf16[8,1040,128]{2,1,0:T(8,128)(2,1)S(1)} %all-to-all-done.q_ref.kv_ref) | copy-start | bytes 6389764
  171.0 15.1 %collective-permute-start.14 = (bf16[128,2048]{1,0:T(8,128)(2,1)}, bf16[128,2048]{1,0:T(8,128)(2,1)S(1)}, u32[]{:S(2)}, u32[]{:S(2)}) collective-permute-start(bf16[128,2048]{1,0:T(8,128)(2,1)} %get-tuple-element.208), channel_id=1, source_target_pairs={{8,0},{16,8},{9,1},{17,9},{10,2},{18,10},{11,3},{19,11},{12,4},{20... | collective-permute-start | bytes 1572872 | tf_op jit(solution)/shard_map/ppermute | solution.py:548
  186.1 1.3 copy-start.18
  186.1 11.9 %collective-permute-start.16 = (bf16[128,2048]{1,0:T(8,128)(2,1)}, bf16[128,2048]{1,0:T(8,128)(2,1)S(1)}, u32[]{:S(2)}, u32[]{:S(2)}) collective-permute-start(bf16[128,2048]{1,0:T(8,128)(2,1)} %get-tuple-element.219), channel_id=1, source_target_pairs={{8,0},{9,1},{10,2},{11,3},{12,4},{13,5},{14,6},{15,7}} | collective-permute-start | bytes 1572872 | tf_op jit(solution)/shard_map/ppermute | solution.py:548
  187.4 10.6 %copy-start.12 = (bf16[512,1024]{1,0:T(8,128)(2,1)}, bf16[512,1024]{1,0:T(8,128)(2,1)S(1)}, u32[]{:S(2)}) copy-start(bf16[512,1024]{1,0:T(8,128)(2,1)S(1)} %collective-permute-done.15.att_got) | copy-start | bytes 3145732
  198.1 1.4 copy-start.15
  198.1 28.2 %collective-permute-start.18 = (bf16[2,2,128,1024]{3,2,1,0:T(8,128)(2,1)}, bf16[2,2,128,1024]{3,2,1,0:T(8,128)(2,1)}, u32[]{:S(2)}, u32[]{:S(2)}) collective-permute-start(bf16[2,2,128,1024]{3,2,1,0:T(8,128)(2,1)} %get-tuple-element.237.parts_and_out_0_), channel_id=1, source_target_pairs={{0,1},{1,0},{2,3},{3,2},{4,5},{5,4},{6,7},{7,6},{8,9},{9,8},{10,11... | collective-permute-start | bytes 3145736 | tf_op jit(solution)/shard_map/ppermute | solution.py:428
  198.1 3.8 %collective-permute-start.17 = (bf16[128,2048]{1,0:T(8,128)(2,1)}, bf16[128,2048]{1,0:T(8,128)(2,1)S(1)}, u32[]{:S(2)}, u32[]{:S(2)}) collective-permute-start(bf16[128,2048]{1,0:T(8,128)(2,1)} %get-tuple-element.220), channel_id=1, source_target_pairs={{8,0},{9,1},{10,2},{11,3},{12,4},{13,5},{14,6},{15,7}} | collective-permute-start | bytes 1572872 | tf_op jit(solution)/shard_map/ppermute | solution.py:548
  200.5 25.8 %collective-permute-start.19 = (bf16[1,2,128,1024]{3,2,1,0:T(8,128)(2,1)}, bf16[1,2,128,1024]{3,2,1,0:T(8,128)(2,1)S(1)}, u32[]{:S(2)}, u32[]{:S(2)}) collective-permute-start(bf16[1,2,128,1024]{3,2,1,0:T(8,128)(2,1)} %get-tuple-element.240.parts_and_out_3_), channel_id=1, source_target_pairs={{0,1},{1,0},{2,3},{3,2},{4,5},{5,4},{6,7},{7,6},{8,9},{9,8},{10,11... | collective-permute-start | bytes 1572872 | tf_op jit(solution)/shard_map/ppermute | solution.py:428
  202.0 0.8 copy-start.19
  203.8 27.0 %copy-start.3 = (bf16[1,2,128,1024]{3,2,1,0:T(8,128)(2,1)S(1)}, bf16[1,2,128,1024]{3,2,1,0:T(8,128)(2,1)}, u32[]{:S(2)}) copy-start(bf16[1,2,128,1024]{3,2,1,0:T(8,128)(2,1)} %get-tuple-element.243.parts_and_out_6_) | copy-start | bytes 1572868
  226.3 22.6 %copy-start.9 = (bf16[1,2,128,1024]{3,2,1,0:T(8,128)(2,1)}, bf16[1,2,128,1024]{3,2,1,0:T(8,128)(2,1)S(1)}, u32[]{:S(2)}) copy-start(bf16[1,2,128,1024]{3,2,1,0:T(8,128)(2,1)S(1)} %collective-permute-done.19.parts_and_out_4_.parts_and_out_5_) | copy-start | bytes 1572868
  226.3 33.9 %all-to-all-start.1 = ((bf16[8,4,128,128]{3,2,1,0:T(8,128)(2,1)}), bf16[8,4,128,128]{3,2,1,0:T(8,128)(2,1)}, u32[]{:S(2)}, u32[]{:S(2)}) async-start(bf16[8,4,128,128]{3,2,1,0:T(8,128)(2,1)} %get-tuple-element.244), calls=%async_computation.1 | async-start | bytes 2097152 | tf_op jit(solution)/shard_map/all_to_all | solution.py:381
  230.5 135.4 %reduce-scatter.2.cloned.1.call-start = ((), (), s32[]{:S(2)}) async-start(), calls=%async_computation.4 | async-start | bytes 5242880 | tf_op jit(solution)/shard_map/reduce_scatter | solution.py:606
  230.8 18.1 %collective-permute-start.20 = (bf16[1,2,128,1024]{3,2,1,0:T(8,128)(2,1)S(1)}, bf16[1,2,128,1024]{3,2,1,0:T(8,128)(2,1)S(1)}, u32[]{:S(2)}, u32[]{:S(2)}) collective-permute-start(bf16[1,2,128,1024]{3,2,1,0:T(8,128)(2,1)S(1)} %copy-done.3), channel_id=1, source_target_pairs={{0,1},{1,0},{2,3},{3,2},{4,5},{5,4},{6,7},{7,6},{8,9},{9,8},{10,11... | collective-permute-start | bytes 1572872 | tf_op jit(solution)/shard_map/ppermute | solution.py:428
  248.9 0.8 copy-start.10
Sparse Core Ops, SparseCore 0:
  260.3 105.5 reduce-scatter.1

commit v4 on v1

--- a/solution.py
+++ b/solution.py
@@ -524,8 +524,12 @@
             compiler_params=params(),
         )(jnp.concatenate([enabled[None].astype(jnp.int32), owners.reshape(-1)]), values, probs, store)
 
-    *stores, attended = unwritten(*store_shapes, jax.ShapeDtypeStruct((micros, tokens, width), BF))
-    arrived = [jnp.zeros((tokens, model), BF)] * 2
+    *stores, attended, no_arrival = unwritten(
+        *store_shapes,
+        jax.ShapeDtypeStruct((micros, tokens, width), BF),
+        jax.ShapeDtypeStruct((tokens, model), BF),
+    )
+    arrived = [no_arrival] * 2
     got = []
     for index in range(ticks):
         if index == micros + 3:

time: 372 us -> 372 us (level)
  no operation moved by 1% of the time
where the time goes in v4:
time: 372 us; the launch traced here: 371 us
  waiting for transfers between devices  107 us (29%)
  Pallas kernels  98.5 us (26%)
  blocking collectives  52.1 us (14%)
  starting transfers between devices  34.8 us (9%)
  local copies, waits for them, and re-layouts  32.9 us (9%)
  between operations  29.9 us (8%)
  other arithmetic  12.2 us (3%)
    all_to_all x1, blocking collectives, exchange(): return lax.all_to_all(x, 'dp', split_axis=0, concat_axis=0, tiled=True)  52.1 us
    pallas_call x10, Pallas kernels, tick(): pl.pallas_call(functools.partial(tick_kernel, chunks, index * table.shape...  48.4 us
    ppermute x5, waiting for transfers between devices, swap(): return lax.ppermute(x, 'dp', partners)  44.6 us
    ppermute x8, waiting for transfers between devices, body(): arrived.append(lax.ppermute(leaving, 'section', hops) if hops else leaving)  27.5 us
    pallas_call x1, Pallas kernels, body(): pl.pallas_call(functools.partial(block_grads_kernel, micros, blk_dev), co...  25.6 us
    reduce_scatter x1, waiting for transfers between devices, body(): lax.psum_scatter(terms, 'dp', scatter_dimension=0, tiled=True, axis_index...  15.1 us
    ppermute x2, waiting for transfers between devices, across(): lax.ppermute(own, 'dp', [(i, i ^ near) for i in range(n_data)])  12.1 us
    all_to_all x2, starting transfers between devices, exchange(): return lax.all_to_all(x, 'dp', split_axis=0, concat_axis=0, tiled=True)  11.5 us
  transfers between devices with their start and end apart: 24, of which 11 were waited for; matrix products, arithmetic and copies ran while one was open for 10% of the time, Pallas kernels for 26%

profile of v4, /device:TPU:9, one launch (start us, length us, event | category | flops | bytes accessed | tf_op | source)
XLA Modules:
  0.0 370.9 jit_solution(787816060409146022)
XLA Ops:
  7.2 1.3 copy.149
  8.5 0.9 slice_bitcast_fusion.2
  9.4 2.3 collective-permute-start
  32.5 1.9 collective-permute-done
  34.5 3.1 collective-permute-start.1
  37.6 1.1 select_select_fusion.5
  38.8 0.9 pad_maximum_fusion.6
  39.7 0.9 pad_maximum_fusion.7
  41.5 1.3 collective-permute-start.2
  42.8 1.4 collective-permute-start.4
  44.2 3.3 convolution_convert_fusion
  47.5 10.2 %collective-permute-done.1 = bf16[2,128,1024]{2,1,0:T(8,128)(2,1)S(1)} collective-permute-done((bf16[2,128,1024]{2,1,0:T(8,128)(2,1)}, bf16[2,128,1024]{2,1,0:T(8,128)(2,1)S(1)}, u32[]{:S(2)}, u32[]{:S(2)}) %collective-permute-start.1) | collective-permute-done | bytes 524320 | tf_op jit(solution)/shard_map/ppermute | solution.py:362
  57.8 0.9 pad_maximum_fusion.1
  59.5 0.9 pad_maximum_fusion.3
  60.4 0.9 pad_maximum_fusion.4
  62.8 1.0 collective-permute-start.5
  63.8 1.3 collective-permute-start.6
  66.1 2.3 copy.127
  68.4 2.3 copy.128
  71.5 1.1 constant_dynamic-update-slice_fusion.2
  72.6 1.1 constant_dynamic-update-slice_fusion.1
  73.6 1.8 maximum_maximum_fusion
  75.5 1.1 constant_dynamic-update-slice_fusion.k_ref.keys
  76.6 1.4 copy-done.2
  78.0 7.5 %shard_map.112.probs = bf16[4,16,128,256]{3,2,1,0:T(8,128)(2,1)} custom-call(s32[16]{0:T(128)} %reshape.318.owners, bf16[4,128,1024]{2,1,0:T(8,128)(2,1)} %bitcast.122, bf16[8,128,1024]{2,1,0:T(8,128)(2,1)} %copy-done.2), custom_call_target="tpu_custom_call" | custom-call | bytes 25200000 | tf_op jit(solution)/shard_map/pallas_call | solution.py:395
  85.7 1.1 pad_maximum_fusion
  86.8 1.1 constant_dynamic-update-slice_fusion.6
  87.9 1.1 constant_dynamic-update-slice_fusion.5
  89.0 7.9 %collective-permute-done.7 = bf16[2,128,1024]{2,1,0:T(8,128)(2,1)} collective-permute-done((bf16[2,128,1024]{2,1,0:T(8,128)(2,1)}, bf16[2,128,1024]{2,1,0:T(8,128)(2,1)}, u32[]{:S(2)}, u32[]{:S(2)}) %collective-permute-start.7) | collective-permute-done | bytes 524320 | tf_op jit(solution)/shard_map/ppermute | solution.py:377
  96.9 1.1 constant_dynamic-update-slice_fusion.4.values
  98.0 1.3 copy-done.1
  99.3 1.0 shard_map.113
  100.2 7.2 %all-to-all-start = ((bf16[8,1040,128]{2,1,0:T(8,128)(2,1)}), bf16[8,1040,128]{2,1,0:T(8,128)(2,1)S(1)}, u32[]{:S(2)}, u32[]{:S(2)}) async-start(bf16[8,1040,128]{2,1,0:T(8,128)(2,1)} %maximum_maximum_fusion), calls=%async_computation | async-start | bytes 4259840 | tf_op jit(solution)/shard_map/all_to_all | solution.py:381
  108.8 5.7 %shard_map.114.a0 = bf16[4,128,1024]{2,1,0:T(8,128)(2,1)} custom-call(s32[17]{0:T(128)} %get-tuple-element.285.scal, bf16[8,128,1024]{2,1,0:T(8,128)(2,1)} %copy-done.1, bf16[4,16,128,256]{3,2,1,0:T(8,128)(2,1)} %shard_map.112.probs, bf16[4,128,1024]{2,1,0:T(8,128)(2,1)} %get-tuple-element.152.a0), custom_call_target="tpu_custom_call", output_to_operand_aliasing={{}: (3, {})} | custom-call | bytes 18000000 | tf_op jit(solution)/shard_map/pallas_call | solution.py:505
  114.5 1.0 shard_map.115
  116.4 1.2 shard_map.116
  117.6 1.3 collective-permute-start.10
  118.9 1.2 collective-permute-start.12
  120.1 1.0 shard_map.117
  121.1 22.1 %collective-permute-done.10.arriving = bf16[128,2048]{1,0:T(8,128)(2,1)S(1)} collective-permute-done((bf16[128,2048]{1,0:T(8,128)(2,1)}, bf16[128,2048]{1,0:T(8,128)(2,1)S(1)}, u32[]{:S(2)}, u32[]{:S(2)}) %collective-permute-start.10) | collective-permute-done | bytes 524320 | tf_op jit(solution)/shard_map/ppermute | solution.py:552
  143.1 1.3 collective-permute-start.11
  144.4 10.6 %shard_map.118 = (bf16[128,2048]{1,0:T(8,128)(2,1)}, bf16[4,128,2048]{2,1,0:T(8,128)(2,1)}, bf16[4,128,2048]{2,1,0:T(8,128)(2,1)}, bf16[8,4,128,128]{3,2,1,0:T(8...) custom-call(s32[80]{0:T(128)} %reshape.317.scal, ...), custom_call_target="tpu_custom_call", output_to_operand_aliasing={{1}: (8, {}), {2}: (9, {}), {3}: (10, {}), {4}: (11, {}), {... | custom-call | bytes 39600000 | tf_op jit(solution)/shard_map/pallas_call | solution.py:466
  155.0 2.2 collective-permute-done.11.arriving
  157.2 1.9 collective-permute-start.13
  160.1 10.6 %shard_map.120 = (bf16[128,2048]{1,0:T(8,128)(2,1)}, bf16[4,128,2048]{2,1,0:T(8,128)(2,1)}, bf16[4,128,2048]{2,1,0:T(8,128)(2,1)}, bf16[8,4,128,128]{3,2,1,0:T(8...) custom-call(s32[80]{0:T(128)} %reshape.317.scal, ...), custom_call_target="tpu_custom_call", output_to_operand_aliasing={{1}: (8, {}), {2}: (9, {}), {3}: (10, {}), {4}: (11, {}), {... | custom-call | bytes 39600000 | tf_op jit(solution)/shard_map/pallas_call | solution.py:466
  170.8 1.9 collective-permute-start.14
  172.7 10.6 %shard_map.121 = (bf16[128,2048]{1,0:T(8,128)(2,1)}, bf16[4,128,2048]{2,1,0:T(8,128)(2,1)}, bf16[4,128,2048]{2,1,0:T(8,128)(2,1)}, bf16[8,4,128,128]{3,2,1,0:T(8...) custom-call(s32[80]{0:T(128)} %reshape.317.scal, ...), custom_call_target="tpu_custom_call", output_to_operand_aliasing={{1}: (8, {}), {2}: (9, {}), {3}: (10, {}), {4}: (11, {}), {... | custom-call | bytes 39600000 | tf_op jit(solution)/shard_map/pallas_call | solution.py:466
  183.3 2.7 collective-permute-done.14.arriving
  186.0 1.3 collective-permute-start.16
  187.3 10.6 %shard_map.122 = (bf16[128,2048]{1,0:T(8,128)(2,1)}, bf16[4,128,2048]{2,1,0:T(8,128)(2,1)}, bf16[4,128,2048]{2,1,0:T(8,128)(2,1)}, bf16[8,4,128,128]{3,2,1,0:T(8...) custom-call(s32[80]{0:T(128)} %reshape.317.scal, ...), custom_call_target="tpu_custom_call", output_to_operand_aliasing={{1}: (8, {}), {2}: (9, {}), {3}: (10, {}), {4}: (11, {}), {... | custom-call | bytes 39600000 | tf_op jit(solution)/shard_map/pallas_call | solution.py:466
  197.9 1.3 collective-permute-start.17
  199.4 1.0 shard_map.123
  201.8 1.0 shard_map.124
  202.8 4.3 %all-to-all-start.1 = ((bf16[8,4,128,128]{3,2,1,0:T(8,128)(2,1)}), bf16[8,4,128,128]{3,2,1,0:T(8,128)(2,1)}, u32[]{:S(2)}, u32[]{:S(2)}) async-start(bf16[8,4,128,128]{3,2,1,0:T(8,128)(2,1)} %get-tuple-element.246), calls=%async_computation.1 | async-start | bytes 2097152 | tf_op jit(solution)/shard_map/all_to_all | solution.py:381
  207.4 13.2 %collective-permute-done.18.parts_and_out_1_.parts_and_out_2_ = bf16[2,2,128,1024]{3,2,1,0:T(8,128)(2,1)} collective-permute-done((bf16[2,2,128,1024]{3,2,1,0:T(8,128)(2,1)}, bf16[2,2,128,1024]{3,2,1,0:T(8,128)(2,1)}, u32[]{:S(2)}, u32[]{:S(2)}) %collective-permute-start.18) | collective-permute-done | bytes 1048608 | tf_op jit(solution)/shard_map/ppermute | solution.py:428
  220.6 18.4 %collective-permute-done.19.parts_and_out_4_.parts_and_out_5_ = bf16[1,2,128,1024]{3,2,1,0:T(8,128)(2,1)S(1)} collective-permute-done((bf16[1,2,128,1024]{3,2,1,0:T(8,128)(2,1)S(1)}, bf16[1,2,128,1024]{3,2,1,0:T(8,128)(2,1)S(1)}, u32[]{:S(2)}, u32[]{:S(2)}) %collective-permute-start.19) | collective-permute-done | bytes 524320 | tf_op jit(solution)/shard_map/ppermute | solution.py:428
  239.0 13.0 %collective-permute-done.20.parts_and_out_7_.parts_and_out_8_ = bf16[1,2,128,1024]{3,2,1,0:T(8,128)(2,1)S(1)} collective-permute-done((bf16[1,2,128,1024]{3,2,1,0:T(8,128)(2,1)S(1)}, bf16[1,2,128,1024]{3,2,1,0:T(8,128)(2,1)S(1)}, u32[]{:S(2)}, u32[]{:S(2)}) %collective-permute-start.20) | collective-permute-done | bytes 524320 | tf_op jit(solution)/shard_map/ppermute | solution.py:428
  252.0 0.8 copy-done.11
  252.8 10.5 %shard_map.125 = bf16[1024,2048]{1,0:T(8,128)(2,1)} custom-call(s32[1]{0:T(128)} %bitcast.44.par, bf16[512,2048]{1,0:T(8,128)(2,1)} %bitcast.112, bf16[512,1024]{1,0:T(8,128)(2,1)} %collective-permute-done.12.x_got, bf16[512,2048]{1,0:T(8,128)(2,1)} %bitcast.106, bf16[512,1024]{1,0:T(8,128)(2,1)} %bitcast.109, bf16[512,1024]{1,0:T(8,128)(2,1)} %copy-done.13, ...), custom_call_target="tpu_custom_call" | custom-call | bytes 32400000 | tf_op jit(solution)/shard_map/pallas_call | solution.py:580
  267.1 25.6 %shard_map.126 = bf16[16,2,128,128]{3,2,1,0:T(8,128)(2,1)} custom-call(s32[128]{0:T(128)} %multiply_add_fusion.ids, s32[128]{0:T(128)} %reshape.327.mask, bf16[8,1040,128]{2,1,0:T(8,128)(2,1)} %copy-done.5, bf16[8,512,128]{2,1,0:T(8,128)(2,1)} %bitcast.46.d_ref, bf16[8,1040,128]{2,1,0:T(8,128)(2,1)} %copy-done.5), custom_call_target="tpu_custom_call" | custom-call | bytes 133200000 | tf_op jit(solution)/shard_map/pallas_call | solution.py:628
  292.7 52.1 %all_to_all.15 = bf16[8,2,2,128,128]{4,3,2,1,0:T(8,128)(2,1)S(1)} all-to-all(bf16[8,2,2,128,128]{4,3,2,1,0:T(8,128)(2,1)} %bitcast.121), channel_id=1, replica_groups=mesh['section'=4,'dp'=8] {'dp'}, dimensions={0} | all-to-all | bytes 2097152 | tf_op jit(solution)/shard_map/all_to_all | solution.py:381
  345.5 1.3 broadcast_in_dim_reshape.3
  346.8 15.1 %reduce-scatter.2.cloned.1.call-done = bf16[256,2048]{1,0:T(8,128)(2,1)} async-done(((bf16[1024,2048]{1,0:T(8,128)(2,1)}), bf16[256,2048]{1,0:T(8,128)(2,1)}) %reduce-scatter.2.cloned.1.call-update) | async-done | bytes 1048592 | tf_op jit(solution)/shard_map/reduce_scatter | solution.py:610
  361.9 2.2 slice_bitcast_fusion
  (141 shorter events, 20.4 us)
Async XLA Ops:
  7.2 4.6 %copy-start.22 = (s32[8,8]{1,0:T(8,128)S(1)}, s32[8,8]{1,0:T(8,128)}, u32[]{:S(2)}) copy-start(s32[8,8]{1,0:T(8,128)} %param.19) | copy-start | bytes 772
  7.2 4.6 %copy-start.21 = (s32[8,8]{1,0:T(8,128)S(1)}, s32[8,8]{1,0:T(8,128)}, u32[]{:S(2)}) copy-start(s32[8,8]{1,0:T(8,128)} %param.18) | copy-start | bytes 772
  8.5 23.9 %copy-start.9 = (bf16[1,2,2,128,1024]{4,3,2,1,0:T(8,128)(2,1)S(1)}, bf16[1,2,2,128,1024]{4,3,2,1,0:T(8,128)(2,1)}, u32[]{:S(2)}) copy-start(bf16[1,2,2,128,1024]{4,3,2,1,0:T(8,128)(2,1)} %param.16) | copy-start | bytes 3145732
  9.4 25.1 %collective-permute-start = (bf16[2,128,1024]{2,1,0:T(8,128)(2,1)S(1)}, bf16[2,128,1024]{2,1,0:T(8,128)(2,1)S(1)}, u32[]{:S(2)}, u32[]{:S(2)}) collective-permute-start(bf16[2,128,1024]{2,1,0:T(8,128)(2,1)S(1)} %get-tuple-element.262), channel_id=1, source_target_pairs={{0,4},{1,5},{2,6},{3,7},{4,0},{5,1},{6,2},{7,3},{8,12},{9,13},{10,... | collective-permute-start | bytes 1572872 | tf_op jit(solution)/shard_map/ppermute | solution.py:362
  34.5 23.3 %collective-permute-start.1 = (bf16[2,128,1024]{2,1,0:T(8,128)(2,1)}, bf16[2,128,1024]{2,1,0:T(8,128)(2,1)S(1)}, u32[]{:S(2)}, u32[]{:S(2)}) collective-permute-start(bf16[2,128,1024]{2,1,0:T(8,128)(2,1)} %get-tuple-element.128), channel_id=1, source_target_pairs={{0,4},{1,5},{2,6},{3,7},{4,0},{5,1},{6,2},{7,3},{8,12},{9,13},{10,... | collective-permute-start | bytes 1572872 | tf_op jit(solution)/shard_map/ppermute | solution.py:362
  38.7 5.6 %copy-start.6 = (bf16[1,4,128,2048]{3,2,1,0:T(8,128)(2,1)S(1)}, bf16[1,4,128,2048]{3,2,1,0:T(8,128)(2,1)}, u32[]{:S(2)}) copy-start(bf16[1,4,128,2048]{3,2,1,0:T(8,128)(2,1)} %param.12) | copy-start | bytes 6291460
  38.8 5.4 %copy-start = (bf16[1,2048,1024]{2,1,0:T(8,128)(2,1)S(1)}, bf16[1,2048,1024]{2,1,0:T(8,128)(2,1)}, u32[]{:S(2)}) copy-start(bf16[1,2048,1024]{2,1,0:T(8,128)(2,1)} %param.14) | copy-start | bytes 12582916
  41.5 29.4 %collective-permute-start.2 = (bf16[2,128,1024]{2,1,0:T(8,128)(2,1)}, bf16[2,128,1024]{2,1,0:T(8,128)(2,1)}, u32[]{:S(2)}, u32[]{:S(2)}) collective-permute-start(bf16[2,128,1024]{2,1,0:T(8,128)(2,1)} %pad_maximum_fusion.6), channel_id=1, source_target_pairs={{0,1},{1,0},{2,3},{3,2},{4,5},{5,4},{6,7},{7,6},{8,9},{9,8},{10,11... | collective-permute-start | bytes 1572872 | tf_op jit(solution)/shard_map/ppermute | solution.py:377
  42.8 29.7 %collective-permute-start.3 = (bf16[2,128,1024]{2,1,0:T(8,128)(2,1)}, bf16[2,128,1024]{2,1,0:T(8,128)(2,1)}, u32[]{:S(2)}, u32[]{:S(2)}) collective-permute-start(bf16[2,128,1024]{2,1,0:T(8,128)(2,1)} %pad_maximum_fusion.7), channel_id=1, source_target_pairs={{0,2},{1,3},{2,0},{3,1},{4,6},{5,7},{6,4},{7,5},{8,10},{9,11},{10,... | collective-permute-start | bytes 1572872 | tf_op jit(solution)/shard_map/ppermute | solution.py:377
  42.8 32.7 %collective-permute-start.4 = (bf16[2,128,1024]{2,1,0:T(8,128)(2,1)}, bf16[2,128,1024]{2,1,0:T(8,128)(2,1)}, u32[]{:S(2)}, u32[]{:S(2)}) collective-permute-start(bf16[2,128,1024]{2,1,0:T(8,128)(2,1)} %pad_maximum_fusion.8), channel_id=1, source_target_pairs={{0,3},{1,2},{2,1},{3,0},{4,7},{5,6},{6,5},{7,4},{8,11},{9,10},{10,... | collective-permute-start | bytes 1572872 | tf_op jit(solution)/shard_map/ppermute | solution.py:377
  57.8 3.4 copy-start.24
  62.8 24.1 %collective-permute-start.5 = (bf16[2,128,1024]{2,1,0:T(8,128)(2,1)}, bf16[2,128,1024]{2,1,0:T(8,128)(2,1)}, u32[]{:S(2)}, u32[]{:S(2)}) collective-permute-start(bf16[2,128,1024]{2,1,0:T(8,128)(2,1)} %pad_maximum_fusion.2), channel_id=1, source_target_pairs={{0,1},{1,0},{2,3},{3,2},{4,5},{5,4},{6,7},{7,6},{8,9},{9,8},{10,11... | collective-permute-start | bytes 1572872 | tf_op jit(solution)/shard_map/ppermute | solution.py:377
  63.8 24.1 %collective-permute-start.6 = (bf16[2,128,1024]{2,1,0:T(8,128)(2,1)}, bf16[2,128,1024]{2,1,0:T(8,128)(2,1)}, u32[]{:S(2)}, u32[]{:S(2)}) collective-permute-start(bf16[2,128,1024]{2,1,0:T(8,128)(2,1)} %pad_maximum_fusion.3), channel_id=1, source_target_pairs={{0,2},{1,3},{2,0},{3,1},{4,6},{5,7},{6,4},{7,5},{8,10},{9,11},{10,... | collective-permute-start | bytes 1572872 | tf_op jit(solution)/shard_map/ppermute | solution.py:377
  70.9 2.7 copy-start.8
  70.9 26.0 %collective-permute-start.7 = (bf16[2,128,1024]{2,1,0:T(8,128)(2,1)}, bf16[2,128,1024]{2,1,0:T(8,128)(2,1)}, u32[]{:S(2)}, u32[]{:S(2)}) collective-permute-start(bf16[2,128,1024]{2,1,0:T(8,128)(2,1)} %pad_maximum_fusion.4), channel_id=1, source_target_pairs={{0,3},{1,2},{2,1},{3,0},{4,7},{5,6},{6,5},{7,4},{8,11},{9,10},{10,... | collective-permute-start | bytes 1572872 | tf_op jit(solution)/shard_map/ppermute | solution.py:377
  76.6 1.4 copy-start.2
  78.0 7.5 %copy-start.12 = (bf16[2,128,1024]{2,1,0:T(8,128)(2,1)S(1)}, bf16[2,128,1024]{2,1,0:T(8,128)(2,1)}, u32[]{:S(2)}) copy-start(bf16[2,128,1024]{2,1,0:T(8,128)(2,1)} %pad_maximum_fusion.1) | copy-start | bytes 1572868
  78.0 7.5 %copy-start.7 = (bf16[1,4,128,2048]{3,2,1,0:T(8,128)(2,1)S(1)}, bf16[1,4,128,2048]{3,2,1,0:T(8,128)(2,1)}, u32[]{:S(2)}) copy-start(bf16[1,4,128,2048]{3,2,1,0:T(8,128)(2,1)} %param.12) | copy-start | bytes 6291460
  97.9 1.3 copy-start.1
  100.2 7.9 %copy-start.23 = (s32[16]{0:T(128)S(1)}, s32[16]{0:T(128)}, u32[]{:S(2)}) copy-start(s32[16]{0:T(128)} %reshape.318.owners) | copy-start | bytes 196
  100.2 59.9 %all-to-all-start = ((bf16[8,1040,128]{2,1,0:T(8,128)(2,1)}), bf16[8,1040,128]{2,1,0:T(8,128)(2,1)S(1)}, u32[]{:S(2)}, u32[]{:S(2)}) async-start(bf16[8,1040,128]{2,1,0:T(8,128)(2,1)} %maximum_maximum_fusion), calls=%async_computation | async-start | bytes 4259840 | tf_op jit(solution)/shard_map/all_to_all | solution.py:381
  107.4 8.1 %collective-permute-start.8 = (bf16[128,2048]{1,0:T(8,128)(2,1)}, bf16[128,2048]{1,0:T(8,128)(2,1)S(1)}, u32[]{:S(2)}, u32[]{:S(2)}) collective-permute-start(bf16[128,2048]{1,0:T(8,128)(2,1)} %get-tuple-element.160), channel_id=1, source_target_pairs={{24,16},{25,17},{26,18},{27,19},{28,20},{29,21},{30,22},{31,23}} | collective-permute-start | bytes 1572872 | tf_op jit(solution)/shard_map/ppermute | solution.py:552
  115.5 0.8 copy-start.15
  115.6 2.0 collective-permute-start.9
  117.5 2.6 copy-start.17
  117.6 25.6 %collective-permute-start.10 = (bf16[128,2048]{1,0:T(8,128)(2,1)}, bf16[128,2048]{1,0:T(8,128)(2,1)S(1)}, u32[]{:S(2)}, u32[]{:S(2)}) collective-permute-start(bf16[128,2048]{1,0:T(8,128)(2,1)} %get-tuple-element.178), channel_id=1, source_target_pairs={{16,8},{24,16},{17,9},{25,17},{18,10},{26,18},{19,11},{27,19},{20,... | collective-permute-start | bytes 1572872 | tf_op jit(solution)/shard_map/ppermute | solution.py:552
  118.9 41.3 %collective-permute-start.12 = (bf16[512,1024]{1,0:T(8,128)(2,1)}, bf16[512,1024]{1,0:T(8,128)(2,1)}, u32[]{:S(2)}, u32[]{:S(2)}) collective-permute-start(bf16[512,1024]{1,0:T(8,128)(2,1)} %pad_maximum_fusion), channel_id=1, source_target_pairs={{0,1},{1,0},{2,3},{3,2},{4,5},{5,4},{6,7},{7,6},{8,9},{9,8},{10,11... | collective-permute-start | bytes 3145736 | tf_op jit(solution)/shard_map/ppermute | solution.py:428
  143.1 1.3 copy-start.18
  143.1 14.0 %collective-permute-start.11 = (bf16[128,2048]{1,0:T(8,128)(2,1)}, bf16[128,2048]{1,0:T(8,128)(2,1)S(1)}, u32[]{:S(2)}, u32[]{:S(2)}) collective-permute-start(bf16[128,2048]{1,0:T(8,128)(2,1)} %get-tuple-element.187), channel_id=1, source_target_pairs={{16,8},{24,16},{17,9},{25,17},{18,10},{26,18},{19,11},{27,19},{20,... | collective-permute-start | bytes 1572872 | tf_op jit(solution)/shard_map/ppermute | solution.py:552
  157.2 2.7 copy-start.14
  157.2 13.6 %collective-permute-start.13 = (bf16[128,2048]{1,0:T(8,128)(2,1)}, bf16[128,2048]{1,0:T(8,128)(2,1)}, u32[]{:S(2)}, u32[]{:S(2)}) collective-permute-start(bf16[128,2048]{1,0:T(8,128)(2,1)} %get-tuple-element.201), channel_id=1, source_target_pairs={{8,0},{16,8},{9,1},{17,9},{10,2},{18,10},{11,3},{19,11},{12,4},{20... | collective-permute-start | bytes 1572872 | tf_op jit(solution)/shard_map/ppermute | solution.py:552
  159.9 27.4 %collective-permute-start.15 = (bf16[512,1024]{1,0:T(8,128)(2,1)}, bf16[512,1024]{1,0:T(8,128)(2,1)S(1)}, u32[]{:S(2)}, u32[]{:S(2)}) collective-permute-start(bf16[512,1024]{1,0:T(8,128)(2,1)} %bitcast.108), channel_id=1, source_target_pairs={{0,1},{1,0},{2,3},{3,2},{4,5},{5,4},{6,7},{7,6},{8,9},{9,8},{10,11... | collective-permute-start | bytes 3145736 | tf_op jit(solution)/shard_map/ppermute | solution.py:428
  160.1 104.7 %copy-start.5 = (bf16[8,1040,128]{2,1,0:T(8,128)(2,1)}, bf16[8,1040,128]{2,1,0:T(8,128)(2,1)S(1)}, u32[]{:S(2)}) copy-start(bf16[8,1040,128]{2,1,0:T(8,128)(2,1)S(1)} %all-to-all-done.q_ref.kv_ref) | copy-start | bytes 6389764
  170.8 15.2 %collective-permute-start.14 = (bf16[128,2048]{1,0:T(8,128)(2,1)}, bf16[128,2048]{1,0:T(8,128)(2,1)S(1)}, u32[]{:S(2)}, u32[]{:S(2)}) collective-permute-start(bf16[128,2048]{1,0:T(8,128)(2,1)} %get-tuple-element.210), channel_id=1, source_target_pairs={{8,0},{16,8},{9,1},{17,9},{10,2},{18,10},{11,3},{19,11},{12,4},{20... | collective-permute-start | bytes 1572872 | tf_op jit(solution)/shard_map/ppermute | solution.py:552
  186.0 1.3 copy-start.19
  186.0 11.9 %collective-permute-start.16 = (bf16[128,2048]{1,0:T(8,128)(2,1)}, bf16[128,2048]{1,0:T(8,128)(2,1)S(1)}, u32[]{:S(2)}, u32[]{:S(2)}) collective-permute-start(bf16[128,2048]{1,0:T(8,128)(2,1)} %get-tuple-element.221), channel_id=1, source_target_pairs={{8,0},{9,1},{10,2},{11,3},{12,4},{13,5},{14,6},{15,7}} | collective-permute-start | bytes 1572872 | tf_op jit(solution)/shard_map/ppermute | solution.py:552
  187.3 10.6 %copy-start.13 = (bf16[512,1024]{1,0:T(8,128)(2,1)}, bf16[512,1024]{1,0:T(8,128)(2,1)S(1)}, u32[]{:S(2)}) copy-start(bf16[512,1024]{1,0:T(8,128)(2,1)S(1)} %collective-permute-done.15.att_got) | copy-start | bytes 3145732
  197.9 1.4 copy-start.16
  197.9 3.0 collective-permute-start.17
  199.3 21.3 %collective-permute-start.18 = (bf16[2,2,128,1024]{3,2,1,0:T(8,128)(2,1)}, bf16[2,2,128,1024]{3,2,1,0:T(8,128)(2,1)}, u32[]{:S(2)}, u32[]{:S(2)}) collective-permute-start(bf16[2,2,128,1024]{3,2,1,0:T(8,128)(2,1)} %get-tuple-element.239.parts_and_out_0_), channel_id=1, source_target_pairs={{0,1},{1,0},{2,3},{3,2},{4,5},{5,4},{6,7},{7,6},{8,9},{9,8},{10,11... | collective-permute-start | bytes 3145736 | tf_op jit(solution)/shard_map/ppermute | solution.py:428
  201.0 0.8 copy-start.20
  202.7 17.8 %copy-start.4 = (bf16[1,2,128,1024]{3,2,1,0:T(8,128)(2,1)S(1)}, bf16[1,2,128,1024]{3,2,1,0:T(8,128)(2,1)}, u32[]{:S(2)}) copy-start(bf16[1,2,128,1024]{3,2,1,0:T(8,128)(2,1)} %get-tuple-element.242.parts_and_out_3_) | copy-start | bytes 1572868
  202.8 36.2 %copy-start.3 = (bf16[1,2,128,1024]{3,2,1,0:T(8,128)(2,1)S(1)}, bf16[1,2,128,1024]{3,2,1,0:T(8,128)(2,1)}, u32[]{:S(2)}) copy-start(bf16[1,2,128,1024]{3,2,1,0:T(8,128)(2,1)} %get-tuple-element.245.parts_and_out_6_) | copy-start | bytes 1572868
  202.8 60.5 %all-to-all-start.1 = ((bf16[8,4,128,128]{3,2,1,0:T(8,128)(2,1)}), bf16[8,4,128,128]{3,2,1,0:T(8,128)(2,1)}, u32[]{:S(2)}, u32[]{:S(2)}) async-start(bf16[8,4,128,128]{3,2,1,0:T(8,128)(2,1)} %get-tuple-element.246), calls=%async_computation.1 | async-start | bytes 2097152 | tf_op jit(solution)/shard_map/all_to_all | solution.py:381
  207.1 154.8 %reduce-scatter.2.cloned.1.call-start = ((), (), s32[]{:S(2)}) async-start(), calls=%async_computation.4 | async-start | bytes 5242880 | tf_op jit(solution)/shard_map/reduce_scatter | solution.py:610
  220.6 18.4 %collective-permute-start.19 = (bf16[1,2,128,1024]{3,2,1,0:T(8,128)(2,1)S(1)}, bf16[1,2,128,1024]{3,2,1,0:T(8,128)(2,1)S(1)}, u32[]{:S(2)}, u32[]{:S(2)}) collective-permute-start(bf16[1,2,128,1024]{3,2,1,0:T(8,128)(2,1)S(1)} %copy-done.4), channel_id=1, source_target_pairs={{0,1},{1,0},{2,3},{3,2},{4,5},{5,4},{6,7},{7,6},{8,9},{9,8},{10,11... | collective-permute-start | bytes 1572872 | tf_op jit(solution)/shard_map/ppermute | solution.py:428
  239.0 13.0 %copy-start.10 = (bf16[1,2,128,1024]{3,2,1,0:T(8,128)(2,1)}, bf16[1,2,128,1024]{3,2,1,0:T(8,128)(2,1)S(1)}, u32[]{:S(2)}) copy-start(bf16[1,2,128,1024]{3,2,1,0:T(8,128)(2,1)S(1)} %collective-permute-done.19.parts_and_out_4_.parts_and_out_5_) | copy-start | bytes 1572868
  239.0 13.0 %collective-permute-start.20 = (bf16[1,2,128,1024]{3,2,1,0:T(8,128)(2,1)S(1)}, bf16[1,2,128,1024]{3,2,1,0:T(8,128)(2,1)S(1)}, u32[]{:S(2)}, u32[]{:S(2)}) collective-permute-start(bf16[1,2,128,1024]{3,2,1,0:T(8,128)(2,1)S(1)} %copy-done.3), channel_id=1, source_target_pairs={{0,1},{1,0},{2,3},{3,2},{4,5},{5,4},{6,7},{7,6},{8,9},{9,8},{10,11... | collective-permute-start | bytes 1572872 | tf_op jit(solution)/shard_map/ppermute | solution.py:428
  252.0 0.8 copy-start.11
Sparse Core Ops, SparseCore 0:
  263.4 98.3 reduce-scatter.1
